TPU v7x, 32 devices: a whole 2x2x4 slice. The times are simulated.
32 devices in a mesh: dp: 8 (over y, x, core), seq: 4 (over z).
Axes of the slice: x: 2, y: 2, z: 4, core: 2. Of those that a mesh axis runs over, the one named last changes fastest.
Arguments:
- video: bfloat16 [8, 512, 3072], P('dp', 'seq'), may hold values from -6 to 6
- cotangent: bfloat16 [8, 512, 3072], P('dp', 'seq'), may hold values from -6 to 6
- w_query: bfloat16 [3072, 3072], P(None, 'seq'), may hold values from -0.109375 to 0.109375
- w_out: bfloat16 [3072, 3072], P('seq'), may hold values from -0.109375 to 0.109375
- ref_kv: bfloat16 [8, 2, 1024, 3072], P('dp', None, 'seq'), may hold values from -400 to 400, as said below
- tile_lists: int32 [8, 2, 4, 3], P('dp'), may hold values from -1 to 3, as said below
Outputs:
- output: bfloat16 [8, 512, 3072], P('dp', 'seq')
- grad_video: bfloat16 [8, 512, 3072], P('dp', 'seq')
- grad_wq: float32 [3072, 3072], P(None, 'seq')
- grad_wo: float32 [3072, 3072], P('seq')
- grad_ref: bfloat16 [8, 2, 1024, 3072], P('dp', None, 'seq')
Inputs may be any that keep to these rules, and one draw needn't show every extreme that they name: `ref_kv`: values are of order one; key rows may carry scales of up to some tens. `tile_lists`: each row lists first 1 to 3 different tile indices from 0 to 3, consecutive modulo 4, then -1; the first video tile of every clip lists exactly 3 tiles for each person.
All inputs are finite; a program needn't handle non-finite values.
Results may differ from a plain program's by a relative error of at most 0.012.
The roundings to bfloat16 on the way count: a program that leaves them out, or rounds other values in their place, can miss the bound.
Values may be sent and summed in bfloat16 or wider, within the bound.
No kernel may reach another device: no remote copies, remote signals or barrier semaphores. Data moves between devices by JAX's collectives and lax.ppermute only.
A program may use at most 128 MiB of HBM per device.

v0:
```python
import math

import jax
import jax.numpy as jnp
from jax import lax
from jax.sharding import PartitionSpec as P

HD = 128
REF = 512
TILE = 128


def build_allowed(tile_lists, tile_size, ref_tokens):
    tiles_each = ref_tokens // tile_size
    matched = jnp.any(tile_lists[..., None] == jnp.arange(tiles_each, dtype=jnp.int32), axis=-2)
    tile_table = jnp.transpose(matched, (1, 0, 2)).reshape(matched.shape[1], -1)
    return jnp.repeat(jnp.repeat(tile_table, tile_size, axis=0), tile_size, axis=1)


def split_heads(array, heads_count):
    return jnp.transpose(array.reshape(array.shape[0], heads_count, -1), (1, 0, 2))


def merge_heads(array):
    return jnp.transpose(array, (1, 0, 2)).reshape(array.shape[1], -1)


def contract_last(left, right):
    return lax.dot_general(
        left, right, (((1,), (1,)), ((), ())), preferred_element_type=jnp.float32
    )


def contract_first(left, right):
    return lax.dot_general(
        left, right, (((0,), (0,)), ((), ())), preferred_element_type=jnp.float32
    )


def softmax_weights(query, keys, allowed, score_scale):
    scores = contract_last(query, keys) * score_scale
    scores = jnp.where(allowed, scores, -1e30)
    peak = jnp.max(scores, axis=-1, keepdims=True)
    weights = jnp.exp(scores - peak)
    return weights / jnp.sum(weights, axis=-1, keepdims=True)


def head_forward(query, keys, values, allowed, score_scale):
    weights = softmax_weights(query, keys, allowed, score_scale)
    probs = weights.astype(jnp.bfloat16)
    return jnp.dot(probs, values, preferred_element_type=jnp.float32).astype(jnp.bfloat16)


def head_backward(query, keys, values, grad_out, allowed, score_scale):
    weights = softmax_weights(query, keys, allowed, score_scale)
    probs = weights.astype(jnp.bfloat16)
    grad_probs = contract_last(grad_out, values)
    delta = jnp.sum(grad_probs * weights, axis=-1, keepdims=True)
    grad_scores = (weights * (grad_probs - delta) * score_scale).astype(jnp.bfloat16)
    grad_query = jnp.dot(grad_scores, keys, preferred_element_type=jnp.float32).astype(jnp.bfloat16)
    grad_keys = contract_first(grad_scores, query).astype(jnp.bfloat16)
    grad_values = contract_first(probs, grad_out).astype(jnp.bfloat16)
    return (grad_query, grad_keys, grad_values)


def body(video, cotangent, w_query, w_out, ref_kv, tile_lists):
    local_width = w_query.shape[1]
    heads_here = local_width // HD
    score_scale = 1.0 / math.sqrt(HD)
    gathered = lax.all_gather(video, "seq", axis=1, tiled=True)[0]
    query = jnp.dot(gathered, w_query, preferred_element_type=jnp.float32).astype(jnp.bfloat16)
    both_kv = lax.all_to_all(ref_kv, "seq", split_axis=3, concat_axis=2, tiled=True)[0]
    allowed = build_allowed(tile_lists[0], TILE, REF)
    q_heads = split_heads(query, heads_here)
    k_heads = split_heads(both_kv[0], heads_here)
    v_heads = split_heads(both_kv[1], heads_here)
    attn_heads = lax.map(
        lambda item: head_forward(item[0], item[1], item[2], allowed, score_scale),
        (q_heads, k_heads, v_heads),
    )
    attention = merge_heads(attn_heads)
    rows = attention
    output = lax.psum_scatter(
        jnp.dot(rows, w_out, preferred_element_type=jnp.float32),
        "seq",
        scatter_dimension=0,
        tiled=True,
    )
    output = output.astype(jnp.bfloat16)[None]
    grad_rows = lax.all_gather(cotangent, "seq", axis=1, tiled=True)[0]
    grad_attention = contract_last(grad_rows, w_out).astype(jnp.bfloat16)
    grad_wo = contract_first(attention, grad_rows)
    back = lax.map(
        lambda item: head_backward(item[0], item[1], item[2], item[3], allowed, score_scale),
        (q_heads, k_heads, v_heads, split_heads(grad_attention, heads_here)),
    )
    grad_query = merge_heads(back[0])
    grad_kv = jnp.stack([merge_heads(back[1]), merge_heads(back[2])])[None]
    grad_ref = lax.all_to_all(grad_kv, "seq", split_axis=2, concat_axis=3, tiled=True)
    rows = grad_query
    grad_video = lax.psum_scatter(
        contract_last(rows, w_query).astype(jnp.bfloat16), "seq", scatter_dimension=0, tiled=True
    ).astype(jnp.float32)
    grad_video = grad_video.astype(jnp.bfloat16)[None]
    grad_wq = contract_first(gathered, grad_query)
    grad_wq, grad_wo = (
        lax.psum(grad_wq.astype(jnp.bfloat16), "dp").astype(jnp.float32),
        lax.psum(grad_wo.astype(jnp.bfloat16), "dp").astype(jnp.float32),
    )
    return (output, grad_video, grad_wq, grad_wo, grad_ref)


def solution(mesh):
    in_specs = (
        P("dp", "seq", None),
        P("dp", "seq", None),
        P(None, "seq"),
        P("seq", None),
        P("dp", None, "seq", None),
        P("dp", None, None, None),
    )
    out_specs = (
        P("dp", "seq", None),
        P("dp", "seq", None),
        P(None, "seq"),
        P("seq", None),
        P("dp", None, "seq", None),
    )
    return jax.shard_map(body, mesh=mesh, in_specs=in_specs, out_specs=out_specs, check_vma=False)
```

profile of v0, /device:TPU:0, one launch (start us, length us, event | category | flops | bytes accessed | tf_op | source)
XLA Modules:
  0.0 661.5 jit_solution(8851351125706962845)
XLA Ops:
  8.6 8.6 %copy.77 = bf16[1,2,256,3072]{2,1,0,3:T(2,128)(2,1)} copy(bf16[1,2,256,3072]{3,2,1,0:T(8,128)(2,1)} %param.14) | data formatting | bytes 6291456 | tf_op args[4]
  17.3 6.4 all-to-all-start
  24.1 109.5 %all-gather.5.cloned.1.call-done = bf16[1,512,3072]{2,1,0:T(8,128)(2,1)} async-done(((bf16[1,128,3072]{2,1,0:T(8,128)(2,1)}), bf16[1,512,3072]{2,1,0:T(8,128)(2,1)}) %all-gather.5.cloned.1.call-update) | async-done | bytes 3145744 | tf_op jit(solution)/shard_map/all_gather | solution.py:90
  133.5 6.8 %fusion.51 = bf16[512,768]{1,0:T(8,128)(2,1)} fusion(bf16[768,3072]{1,0:T(8,128)(2,1)} %param.13, bf16[1,512,3072]{2,1,0:T(8,128)(2,1)} %all-gather.5.cloned.1.call-done), kind=kOutput, calls=%fused_computation.66 | convolution fusion | flops 2416312320 | bytes 8650752 | tf_op jit(solution)/shard_map/dot_general | solution.py:29
  140.4 2.4 copy.86
  142.7 54.0 %all-gather.3.cloned.1.call-done = bf16[1,512,3072]{2,1,0:T(8,128)(2,1)} async-done(((bf16[1,128,3072]{2,1,0:T(8,128)(2,1)}), bf16[1,512,3072]{2,1,0:T(8,128)(2,1)}) %all-gather.3.cloned.1.call-update) | async-done | bytes 3145744 | tf_op jit(solution)/shard_map/all_gather | solution.py:70
  196.7 6.8 %fusion.48 = bf16[512,768]{1,0:T(8,128)(2,1)} fusion(bf16[3072,768]{1,0:T(8,128)(2,1)} %param.12, bf16[1,512,3072]{2,1,0:T(8,128)(2,1)} %all-gather.3.cloned.1.call-done), kind=kOutput, calls=%fused_computation.65 | convolution fusion | flops 2416312320 | bytes 8650752 | tf_op jit(solution)/shard_map/dot_general | solution.py:71
  203.5 2.3 copy.76
  205.8 2.3 copy.82
  208.1 2.4 copy.113
  210.5 2.2 fusion.57
  212.7 2.8 reshape_squeeze.7
  219.9 32.9 %while.26 = (s32[]{:T(128)}, bf16[6,512,128]{1,2,0:T(8,128)(2,1)S(1)}, bf16[6,512,128]{2,1,0:T(8,128)(2,1)}, bf16[6,1024,128]{2,1,0:T(8,128)(2,1)}, bf16[6,1024,...) while((s32[]{:T(128)}, bf16[6,512,128]{1,2,0:T(8,128)(2,1)S(1)}, ...), condition=%wide.region_4.5_spmd.clone, body=%wide.region_1.4_spmd.clone.sunk | while | flops 272694272 | bytes 8666205 | solution.py:77
  221.5 1.7 fusion.85
  227.0 1.7 fusion.85
  232.5 1.7 fusion.85
  238.0 1.7 fusion.85
  243.5 1.7 fusion.85
  249.0 1.7 fusion.85
  253.8 76.0 %while.27 = (s32[]{:T(128)}, bf16[6,512,128]{1,2,0:T(8,128)(2,1)}, bf16[6,1024,128]{1,2,0:T(8,128)(2,1)}, bf16[6,1024,128]{1,2,0:T(8,128)(2,1)}, bf16[6,512,128]...) while((s32[]{:T(128)}, bf16[6,512,128]{1,2,0:T(8,128)(2,1)}, ...), condition=%wide.region_10.11_spmd.clone, body=%wide.region_6.10_spmd.clone.sunk | while | flops 680851968 | bytes 23490688 | solution.py:93
  255.4 1.7 fusion.94
  259.3 1.8 multiply_reduce_fusion.2
  268.1 1.7 fusion.94
  272.0 1.8 multiply_reduce_fusion.2
  280.7 1.7 fusion.94
  284.7 1.8 multiply_reduce_fusion.2
  293.4 1.7 fusion.94
  297.4 1.8 multiply_reduce_fusion.2
  306.1 1.7 fusion.94
  308.2 1.7 fusion.97
  310.0 1.8 multiply_reduce_fusion.2
  318.7 1.7 fusion.94
  322.7 1.8 multiply_reduce_fusion.2
  329.8 7.1 %fusion.41 = bf16[3072,768]{0,1:T(8,128)(2,1)} fusion(bf16[512,768]{0,1:T(8,128)(2,1)} %bitcast.173, bf16[1,512,3072]{2,1,0:T(8,128)(2,1)} %all-gather.3.cloned.1.call-done), kind=kOutput, calls=%fused_computation.55 | convolution fusion | flops 2418278400 | bytes 8650752 | tf_op jit(solution)/shard_map/dot_general | solution.py:35
  336.9 4.2 convolution_convert_fusion.4
  341.2 7.1 %fusion.58 = f32[512,3072]{1,0:T(8,128)} fusion(bf16[512,768]{0,1:T(8,128)(2,1)S(1)} %bitcast.168, bf16[768,3072]{1,0:T(8,128)(2,1)} %param.13), kind=kOutput, calls=%fused_computation.73 | convolution fusion | flops 2415919104 | bytes 11796480 | tf_op jit(solution)/shard_map/dot_general | solution.py:84
  349.4 6.5 convolution_convert_fusion.6
  356.0 2.3 maximum_bitcast_fusion
  358.3 5.6 copy.94
  363.9 74.7 %all_to_all.33 = bf16[1,2,1024,768]{3,1,0,2:T(2,128)(2,1)S(1)} all-to-all(bf16[1,2,1024,768]{3,1,0,2:T(2,128)(2,1)} %copy.94), channel_id=1, replica_groups=mesh['dp'=8,'seq'=4] {'seq'}, dimensions={2} | all-to-all | bytes 6291456 | tf_op jit(solution)/shard_map/all_to_all | solution.py:99
  439.1 2.8 copy.96
  441.9 4.7 copy.98
  446.6 31.6 %all-reduce.3.cloned.1.call-done = (bf16[3072,768]{0,1:T(8,128)(2,1)}, bf16[768,3072]{1,0:T(8,128)(2,1)}) async-done(((bf16[3072,768]{0,1:T(8,128)(2,1)}, bf16[768,3072]{1,0:T(8,128)(2,1)}), (bf16[3072,768]{0,1:T(8,128)(2,1)}, bf16[768,3072]{1,0:T(8,128)(2,1)})) %all-reduce.3.cloned.1.call-update) | async-done | bytes 9437200 | tf_op jit(solution)/shard_map/psum | solution.py:107
  478.2 7.4 %copy.97 = f32[3072,768]{1,0:T(8,128)} copy(bf16[3072,768]{0,1:T(8,128)(2,1)} %get-tuple-element.241) | data formatting | bytes 14155776
  485.6 8.5 %convert_element_type.58 = f32[768,3072]{1,0:T(8,128)} convert(bf16[768,3072]{1,0:T(8,128)(2,1)} %get-tuple-element.242) | non-fusion elementwise | flops 2359296 | bytes 14155776 | tf_op jit(solution)/shard_map/convert_element_type | solution.py:108
  494.1 97.3 %reduce-scatter.3.cloned.1.call-done = f32[128,3072]{1,0:T(8,128)} async-done(((f32[512,3072]{1,0:T(8,128)}), f32[128,3072]{1,0:T(8,128)}) %reduce-scatter.3.cloned.1.call-update) | async-done | bytes 1572880 | tf_op jit(solution)/shard_map/reduce_scatter | solution.py:83
  591.3 2.4 convert_bitcast_fusion
  593.7 61.3 %reduce-scatter.5.cloned.1.call-done = bf16[128,3072]{1,0:T(8,128)(2,1)} async-done(((bf16[512,3072]{1,0:T(8,128)(2,1)}), bf16[128,3072]{1,0:T(8,128)(2,1)}) %reduce-scatter.5.cloned.1.call-update) | async-done | bytes 786448 | tf_op jit(solution)/shard_map/reduce_scatter | solution.py:101
  (125 shorter events, 84.0 us)
Async XLA Ops:
  7.2 126.4 %all-gather.5.cloned.1.call-start = ((), (), s32[]{:S(2)}) async-start(), calls=%async_computation.6 | async-start | bytes 3932160 | tf_op jit(solution)/shard_map/all_gather | solution.py:90
  7.9 188.8 %all-gather.3.cloned.1.call-start = ((), (), s32[]{:S(2)}) async-start(), calls=%async_computation.4 | async-start | bytes 3932160 | tf_op jit(solution)/shard_map/all_gather | solution.py:70
  17.3 6.5 copy-start.1
  17.3 190.8 %all-to-all-start = ((bf16[1,2,256,3072]{2,1,0,3:T(2,128)(2,1)}), bf16[1,2,256,3072]{2,1,0,3:T(2,128)(2,1)S(1)}, u32[]{:S(2)}, u32[]{:S(2)}) async-start(bf16[1,2,256,3072]{2,1,0,3:T(2,128)(2,1)} %copy.77), calls=%async_computation | async-start | bytes 6291456 | tf_op jit(solution)/shard_map/all_to_all | solution.py:72
  23.7 454.5 %all-reduce.3.cloned.1.call-start = ((), (), s32[]{:S(2)}) async-start(), calls=%async_computation.8 | async-start | bytes 18874368 | tf_op jit(solution)/shard_map/psum | solution.py:107
  329.8 7.1 %copy-start.2 = (bf16[1,512,3072]{2,1,0:T(8,128)(2,1)S(1)}, bf16[1,512,3072]{2,1,0:T(8,128)(2,1)}, u32[]{:S(2)}) copy-start(bf16[1,512,3072]{2,1,0:T(8,128)(2,1)} %all-gather.5.cloned.1.call-done) | copy-start | bytes 9437188
  341.1 250.2 %reduce-scatter.3.cloned.1.call-start = ((), (), s32[]{:S(2)}) async-start(), calls=%async_computation.5 | async-start | bytes 7864320 | tf_op jit(solution)/shard_map/reduce_scatter | solution.py:83
  348.3 1.1 copy-start
  348.3 306.6 %reduce-scatter.5.cloned.1.call-start = ((), (), s32[]{:S(2)}) async-start(), calls=%async_computation.7 | async-start | bytes 3932160 | tf_op jit(solution)/shard_map/reduce_scatter | solution.py:101
Sparse Core Ops, SparseCore 0:
  9.6 123.9 all-gather.4
  135.1 61.5 all-gather.2
  341.3 136.9 all-reduce.2
  480.5 110.8 reduce-scatter.2
  594.2 60.7 reduce-scatter.4
where the time goes:
time: 664 us; the launch traced here: 662 us
  waiting for transfers between devices  355 us (53%)
  matrix products  106 us (16%)
  local copies, waits for them, and re-layouts  82 us (12%)
  blocking collectives  74.7 us (11%)
  other arithmetic  23.1 us (3%)
  between operations  13.8 us (2%)
    all_gather x1, waiting for transfers between devices, body(): grad_rows = lax.all_gather(cotangent, 'seq', axis=1, tiled=True)[0]  109 us
    reduce_scatter x1, waiting for transfers between devices, body(): lax.psum_scatter(jnp.dot(rows, w_out, preferred_element_type=jnp.float32)...  97.3 us
    all_to_all x1, blocking collectives, body(): lax.all_to_all(grad_kv, 'seq', split_axis=2, concat_axis=3, tiled=True)  74.7 us
    reduce_scatter x1, waiting for transfers between devices, body(): lax.psum_scatter(contract_last(rows, w_query).astype(jnp.bfloat16), 'seq'...  61.3 us
    all_gather x1, waiting for transfers between devices, body(): gathered = lax.all_gather(video, 'seq', axis=1, tiled=True)[0]  54 us
    dot_general x20, matrix products, contract_last(): lax.dot_general(left, right, (((1,), (1,)), ((), ())), preferred_element_...  44.7 us
    psum x1, waiting for transfers between devices, body(): lax.psum(grad_wq.astype(jnp.bfloat16), 'dp').astype(jnp.float32)  31.6 us
    dot_general x14, matrix products, contract_first(): lax.dot_general(left, right, (((0,), (0,)), ((), ())), preferred_element_...  29.6 us
  transfers between devices with their start and end apart: 6, of which 5 were waited for; matrix products, arithmetic and copies ran while one was open for 12% of the time, Pallas kernels for 0%

commit v1 on v0

v1 whole, which is shorter than its diff:
```python
import functools
import math

import jax
import jax.numpy as jnp
from jax import lax
from jax.experimental import pallas as pl
from jax.experimental.pallas import tpu as pltpu
from jax.sharding import PartitionSpec as P

HD = 128
TILE = 128
F32 = jnp.float32
BF16 = jnp.bfloat16
NEG = -1e30


def contract_last(left, right):
    return lax.dot_general(left, right, (((1,), (1,)), ((), ())), preferred_element_type=F32)


def contract_first(left, right):
    return lax.dot_general(left, right, (((0,), (0,)), ((), ())), preferred_element_type=F32)


def tile_table(tile_lists, ref_tiles, me, n):
    matched = jnp.any(tile_lists[..., None] == jnp.arange(ref_tiles, dtype=jnp.int32), axis=-2)
    table = jnp.transpose(matched, (1, 0, 2)).reshape(matched.shape[1], -1).astype(jnp.int32)
    source = lax.rem(me - jnp.arange(n, dtype=jnp.int32) + n, n)
    table = table.reshape(n, -1, table.shape[1])[source].reshape(table.shape)
    return table.reshape(table.shape[0], n, -1)[:, source].reshape(table.shape)


def masked(scores, table_ref, row, first, scale, axis):
    tiles = []
    for t in range(scores.shape[axis] // TILE):
        part = lax.slice_in_dim(scores, t * TILE, (t + 1) * TILE, axis=axis) * scale
        tiles.append(jnp.where(table_ref[row, first + t] != 0, part, NEG))
    return tiles


def forward_kernel(n, scale, table_ref, q_ref, *refs):
    kv_refs, out_ref = refs[:n], refs[n]
    local = kv_refs[0].shape[1] // TILE
    for i in range(q_ref.shape[0] // TILE):
        rows = pl.ds(i * TILE, TILE)
        query = q_ref[rows, :]
        scores = []
        for k in range(n):
            scores += masked(contract_last(query, kv_refs[k][0]), table_ref, i, k * local, scale, 1)
        peak = functools.reduce(jnp.maximum, scores)
        peak = jnp.max(peak, axis=1, keepdims=True)
        powers = [jnp.exp(s - peak) for s in scores]
        total = jnp.sum(functools.reduce(jnp.add, powers), axis=1, keepdims=True)
        inverse = 1.0 / total
        probs = [(p * inverse).astype(BF16) for p in powers]
        acc = None
        for k in range(n):
            part = jnp.concatenate(probs[k * local : (k + 1) * local], axis=1)
            part = jnp.dot(part, kv_refs[k][1], preferred_element_type=F32)
            acc = part if acc is None else acc + part
        out_ref[rows, :] = acc.astype(BF16)


def backward_kernel(n, scale, table_ref, q_ref, g_ref, *refs):
    kv_refs, dq_ref, dkv_refs = refs[:n], refs[n], refs[n + 1 : 2 * n + 1]
    probs_ref, dscores_ref = refs[2 * n + 1 :]
    length = kv_refs[0].shape[1]
    local = length // TILE
    for i in range(q_ref.shape[0] // TILE):
        rows = pl.ds(i * TILE, TILE)
        query, grad = q_ref[rows, :], g_ref[rows, :]
        scores, dprobs = [], []
        for k in range(n):
            scores += masked(contract_last(kv_refs[k][0], query), table_ref, i, k * local, scale, 0)
        peak = functools.reduce(jnp.maximum, scores)
        peak = jnp.max(peak, axis=0, keepdims=True)
        powers = [jnp.exp(s - peak) for s in scores]
        total = jnp.sum(functools.reduce(jnp.add, powers), axis=0, keepdims=True)
        inverse = 1.0 / total
        weights = [p * inverse for p in powers]
        for k in range(n):
            part = contract_last(kv_refs[k][1], grad)
            dprobs += [part[t * TILE : (t + 1) * TILE] for t in range(local)]
        delta = functools.reduce(jnp.add, [d * w for d, w in zip(dprobs, weights)])
        delta = jnp.sum(delta, axis=0, keepdims=True)
        for j in range(n * local):
            keys = pl.ds(j * TILE, TILE)
            probs_ref[keys, rows] = weights[j].astype(BF16)
            dscores_ref[keys, rows] = (weights[j] * (dprobs[j] - delta) * scale).astype(BF16)
    dq = None
    for k in range(n):
        keys = pl.ds(k * length, length)
        dscores = dscores_ref[keys, :]
        dkv_refs[k][0] = jnp.dot(dscores, q_ref[...], preferred_element_type=F32).astype(BF16)
        dkv_refs[k][1] = jnp.dot(probs_ref[keys, :], g_ref[...], preferred_element_type=F32).astype(BF16)
        part = contract_first(kv_refs[k][0], dscores)
        dq = part if dq is None else dq + part
    dq_ref[...] = dq.T.astype(BF16)


def attend(table, query, pieces, scale):
    n = len(pieces)
    tokens, width = query.shape
    length = pieces[0].shape[1]
    rows = pl.BlockSpec((tokens, HD), lambda h, t: (0, h))
    piece = pl.BlockSpec((2, length, HD), lambda h, t: (0, 0, h))
    work = tokens * n * length * width
    return pl.pallas_call(
        functools.partial(forward_kernel, n, scale),
        out_shape=jax.ShapeDtypeStruct(query.shape, BF16),
        grid_spec=pltpu.PrefetchScalarGridSpec(
            num_scalar_prefetch=1,
            grid=(width // HD,),
            in_specs=[rows] + [piece] * n,
            out_specs=rows,
        ),
        cost_estimate=pl.CostEstimate(
            flops=4 * work, transcendentals=work // HD, bytes_accessed=4 * width * (tokens + n * length)
        ),
        compiler_params=pltpu.CompilerParams(vmem_limit_bytes=48 << 20),
    )(table, query, *pieces)


def attend_back(table, query, grad, pieces, scale, first, heads):
    n = len(pieces)
    tokens = query.shape[0]
    length = pieces[0].shape[1]
    width = heads * HD
    rows = pl.BlockSpec((tokens, HD), lambda h, t: (0, first + h))
    piece = pl.BlockSpec((2, length, HD), lambda h, t: (0, 0, first + h))
    work = tokens * n * length * width
    return pl.pallas_call(
        functools.partial(backward_kernel, n, scale),
        out_shape=[jax.ShapeDtypeStruct((tokens, width), BF16)]
        + [jax.ShapeDtypeStruct((2, length, width), BF16)] * n,
        grid_spec=pltpu.PrefetchScalarGridSpec(
            num_scalar_prefetch=1,
            grid=(heads,),
            in_specs=[rows, rows] + [piece] * n,
            out_specs=[pl.BlockSpec((tokens, HD), lambda h, t: (0, h))]
            + [pl.BlockSpec((2, length, HD), lambda h, t: (0, 0, h))] * n,
            scratch_shapes=[pltpu.VMEM((n * length, tokens), BF16)] * 2,
        ),
        cost_estimate=pl.CostEstimate(
            flops=10 * work, transcendentals=work // HD, bytes_accessed=2 * width * (3 * tokens + 4 * n * length)
        ),
        compiler_params=pltpu.CompilerParams(vmem_limit_bytes=48 << 20),
    )(table, query, grad, *pieces)


def shift(array, n, by):
    return lax.ppermute(array, "seq", [(i, (i + by) % n) for i in range(n)])


def line_gather(block, n, me):
    right, left = [block], [block]
    for s in range(1, n):
        right.append(lax.ppermute(right[-1], "seq", [(i, i + 1) for i in range(s - 1, n - 1)]))
        left.append(lax.ppermute(left[-1], "seq", [(i, i - 1) for i in range(1, n - s + 1)]))
    parts = [block] + [jnp.where(me >= k, right[k], left[n - k]) for k in range(1, n)]
    return jnp.concatenate(parts, axis=0)


def line_scatter(partial, n):
    size = partial.shape[0] // n
    parts = [partial[k * size : (k + 1) * size].astype(F32) for k in range(n)]
    right = left = None
    for s in range(1, n):
        to_right = parts[s] if right is None else parts[s] + right.astype(F32)
        to_left = parts[n - s] if left is None else parts[n - s] + left.astype(F32)
        right = lax.ppermute(to_right.astype(BF16), "seq", [(i, i + 1) for i in range(s)])
        left = lax.ppermute(to_left.astype(BF16), "seq", [(i, i - 1) for i in range(n - s, n)])
    return (parts[0] + right.astype(F32) + left.astype(F32)).astype(BF16)


def body(video, cotangent, w_query, w_out, ref_kv, tile_lists):
    n = lax.axis_size("seq")
    me = lax.axis_index("seq")
    width = w_query.shape[1]
    heads = width // HD
    chunks = 3 if heads % 3 == 0 else 1
    length = ref_kv.shape[2]
    ref_tiles = length * n // TILE // tile_lists.shape[1]
    scale = 1.0 / math.sqrt(HD)
    table = tile_table(tile_lists[0], ref_tiles, me, n)

    gathered = line_gather(video[0], n, me)
    pieces = []
    for k in range(n):
        columns = lax.rem(me + k, n) * width
        piece = lax.dynamic_slice_in_dim(ref_kv[0], columns, width, axis=2)
        pieces.append(piece if k == 0 else shift(piece, n, k))
    query = jnp.dot(gathered, w_query, preferred_element_type=F32).astype(BF16)
    attention = attend(table, query, pieces, scale)

    late = lax.optimization_barrier((cotangent[0], *pieces[1:]))[0]
    grad_rows = line_gather(late, n, me)
    output = line_scatter(jnp.dot(attention, w_out, preferred_element_type=F32), n)

    grad_attention = contract_last(grad_rows, w_out).astype(BF16)
    grad_wo = contract_first(attention, grad_rows).astype(BF16)
    grad_wo = lax.psum(grad_wo, "dp").astype(F32)

    grad_ref = jnp.zeros(ref_kv.shape[1:], BF16)
    grad_query = []
    per = heads // chunks
    for c in range(chunks):
        back = attend_back(table, query, grad_attention, pieces, scale, c * per, per)
        grad_query.append(back[0])
        for k in range(n):
            block = back[1 + k] if k == 0 else shift(back[1 + k], n, -k)
            columns = lax.rem(me + k, n) * width + c * per * HD
            grad_ref = lax.dynamic_update_slice_in_dim(grad_ref, block, columns, axis=2)
    grad_query = jnp.concatenate(grad_query, axis=1)
    grad_video = line_scatter(contract_last(grad_query, w_query).astype(BF16), n)
    grad_wq = contract_first(gathered, grad_query).astype(BF16)
    grad_wq = lax.psum(grad_wq, "dp").astype(F32)
    return (output[None], grad_video[None], grad_wq, grad_wo, grad_ref[None])


def solution(mesh):
    in_specs = (
        P("dp", "seq", None),
        P("dp", "seq", None),
        P(None, "seq"),
        P("seq", None),
        P("dp", None, "seq", None),
        P("dp", None, None, None),
    )
    out_specs = (
        P("dp", "seq", None),
        P("dp", "seq", None),
        P(None, "seq"),
        P("seq", None),
        P("dp", None, "seq", None),
    )
    return jax.shard_map(body, mesh=mesh, in_specs=in_specs, out_specs=out_specs, check_vma=False)
```

time: 664 us -> 390 us (0.59)
  waiting for transfers between devices: 355 us -> 200 us
  matrix products: 106 us -> 24.9 us
  blocking collectives: 74.7 us -> 0 us
  local copies, waits for them, and re-layouts: 82 us -> 9.6 us
  starting transfers between devices: 6.61 us -> 77.9 us
  Pallas kernels: 0 us -> 35.9 us
    ppermute x0 -> x36, waiting for transfers between devices: none -> 200 us  [the longest x12 89.8 us: shift(): return lax.ppermute(array, 'seq', [(i, (i + by) % n) for i in range(n)])]
    all_gather x2 -> x0, waiting for transfers between devices: 163 us -> none  [the longest x1 109 us: body(): grad_rows = lax.all_gather(cotangent, 'seq', axis=1, tiled=True)[0]]
    reduce_scatter x2 -> x0, waiting for transfers between devices: 159 us -> none  [the longest x1 97.3 us: body(): lax.psum_scatter(jnp.dot(rows, w_out, preferred_element_type=jnp.float32)...]
    ppermute x0 -> x36, starting transfers between devices: none -> 77.9 us  [the longest x6 27.8 us: line_scatter(): lax.ppermute(to_right.astype(BF16), 'seq', [(i, i + 1) for i in range(s)])]
    all_to_all x1 -> x0, blocking collectives: 74.7 us -> none  [body(): lax.all_to_all(grad_kv, 'seq', split_axis=2, concat_axis=3, tiled=True)]
    pallas_call x0 -> x4, Pallas kernels: none -> 35.9 us  [the longest x3 22.7 us: attend_back(): pl.pallas_call(functools.partial(backward_kernel, n, scale), out_shape=[j...]
    dot_general x20 -> x2, matrix products: 44.7 us -> 9.24 us  [contract_last(): lax.dot_general(left, right, (((1,), (1,)), ((), ())), preferred_element_...]
    psum x1, waiting for transfers between devices: 31.6 us -> 0.01 us  [body(): grad_wq = lax.psum(grad_wq, 'dp').astype(F32)]
  transfers between devices with their start and end apart: 6 -> 37, of which waited for: 5 -> 15; matrix products, arithmetic and copies ran while one was open for 12% -> 12% of each run, Pallas kernels for 0% -> 9%
where the time goes in v1:
time: 390 us; the launch traced here: 389 us
  waiting for transfers between devices  200 us (51%)
  starting transfers between devices  77.9 us (20%)
  Pallas kernels  35.9 us (9%)
  other arithmetic  25.5 us (7%)
  matrix products  24.9 us (6%)
  between operations  14.9 us (4%)
  local copies, waits for them, and re-layouts  9.6 us (2%)
    ppermute x12, waiting for transfers between devices, shift(): return lax.ppermute(array, 'seq', [(i, (i + by) % n) for i in range(n)])  89.8 us
    ppermute x6, waiting for transfers between devices, line_scatter(): lax.ppermute(to_right.astype(BF16), 'seq', [(i, i + 1) for i in range(s)])  65 us
    ppermute x6, waiting for transfers between devices, line_gather(): lax.ppermute(left[-1], 'seq', [(i, i - 1) for i in range(1, n - s + 1)])  38.9 us
    ppermute x6, starting transfers between devices, line_scatter(): lax.ppermute(to_right.astype(BF16), 'seq', [(i, i + 1) for i in range(s)])  27.8 us
    pallas_call x3, Pallas kernels, attend_back(): pl.pallas_call(functools.partial(backward_kernel, n, scale), out_shape=[j...  22.7 us
    ppermute x12, starting transfers between devices, shift(): return lax.ppermute(array, 'seq', [(i, (i + by) % n) for i in range(n)])  19.3 us
    ppermute x6, starting transfers between devices, line_gather(): lax.ppermute(right[-1], 'seq', [(i, i + 1) for i in range(s - 1, n - 1)])  16.8 us
    pallas_call x1, Pallas kernels, attend(): pl.pallas_call(functools.partial(forward_kernel, n, scale), out_shape=jax...  13.2 us
  transfers between devices with their start and end apart: 37, of which 15 were waited for; matrix products, arithmetic and copies ran while one was open for 12% of the time, Pallas kernels for 9%

profile of v1, /device:TPU:0, one launch (start us, length us, event | category | flops | bytes accessed | tf_op | source)
XLA Modules:
  0.0 388.9 jit_solution(13914979114805265326)
XLA Ops:
  8.5 6.5 %collective-permute-start = (bf16[128,3072]{1,0:T(8,128)(2,1)}, bf16[128,3072]{1,0:T(8,128)(2,1)}, u32[]{:S(2)}, u32[]{:S(2)}) collective-permute-start(bf16[128,3072]{1,0:T(8,128)(2,1)} %bitcast.63), channel_id=1, source_target_pairs={{0,1},{1,2},{2,3},{4,5},{5,6},{6,7},{8,9},{9,10},{10,11},{12,13},{... | collective-permute-start | bytes 2359304 | tf_op jit(solution)/shard_map/ppermute | solution.py:159
  15.0 2.1 dynamic-slice_bitcast_fusion
  17.1 1.9 collective-permute-start.8
  19.2 3.0 collective-permute-start.7
  22.2 8.6 %collective-permute-done.1 = bf16[128,3072]{1,0:T(8,128)(2,1)} collective-permute-done((bf16[128,3072]{1,0:T(8,128)(2,1)}, bf16[128,3072]{1,0:T(8,128)(2,1)}, u32[]{:S(2)}, u32[]{:S(2)}) %collective-permute-start.1) | collective-permute-done | bytes 786464 | tf_op jit(solution)/shard_map/ppermute | solution.py:160
  32.3 1.5 collective-permute-start.4
  34.0 15.1 %collective-permute-done.8.refs_3_ = bf16[2,256,768]{2,1,0:T(8,128)(2,1)S(1)} collective-permute-done((bf16[2,256,768]{2,1,0:T(8,128)(2,1)S(1)}, bf16[2,256,768]{2,1,0:T(8,128)(2,1)S(1)}, u32[]{:S(2)}, u32[]{:S(2)}) %collective-permute-start.8) | collective-permute-done | bytes 786464 | tf_op jit(solution)/shard_map/ppermute | solution.py:153
  49.1 17.9 %collective-permute-done.6.refs_1_ = bf16[2,256,768]{2,1,0:T(8,128)(2,1)S(1)} collective-permute-done((bf16[2,256,768]{2,1,0:T(8,128)(2,1)S(1)}, bf16[2,256,768]{2,1,0:T(8,128)(2,1)S(1)}, u32[]{:S(2)}, u32[]{:S(2)}) %collective-permute-start.6) | collective-permute-done | bytes 786464 | tf_op jit(solution)/shard_map/ppermute | solution.py:153
  67.0 32.6 %collective-permute-done.7.refs_2_ = bf16[2,256,768]{2,1,0:T(8,128)(2,1)S(1)} collective-permute-done((bf16[2,256,768]{2,1,0:T(8,128)(2,1)S(1)}, bf16[2,256,768]{2,1,0:T(8,128)(2,1)S(1)}, u32[]{:S(2)}, u32[]{:S(2)}) %collective-permute-start.7) | collective-permute-done | bytes 786464 | tf_op jit(solution)/shard_map/ppermute | solution.py:153
  100.9 5.5 %collective-permute-start.15 = (bf16[128,3072]{1,0:T(8,128)(2,1)}, bf16[128,3072]{1,0:T(8,128)(2,1)}, u32[]{:S(2)}, u32[]{:S(2)}) collective-permute-start(bf16[128,3072]{1,0:T(8,128)(2,1)} %bitcast.13), channel_id=1, source_target_pairs={{0,1},{1,2},{2,3},{4,5},{5,6},{6,7},{8,9},{9,10},{10,11},{12,13},{... | collective-permute-start | bytes 2359304 | tf_op jit(solution)/shard_map/ppermute | solution.py:159
  110.1 1.7 broadcast_select_fusion.3
  111.7 9.0 %collective-permute-done.16 = bf16[128,3072]{1,0:T(8,128)(2,1)} collective-permute-done((bf16[128,3072]{1,0:T(8,128)(2,1)}, bf16[128,3072]{1,0:T(8,128)(2,1)}, u32[]{:S(2)}, u32[]{:S(2)}) %collective-permute-start.16) | collective-permute-done | bytes 786464 | tf_op jit(solution)/shard_map/ppermute | solution.py:160
  122.0 1.6 collective-permute-start.19
  123.6 13.4 %collective-permute-done.3 = bf16[128,3072]{1,0:T(8,128)(2,1)} collective-permute-done((bf16[128,3072]{1,0:T(8,128)(2,1)}, bf16[128,3072]{1,0:T(8,128)(2,1)}, u32[]{:S(2)}, u32[]{:S(2)}) %collective-permute-start.3) | collective-permute-done | bytes 786464 | tf_op jit(solution)/shard_map/ppermute | solution.py:160
  138.2 1.5 broadcast_select_fusion.1
  139.8 2.6 convolution_convert_fusion.4.q_ref
  142.4 13.2 %shard_map.101 = bf16[512,768]{1,0:T(8,128)(2,1)S(1)} custom-call(s32[4,8]{1,0:T(4,128)S(1)} %copy.20.table_ref, bf16[512,768]{1,0:T(8,128)(2,1)S(1)} %convolution_convert_fusion.4.q_ref, bf16[2,256,768]{2,1,0:T(8,128)(2,1)S(1)} %get-tuple-element.51.refs_0_, bf16[2,256,768]{2,1,0:T(8,128)(2,1)S(1)} %collective-permute-done.6.refs_1_, ...), custom_call_target="tpu_custom_call" | custom-call | flops 1610612736 | bytes 4718592 | tf_op jit(solution)/shard_map/pallas_call | solution.py:109
  155.7 2.6 fusion.15
  159.6 1.9 fusion.13
  161.5 6.3 %collective-permute-start.9 = (bf16[128,3072]{1,0:T(8,128)(2,1)}, bf16[128,3072]{1,0:T(8,128)(2,1)}, u32[]{:S(2)}, u32[]{:S(2)}) collective-permute-start(bf16[128,3072]{1,0:T(8,128)(2,1)} %get-tuple-element.41), channel_id=1, source_target_pairs={{0,1},{4,5},{8,9},{12,13},{16,17},{20,21},{24,25},{28,29}} | collective-permute-start | bytes 2359304 | tf_op jit(solution)/shard_map/ppermute | solution.py:172
  167.8 1.6 collective-permute-start.12
  171.5 8.0 %collective-permute-done.18 = bf16[128,3072]{1,0:T(8,128)(2,1)S(1)} collective-permute-done((bf16[128,3072]{1,0:T(8,128)(2,1)}, bf16[128,3072]{1,0:T(8,128)(2,1)S(1)}, u32[]{:S(2)}, u32[]{:S(2)}) %collective-permute-start.18) | collective-permute-done | bytes 786464 | tf_op jit(solution)/shard_map/ppermute | solution.py:160
  180.8 3.8 convolution_convert_fusion.3.g_ref
  184.6 6.1 %convolution_convert_fusion = bf16[768,3072]{1,0:T(8,128)(2,1)} fusion(bf16[512,768]{1,0:T(8,128)(2,1)S(1)} %shard_map.101, bf16[128,3072]{1,0:T(8,128)(2,1)S(1)} %broadcast_select_fusion, bf16[128,3072]{1,0:T(8,128)(2,1)S(1)} %broadcast_select_fusion.2, bf16[128,3072]{1,0:T(8,128)(2,1)S(1)} %broadcast_select_fusion.4, bf16[128,3072]{1,0:T(8,128)(2,1)} %bitcast.13), kind=kOutput, calls=%fused_computation.2 | convolution fusion | flops 2430861312 | bytes 8650752 | tf_op jit(solution)/shard_map/dot_general | solution.py:23
  190.7 7.6 %shard_map.104 = (bf16[512,256]{1,0:T(8,128)(2,1)S(1)}, bf16[2,256,256]{2,1,0:T(8,128)(2,1)S(1)}, bf16[2,256,256]{2,1,0:T(8,128)(2,1)}, bf16[2,256,256]{2,1,0:T(8,128)(2,1)S(1)}, bf16[2,256,256]{2,1,0:T(8,128)(2,1)S(1)}) custom-call(s32[4,8]{1,0:T(4,128)S(1)} %copy.20.table_ref, bf16[512,768]{1,0:T(8,128)(2,1)S(1)} %convolution_convert_fusion.4.q_ref, ...), custom_call_target="tpu_custom_call" | custom-call | flops 1342177280 | bytes 2883584 | tf_op jit(solution)/shard_map/pallas_call | solution.py:133
  198.2 8.1 %collective-permute-start.33 = (bf16[2,256,256]{2,1,0:T(8,128)(2,1)}, bf16[2,256,256]{2,1,0:T(8,128)(2,1)}, u32[]{:S(2)}, u32[]{:S(2)}) collective-permute-start(bf16[2,256,256]{2,1,0:T(8,128)(2,1)} %get-tuple-element.34), channel_id=1, source_target_pairs={{0,3},{1,0},{2,1},{3,2},{4,7},{5,4},{6,5},{7,6},{8,11},{9,8},{10,9... | collective-permute-start | bytes 786440 | tf_op jit(solution)/shard_map/ppermute | solution.py:153
  206.4 7.6 %shard_map.103 = (bf16[512,256]{1,0:T(8,128)(2,1)S(1)}, bf16[2,256,256]{2,1,0:T(8,128)(2,1)S(1)}, bf16[2,256,256]{2,1,0:T(8,128)(2,1)}, bf16[2,256,256]{2,1,0:T(8,128)(2,1)S(1)}, bf16[2,256,256]{2,1,0:T(8,128)(2,1)S(1)}) custom-call(s32[4,8]{1,0:T(4,128)S(1)} %copy.20.table_ref, bf16[512,768]{1,0:T(8,128)(2,1)S(1)} %convolution_convert_fusion.4.q_ref, ...), custom_call_target="tpu_custom_call" | custom-call | flops 1342177280 | bytes 2883584 | tf_op jit(solution)/shard_map/pallas_call | solution.py:133
  215.7 7.5 %shard_map.102 = (bf16[512,256]{1,0:T(8,128)(2,1)S(1)}, bf16[2,256,256]{2,1,0:T(8,128)(2,1)S(1)}, bf16[2,256,256]{2,1,0:T(8,128)(2,1)}, bf16[2,256,256]{2,1,0:T(8,128)(2,1)S(1)}, bf16[2,256,256]{2,1,0:T(8,128)(2,1)S(1)}) custom-call(s32[4,8]{1,0:T(4,128)S(1)} %copy.20.table_ref, bf16[512,768]{1,0:T(8,128)(2,1)S(1)} %convolution_convert_fusion.4.q_ref, ...), custom_call_target="tpu_custom_call" | custom-call | flops 1342177280 | bytes 2883584 | tf_op jit(solution)/shard_map/pallas_call | solution.py:133
  224.1 4.3 %convolution_convert_fusion.1 = bf16[3072,768]{1,0:T(8,128)(2,1)} fusion(bf16[512,768]{1,0:T(8,128)(2,1)S(1)} %constant_dynamic-update-slice_fusion, bf16[128,3072]{1,0:T(8,128)(2,1)S(1)} %copy-done.20, bf16[128,3072]{1,0:T(8,128)(2,1)S(1)} %copy-done.16, bf16[128,3072]{1,0:T(8,128)(2,1)S(1)} %copy-done.18, bf16[128,3072]{1,0:T(8,128)(2,1)S(1)} %bitcast.65), kind=kOutput, calls=%fused_computation.3 | convolution fusion | flops 2430861312 | bytes 8650752 | tf_op jit(solution)/shard_map/dot_general | solution.py:23
  228.9 5.4 %convolution_convert_fusion.2 = bf16[512,3072]{1,0:T(8,128)(2,1)S(1)} fusion(bf16[512,768]{1,0:T(8,128)(2,1)S(1)} %constant_dynamic-update-slice_fusion, bf16[3072,768]{1,0:T(8,128)(2,1)} %param.8), kind=kOutput, calls=%fused_computation.4 | convolution fusion | flops 2417491968 | bytes 8650752 | tf_op jit(solution)/shard_map/dot_general | solution.py:19
  234.4 2.1 collective-permute-start.28
  236.5 1.3 add_convert_fusion.6
  238.1 17.1 %collective-permute-done.28 = bf16[2,256,256]{2,1,0:T(8,128)(2,1)S(1)} collective-permute-done((bf16[2,256,256]{2,1,0:T(8,128)(2,1)S(1)}, bf16[2,256,256]{2,1,0:T(8,128)(2,1)S(1)}, u32[]{:S(2)}, u32[]{:S(2)}) %collective-permute-start.28) | collective-permute-done | bytes 262176 | tf_op jit(solution)/shard_map/ppermute | solution.py:153
  255.4 5.4 %collective-permute-start.21 = (bf16[128,3072]{1,0:T(8,128)(2,1)S(1)}, bf16[128,3072]{1,0:T(8,128)(2,1)S(1)}, u32[]{:S(2)}, u32[]{:S(2)}) collective-permute-start(bf16[128,3072]{1,0:T(8,128)(2,1)S(1)} %get-tuple-element.47), channel_id=1, source_target_pairs={{0,1},{4,5},{8,9},{12,13},{16,17},{20,21},{24,25},{28,29}} | collective-permute-start | bytes 2359304 | tf_op jit(solution)/shard_map/ppermute | solution.py:172
  261.8 7.0 %collective-permute-done.31 = bf16[2,256,256]{2,1,0:T(8,128)(2,1)S(1)} collective-permute-done((bf16[2,256,256]{2,1,0:T(8,128)(2,1)S(1)}, bf16[2,256,256]{2,1,0:T(8,128)(2,1)S(1)}, u32[]{:S(2)}, u32[]{:S(2)}) %collective-permute-start.31) | collective-permute-done | bytes 262176 | tf_op jit(solution)/shard_map/ppermute | solution.py:153
  269.9 4.6 %collective-permute-start.10 = (bf16[128,3072]{1,0:T(8,128)(2,1)S(1)}, bf16[128,3072]{1,0:T(8,128)(2,1)S(1)}, u32[]{:S(2)}, u32[]{:S(2)}) collective-permute-start(bf16[128,3072]{1,0:T(8,128)(2,1)S(1)} %add_convert_fusion.6), channel_id=1, source_target_pairs={{0,1},{1,2},{4,5},{5,6},{8,9},{9,10},{12,13},{13,14},{16,17},{17,1... | collective-permute-start | bytes 2359304 | tf_op jit(solution)/shard_map/ppermute | solution.py:172
  275.5 8.9 %collective-permute-done.21 = bf16[128,3072]{1,0:T(8,128)(2,1)S(1)} collective-permute-done((bf16[128,3072]{1,0:T(8,128)(2,1)S(1)}, bf16[128,3072]{1,0:T(8,128)(2,1)S(1)}, u32[]{:S(2)}, u32[]{:S(2)}) %collective-permute-start.21) | collective-permute-done | bytes 786464 | tf_op jit(solution)/shard_map/ppermute | solution.py:172
  284.5 2.5 collective-permute-start.35
  287.3 2.0 collective-permute-start.22
  290.0 16.9 %collective-permute-done.10 = bf16[128,3072]{1,0:T(8,128)(2,1)S(1)} collective-permute-done((bf16[128,3072]{1,0:T(8,128)(2,1)S(1)}, bf16[128,3072]{1,0:T(8,128)(2,1)S(1)}, u32[]{:S(2)}, u32[]{:S(2)}) %collective-permute-start.10) | collective-permute-done | bytes 786464 | tf_op jit(solution)/shard_map/ppermute | solution.py:172
  307.0 1.6 add_convert_fusion.5
  309.4 5.0 %collective-permute-start.11 = (bf16[128,3072]{1,0:T(8,128)(2,1)S(1)}, bf16[128,3072]{1,0:T(8,128)(2,1)S(1)}, u32[]{:S(2)}, u32[]{:S(2)}) collective-permute-start(bf16[128,3072]{1,0:T(8,128)(2,1)S(1)} %get-tuple-element.39), channel_id=1, source_target_pairs={{0,1},{1,2},{2,3},{4,5},{5,6},{6,7},{8,9},{9,10},{10,11},{12,13},{... | collective-permute-start | bytes 2359304 | tf_op jit(solution)/shard_map/ppermute | solution.py:172
  314.4 15.1 %collective-permute-done.22 = bf16[128,3072]{1,0:T(8,128)(2,1)S(1)} collective-permute-done((bf16[128,3072]{1,0:T(8,128)(2,1)S(1)}, bf16[128,3072]{1,0:T(8,128)(2,1)S(1)}, u32[]{:S(2)}, u32[]{:S(2)}) %collective-permute-start.22) | collective-permute-done | bytes 786464 | tf_op jit(solution)/shard_map/ppermute | solution.py:172
  330.0 4.4 %collective-permute-start.23 = (bf16[128,3072]{1,0:T(8,128)(2,1)S(1)}, bf16[128,3072]{1,0:T(8,128)(2,1)S(1)}, u32[]{:S(2)}, u32[]{:S(2)}) collective-permute-start(bf16[128,3072]{1,0:T(8,128)(2,1)S(1)} %get-tuple-element.43), channel_id=1, source_target_pairs={{0,1},{1,2},{2,3},{4,5},{5,6},{6,7},{8,9},{9,10},{10,11},{12,13},{... | collective-permute-start | bytes 2359304 | tf_op jit(solution)/shard_map/ppermute | solution.py:172
  337.3 24.0 %collective-permute-done.23 = bf16[128,3072]{1,0:T(8,128)(2,1)S(1)} collective-permute-done((bf16[128,3072]{1,0:T(8,128)(2,1)S(1)}, bf16[128,3072]{1,0:T(8,128)(2,1)S(1)}, u32[]{:S(2)}, u32[]{:S(2)}) %collective-permute-start.23) | collective-permute-done | bytes 786464 | tf_op jit(solution)/shard_map/ppermute | solution.py:172
  362.6 6.3 %collective-permute-done.14 = bf16[128,3072]{1,0:T(8,128)(2,1)S(1)} collective-permute-done((bf16[128,3072]{1,0:T(8,128)(2,1)S(1)}, bf16[128,3072]{1,0:T(8,128)(2,1)S(1)}, u32[]{:S(2)}, u32[]{:S(2)}) %collective-permute-start.14) | collective-permute-done | bytes 786464 | tf_op jit(solution)/shard_map/ppermute | solution.py:173
  370.0 7.0 %convert_element_type.158 = f32[3072,768]{1,0:T(8,128)} convert(bf16[3072,768]{1,0:T(8,128)(2,1)} %get-tuple-element.37) | non-fusion elementwise | flops 2359296 | bytes 14155776 | tf_op jit(solution)/shard_map/convert_element_type | solution.py:218
  377.0 5.0 %convert_element_type.160 = f32[768,3072]{1,0:T(8,128)} convert(bf16[768,3072]{1,0:T(8,128)(2,1)S(1)} %copy-done.13) | non-fusion elementwise | flops 2359296 | bytes 14155776 | tf_op jit(solution)/shard_map/convert_element_type | solution.py:203
  (142 shorter events, 29.1 us)
Async XLA Ops:
  7.2 362.8 %all-reduce.3.cloned.1.call-start = ((), (), s32[]{:S(2)}) async-start(), calls=%async_computation | async-start | bytes 18874368 | tf_op jit(solution)/shard_map/psum | solution.py:218
  7.2 23.6 %collective-permute-start.1 = (bf16[128,3072]{1,0:T(8,128)(2,1)}, bf16[128,3072]{1,0:T(8,128)(2,1)}, u32[]{:S(2)}, u32[]{:S(2)}) collective-permute-start(bf16[128,3072]{1,0:T(8,128)(2,1)} %bitcast.62), channel_id=1, source_target_pairs={{1,0},{2,1},{3,2},{5,4},{6,5},{7,6},{9,8},{10,9},{11,10},{13,12},{... | collective-permute-start | bytes 2359304 | tf_op jit(solution)/shard_map/ppermute | solution.py:160
  8.5 23.8 %collective-permute-start = (bf16[128,3072]{1,0:T(8,128)(2,1)}, bf16[128,3072]{1,0:T(8,128)(2,1)}, u32[]{:S(2)}, u32[]{:S(2)}) collective-permute-start(bf16[128,3072]{1,0:T(8,128)(2,1)} %bitcast.63), channel_id=1, source_target_pairs={{0,1},{1,2},{2,3},{4,5},{5,6},{6,7},{8,9},{9,10},{10,11},{12,13},{... | collective-permute-start | bytes 2359304 | tf_op jit(solution)/shard_map/ppermute | solution.py:159
  15.0 18.9 %copy-start.21 = (s32[1,2,4,3]{2,1,3,0:T(2,128)S(1)}, s32[1,2,4,3]{2,1,3,0:T(2,128)}, u32[]{:S(2)}) copy-start(s32[1,2,4,3]{2,1,3,0:T(2,128)} %param.11) | copy-start | bytes 292
  17.1 32.0 %collective-permute-start.8 = (bf16[2,256,768]{2,1,0:T(8,128)(2,1)S(1)}, bf16[2,256,768]{2,1,0:T(8,128)(2,1)S(1)}, u32[]{:S(2)}, u32[]{:S(2)}) collective-permute-start(bf16[2,256,768]{2,1,0:T(8,128)(2,1)S(1)} %get-tuple-element.49), channel_id=1, source_target_pairs={{0,3},{1,0},{2,1},{3,2},{4,7},{5,4},{6,5},{7,6},{8,11},{9,8},{10,9... | collective-permute-start | bytes 2359304 | tf_op jit(solution)/shard_map/ppermute | solution.py:153
  19.0 48.0 %collective-permute-start.6 = (bf16[2,256,768]{2,1,0:T(8,128)(2,1)S(1)}, bf16[2,256,768]{2,1,0:T(8,128)(2,1)S(1)}, u32[]{:S(2)}, u32[]{:S(2)}) collective-permute-start(bf16[2,256,768]{2,1,0:T(8,128)(2,1)S(1)} %get-tuple-element.50), channel_id=1, source_target_pairs={{0,1},{1,2},{2,3},{3,0},{4,5},{5,6},{6,7},{7,4},{8,9},{9,10},{10,1... | collective-permute-start | bytes 2359304 | tf_op jit(solution)/shard_map/ppermute | solution.py:153
  19.2 80.5 %collective-permute-start.7 = (bf16[2,256,768]{2,1,0:T(8,128)(2,1)S(1)}, bf16[2,256,768]{2,1,0:T(8,128)(2,1)S(1)}, u32[]{:S(2)}, u32[]{:S(2)}) collective-permute-start(bf16[2,256,768]{2,1,0:T(8,128)(2,1)S(1)} %get-tuple-element.52), channel_id=1, source_target_pairs={{0,2},{1,3},{2,0},{3,1},{4,6},{5,7},{6,4},{7,5},{8,10},{9,11},{10,... | collective-permute-start | bytes 2359304 | tf_op jit(solution)/shard_map/ppermute | solution.py:153
  30.8 75.6 %collective-permute-start.2 = (bf16[128,3072]{1,0:T(8,128)(2,1)}, bf16[128,3072]{1,0:T(8,128)(2,1)}, u32[]{:S(2)}, u32[]{:S(2)}) collective-permute-start(bf16[128,3072]{1,0:T(8,128)(2,1)} %collective-permute-done.1), channel_id=1, source_target_pairs={{1,0},{2,1},{5,4},{6,5},{9,8},{10,9},{13,12},{14,13},{17,16},{18,1... | collective-permute-start | bytes 2359304 | tf_op jit(solution)/shard_map/ppermute | solution.py:160
  32.3 76.9 %collective-permute-start.4 = (bf16[128,3072]{1,0:T(8,128)(2,1)}, bf16[128,3072]{1,0:T(8,128)(2,1)}, u32[]{:S(2)}, u32[]{:S(2)}) collective-permute-start(bf16[128,3072]{1,0:T(8,128)(2,1)} %collective-permute-done), channel_id=1, source_target_pairs={{1,2},{2,3},{5,6},{6,7},{9,10},{10,11},{13,14},{14,15},{17,18},{18... | collective-permute-start | bytes 2359304 | tf_op jit(solution)/shard_map/ppermute | solution.py:159
  99.6 42.8 %copy-start = (bf16[2,256,768]{2,1,0:T(8,128)(2,1)}, bf16[2,256,768]{2,1,0:T(8,128)(2,1)S(1)}, u32[]{:S(2)}) copy-start(bf16[2,256,768]{2,1,0:T(8,128)(2,1)S(1)} %collective-permute-done.7.refs_2_) | copy-start | bytes 2359300
  99.6 21.1 %collective-permute-start.16 = (bf16[128,3072]{1,0:T(8,128)(2,1)}, bf16[128,3072]{1,0:T(8,128)(2,1)}, u32[]{:S(2)}, u32[]{:S(2)}) collective-permute-start(bf16[128,3072]{1,0:T(8,128)(2,1)} %bitcast.13), channel_id=1, source_target_pairs={{1,0},{2,1},{3,2},{5,4},{6,5},{7,6},{9,8},{10,9},{11,10},{13,12},{... | collective-permute-start | bytes 2359304 | tf_op jit(solution)/shard_map/ppermute | solution.py:160
  100.9 21.1 %collective-permute-start.15 = (bf16[128,3072]{1,0:T(8,128)(2,1)}, bf16[128,3072]{1,0:T(8,128)(2,1)}, u32[]{:S(2)}, u32[]{:S(2)}) collective-permute-start(bf16[128,3072]{1,0:T(8,128)(2,1)} %bitcast.13), channel_id=1, source_target_pairs={{0,1},{1,2},{2,3},{4,5},{5,6},{6,7},{8,9},{9,10},{10,11},{12,13},{... | collective-permute-start | bytes 2359304 | tf_op jit(solution)/shard_map/ppermute | solution.py:159
  106.5 30.5 %collective-permute-start.3 = (bf16[128,3072]{1,0:T(8,128)(2,1)}, bf16[128,3072]{1,0:T(8,128)(2,1)}, u32[]{:S(2)}, u32[]{:S(2)}) collective-permute-start(bf16[128,3072]{1,0:T(8,128)(2,1)} %collective-permute-done.2), channel_id=1, source_target_pairs={{1,0},{5,4},{9,8},{13,12},{17,16},{21,20},{25,24},{29,28}} | collective-permute-start | bytes 2359304 | tf_op jit(solution)/shard_map/ppermute | solution.py:160
  109.2 30.5 %copy-start.22 = (bf16[3072,768]{1,0:T(8,128)(2,1)S(1)}, bf16[3072,768]{1,0:T(8,128)(2,1)}, u32[]{:S(2)}) copy-start(bf16[3072,768]{1,0:T(8,128)(2,1)} %param.8) | copy-start | bytes 14155780
  109.2 30.6 %copy-start.23 = (bf16[1,128,3072]{2,1,0:T(8,128)(2,1)S(1)}, bf16[1,128,3072]{2,1,0:T(8,128)(2,1)}, u32[]{:S(2)}) copy-start(bf16[1,128,3072]{2,1,0:T(8,128)(2,1)} %param.6) | copy-start | bytes 2359300
  109.2 29.0 %collective-permute-start.5 = (bf16[128,3072]{1,0:T(8,128)(2,1)}, bf16[128,3072]{1,0:T(8,128)(2,1)S(1)}, u32[]{:S(2)}, u32[]{:S(2)}) collective-permute-start(bf16[128,3072]{1,0:T(8,128)(2,1)} %collective-permute-done.4), channel_id=1, source_target_pairs={{2,3},{6,7},{10,11},{14,15},{18,19},{22,23},{26,27},{30,31}} | collective-permute-start | bytes 2359304 | tf_op jit(solution)/shard_map/ppermute | solution.py:159
  111.7 30.7 %copy-start.15 = (bf16[128,3072]{1,0:T(8,128)(2,1)}, bf16[128,3072]{1,0:T(8,128)(2,1)S(1)}, u32[]{:S(2)}) copy-start(bf16[128,3072]{1,0:T(8,128)(2,1)S(1)} %broadcast_select_fusion.3) | copy-start | bytes 2359300
  120.7 37.6 %collective-permute-start.17 = (bf16[128,3072]{1,0:T(8,128)(2,1)}, bf16[128,3072]{1,0:T(8,128)(2,1)}, u32[]{:S(2)}, u32[]{:S(2)}) collective-permute-start(bf16[128,3072]{1,0:T(8,128)(2,1)} %collective-permute-done.16), channel_id=1, source_target_pairs={{1,0},{2,1},{5,4},{6,5},{9,8},{10,9},{13,12},{14,13},{17,16},{18,1... | collective-permute-start | bytes 2359304 | tf_op jit(solution)/shard_map/ppermute | solution.py:160
  122.0 47.3 %collective-permute-start.19 = (bf16[128,3072]{1,0:T(8,128)(2,1)}, bf16[128,3072]{1,0:T(8,128)(2,1)}, u32[]{:S(2)}, u32[]{:S(2)}) collective-permute-start(bf16[128,3072]{1,0:T(8,128)(2,1)} %collective-permute-done.15), channel_id=1, source_target_pairs={{1,2},{2,3},{5,6},{6,7},{9,10},{10,11},{13,14},{14,15},{17,18},{18... | collective-permute-start | bytes 2359304 | tf_op jit(solution)/shard_map/ppermute | solution.py:159
  138.2 17.5 %slice-start.2 = ((s8[4718592]{0:T(1024)(128)(4,1)}), s8[4194304]{0:T(1024)(128)(4,1)S(1)}, s32[]{:S(2)}) async-start(s8[4718592]{0:T(1024)(128)(4,1)} %bitcast.57), calls=%async_computation.3 | async-start | bytes 8388608
  158.3 21.3 %copy-start.12 = (f32[512,3072]{1,0:T(8,128)}, f32[512,3072]{1,0:T(8,128)S(1)}, u32[]{:S(2)}) copy-start(f32[512,3072]{1,0:T(8,128)S(1)} %fusion.15) | copy-start | bytes 18874372
  158.3 21.1 %collective-permute-start.18 = (bf16[128,3072]{1,0:T(8,128)(2,1)}, bf16[128,3072]{1,0:T(8,128)(2,1)S(1)}, u32[]{:S(2)}, u32[]{:S(2)}) collective-permute-start(bf16[128,3072]{1,0:T(8,128)(2,1)} %collective-permute-done.17), channel_id=1, source_target_pairs={{1,0},{5,4},{9,8},{13,12},{17,16},{21,20},{25,24},{29,28}} | collective-permute-start | bytes 2359304 | tf_op jit(solution)/shard_map/ppermute | solution.py:160
  161.5 72.9 %collective-permute-start.9 = (bf16[128,3072]{1,0:T(8,128)(2,1)}, bf16[128,3072]{1,0:T(8,128)(2,1)}, u32[]{:S(2)}, u32[]{:S(2)}) collective-permute-start(bf16[128,3072]{1,0:T(8,128)(2,1)} %get-tuple-element.41), channel_id=1, source_target_pairs={{0,1},{4,5},{8,9},{12,13},{16,17},{20,21},{24,25},{28,29}} | collective-permute-start | bytes 2359304 | tf_op jit(solution)/shard_map/ppermute | solution.py:172
  167.8 121.5 %collective-permute-start.12 = (bf16[128,3072]{1,0:T(8,128)(2,1)}, bf16[128,3072]{1,0:T(8,128)(2,1)}, u32[]{:S(2)}, u32[]{:S(2)}) collective-permute-start(bf16[128,3072]{1,0:T(8,128)(2,1)} %get-tuple-element.42), channel_id=1, source_target_pairs={{3,2},{7,6},{11,10},{15,14},{19,18},{23,22},{27,26},{31,30}} | collective-permute-start | bytes 2359304 | tf_op jit(solution)/shard_map/ppermute | solution.py:173
  169.4 10.2 %collective-permute-start.20 = (bf16[128,3072]{1,0:T(8,128)(2,1)}, bf16[128,3072]{1,0:T(8,128)(2,1)S(1)}, u32[]{:S(2)}, u32[]{:S(2)}) collective-permute-start(bf16[128,3072]{1,0:T(8,128)(2,1)} %collective-permute-done.19), channel_id=1, source_target_pairs={{2,3},{6,7},{10,11},{14,15},{18,19},{22,23},{26,27},{30,31}} | collective-permute-start | bytes 2359304 | tf_op jit(solution)/shard_map/ppermute | solution.py:159
  198.2 71.6 %collective-permute-start.33 = (bf16[2,256,256]{2,1,0:T(8,128)(2,1)}, bf16[2,256,256]{2,1,0:T(8,128)(2,1)}, u32[]{:S(2)}, u32[]{:S(2)}) collective-permute-start(bf16[2,256,256]{2,1,0:T(8,128)(2,1)} %get-tuple-element.34), channel_id=1, source_target_pairs={{0,3},{1,0},{2,1},{3,2},{4,7},{5,4},{6,5},{7,6},{8,11},{9,8},{10,9... | collective-permute-start | bytes 786440 | tf_op jit(solution)/shard_map/ppermute | solution.py:153
  214.7 40.7 %collective-permute-start.30 = (bf16[2,256,256]{2,1,0:T(8,128)(2,1)}, bf16[2,256,256]{2,1,0:T(8,128)(2,1)}, u32[]{:S(2)}, u32[]{:S(2)}) collective-permute-start(bf16[2,256,256]{2,1,0:T(8,128)(2,1)} %get-tuple-element.30), channel_id=1, source_target_pairs={{0,3},{1,0},{2,1},{3,2},{4,7},{5,4},{6,5},{7,6},{8,11},{9,8},{10,9... | collective-permute-start | bytes 786440 | tf_op jit(solution)/shard_map/ppermute | solution.py:153
  223.3 14.7 %collective-permute-start.27 = (bf16[2,256,256]{2,1,0:T(8,128)(2,1)}, bf16[2,256,256]{2,1,0:T(8,128)(2,1)S(1)}, u32[]{:S(2)}, u32[]{:S(2)}) collective-permute-start(bf16[2,256,256]{2,1,0:T(8,128)(2,1)} %get-tuple-element.26), channel_id=1, source_target_pairs={{0,3},{1,0},{2,1},{3,2},{4,7},{5,4},{6,5},{7,6},{8,11},{9,8},{10,9... | collective-permute-start | bytes 786440 | tf_op jit(solution)/shard_map/ppermute | solution.py:153
  234.4 20.8 %copy-start.7 = (bf16[2,256,256]{2,1,0:T(8,128)(2,1)S(1)}, bf16[2,256,256]{2,1,0:T(8,128)(2,1)}, u32[]{:S(2)}) copy-start(bf16[2,256,256]{2,1,0:T(8,128)(2,1)} %copy-done.6) | copy-start | bytes 786436
  234.4 20.8 %copy-start.5 = (bf16[2,256,256]{2,1,0:T(8,128)(2,1)S(1)}, bf16[2,256,256]{2,1,0:T(8,128)(2,1)}, u32[]{:S(2)}) copy-start(bf16[2,256,256]{2,1,0:T(8,128)(2,1)} %copy-done.4) | copy-start | bytes 786436
  234.4 20.8 %collective-permute-start.28 = (bf16[2,256,256]{2,1,0:T(8,128)(2,1)S(1)}, bf16[2,256,256]{2,1,0:T(8,128)(2,1)S(1)}, u32[]{:S(2)}, u32[]{:S(2)}) collective-permute-start(bf16[2,256,256]{2,1,0:T(8,128)(2,1)S(1)} %copy-done.11), channel_id=1, source_target_pairs={{0,2},{1,3},{2,0},{3,1},{4,6},{5,7},{6,4},{7,5},{8,10},{9,11},{10,... | collective-permute-start | bytes 786440 | tf_op jit(solution)/shard_map/ppermute | solution.py:153
  237.9 31.7 %copy-start.3 = (bf16[2,256,256]{2,1,0:T(8,128)(2,1)S(1)}, bf16[2,256,256]{2,1,0:T(8,128)(2,1)}, u32[]{:S(2)}) copy-start(bf16[2,256,256]{2,1,0:T(8,128)(2,1)} %copy-done.2) | copy-start | bytes 786436
  238.0 17.2 %collective-permute-start.29 = (bf16[2,256,256]{2,1,0:T(8,128)(2,1)S(1)}, bf16[2,256,256]{2,1,0:T(8,128)(2,1)S(1)}, u32[]{:S(2)}, u32[]{:S(2)}) collective-permute-start(bf16[2,256,256]{2,1,0:T(8,128)(2,1)S(1)} %copy-done.9), channel_id=1, source_target_pairs={{0,1},{1,2},{2,3},{3,0},{4,5},{5,6},{6,7},{7,4},{8,9},{9,10},{10,1... | collective-permute-start | bytes 786440 | tf_op jit(solution)/shard_map/ppermute | solution.py:153
  255.2 13.7 %collective-permute-start.31 = (bf16[2,256,256]{2,1,0:T(8,128)(2,1)S(1)}, bf16[2,256,256]{2,1,0:T(8,128)(2,1)S(1)}, u32[]{:S(2)}, u32[]{:S(2)}) collective-permute-start(bf16[2,256,256]{2,1,0:T(8,128)(2,1)S(1)} %copy-done.7), channel_id=1, source_target_pairs={{0,2},{1,3},{2,0},{3,1},{4,6},{5,7},{6,4},{7,5},{8,10},{9,11},{10,... | collective-permute-start | bytes 786440 | tf_op jit(solution)/shard_map/ppermute | solution.py:153
  255.2 14.3 %collective-permute-start.32 = (bf16[2,256,256]{2,1,0:T(8,128)(2,1)S(1)}, bf16[2,256,256]{2,1,0:T(8,128)(2,1)S(1)}, u32[]{:S(2)}, u32[]{:S(2)}) collective-permute-start(bf16[2,256,256]{2,1,0:T(8,128)(2,1)S(1)} %copy-done.5), channel_id=1, source_target_pairs={{0,1},{1,2},{2,3},{3,0},{4,5},{5,6},{6,7},{7,4},{8,9},{9,10},{10,1... | collective-permute-start | bytes 786440 | tf_op jit(solution)/shard_map/ppermute | solution.py:153
  255.4 29.1 %collective-permute-start.21 = (bf16[128,3072]{1,0:T(8,128)(2,1)S(1)}, bf16[128,3072]{1,0:T(8,128)(2,1)S(1)}, u32[]{:S(2)}, u32[]{:S(2)}) collective-permute-start(bf16[128,3072]{1,0:T(8,128)(2,1)S(1)} %get-tuple-element.47), channel_id=1, source_target_pairs={{0,1},{4,5},{8,9},{12,13},{16,17},{20,21},{24,25},{28,29}} | collective-permute-start | bytes 2359304 | tf_op jit(solution)/shard_map/ppermute | solution.py:172
  268.8 18.1 %collective-permute-start.24 = (bf16[128,3072]{1,0:T(8,128)(2,1)S(1)}, bf16[128,3072]{1,0:T(8,128)(2,1)S(1)}, u32[]{:S(2)}, u32[]{:S(2)}) collective-permute-start(bf16[128,3072]{1,0:T(8,128)(2,1)S(1)} %get-tuple-element.48), channel_id=1, source_target_pairs={{3,2},{7,6},{11,10},{15,14},{19,18},{23,22},{27,26},{31,30}} | collective-permute-start | bytes 2359304 | tf_op jit(solution)/shard_map/ppermute | solution.py:173
  269.6 39.7 %collective-permute-start.34 = (bf16[2,256,256]{2,1,0:T(8,128)(2,1)S(1)}, bf16[2,256,256]{2,1,0:T(8,128)(2,1)S(1)}, u32[]{:S(2)}, u32[]{:S(2)}) collective-permute-start(bf16[2,256,256]{2,1,0:T(8,128)(2,1)S(1)} %copy-done.3), channel_id=1, source_target_pairs={{0,2},{1,3},{2,0},{3,1},{4,6},{5,7},{6,4},{7,5},{8,10},{9,11},{10,... | collective-permute-start | bytes 786440 | tf_op jit(solution)/shard_map/ppermute | solution.py:153
  269.9 37.1 %collective-permute-start.10 = (bf16[128,3072]{1,0:T(8,128)(2,1)S(1)}, bf16[128,3072]{1,0:T(8,128)(2,1)S(1)}, u32[]{:S(2)}, u32[]{:S(2)}) collective-permute-start(bf16[128,3072]{1,0:T(8,128)(2,1)S(1)} %add_convert_fusion.6), channel_id=1, source_target_pairs={{0,1},{1,2},{4,5},{5,6},{8,9},{9,10},{12,13},{13,14},{16,17},{17,1... | collective-permute-start | bytes 2359304 | tf_op jit(solution)/shard_map/ppermute | solution.py:172
  284.5 52.8 %collective-permute-start.35 = (bf16[2,256,256]{2,1,0:T(8,128)(2,1)S(1)}, bf16[2,256,256]{2,1,0:T(8,128)(2,1)S(1)}, u32[]{:S(2)}, u32[]{:S(2)}) collective-permute-start(bf16[2,256,256]{2,1,0:T(8,128)(2,1)S(1)} %get-tuple-element.36), channel_id=1, source_target_pairs={{0,1},{1,2},{2,3},{3,0},{4,5},{5,6},{6,7},{7,4},{8,9},{9,10},{10,1... | collective-permute-start | bytes 786440 | tf_op jit(solution)/shard_map/ppermute | solution.py:153
  287.3 42.1 %collective-permute-start.22 = (bf16[128,3072]{1,0:T(8,128)(2,1)S(1)}, bf16[128,3072]{1,0:T(8,128)(2,1)S(1)}, u32[]{:S(2)}, u32[]{:S(2)}) collective-permute-start(bf16[128,3072]{1,0:T(8,128)(2,1)S(1)} %get-tuple-element.45), channel_id=1, source_target_pairs={{0,1},{1,2},{4,5},{5,6},{8,9},{9,10},{12,13},{13,14},{16,17},{17,1... | collective-permute-start | bytes 2359304 | tf_op jit(solution)/shard_map/ppermute | solution.py:172
  289.3 40.1 %collective-permute-start.25 = (bf16[128,3072]{1,0:T(8,128)(2,1)S(1)}, bf16[128,3072]{1,0:T(8,128)(2,1)S(1)}, u32[]{:S(2)}, u32[]{:S(2)}) collective-permute-start(bf16[128,3072]{1,0:T(8,128)(2,1)S(1)} %get-tuple-element.46), channel_id=1, source_target_pairs={{2,1},{3,2},{6,5},{7,6},{10,9},{11,10},{14,13},{15,14},{18,17},{19... | collective-permute-start | bytes 2359304 | tf_op jit(solution)/shard_map/ppermute | solution.py:173
  308.6 27.2 %collective-permute-start.13 = (bf16[128,3072]{1,0:T(8,128)(2,1)S(1)}, bf16[128,3072]{1,0:T(8,128)(2,1)S(1)}, u32[]{:S(2)}, u32[]{:S(2)}) collective-permute-start(bf16[128,3072]{1,0:T(8,128)(2,1)S(1)} %get-tuple-element.40), channel_id=1, source_target_pairs={{2,1},{3,2},{6,5},{7,6},{10,9},{11,10},{14,13},{15,14},{18,17},{19... | collective-permute-start | bytes 2359304 | tf_op jit(solution)/shard_map/ppermute | solution.py:173
  309.4 53.2 %collective-permute-start.11 = (bf16[128,3072]{1,0:T(8,128)(2,1)S(1)}, bf16[128,3072]{1,0:T(8,128)(2,1)S(1)}, u32[]{:S(2)}, u32[]{:S(2)}) collective-permute-start(bf16[128,3072]{1,0:T(8,128)(2,1)S(1)} %get-tuple-element.39), channel_id=1, source_target_pairs={{0,1},{1,2},{2,3},{4,5},{5,6},{6,7},{8,9},{9,10},{10,11},{12,13},{... | collective-permute-start | bytes 2359304 | tf_op jit(solution)/shard_map/ppermute | solution.py:172
  330.0 31.3 %collective-permute-start.23 = (bf16[128,3072]{1,0:T(8,128)(2,1)S(1)}, bf16[128,3072]{1,0:T(8,128)(2,1)S(1)}, u32[]{:S(2)}, u32[]{:S(2)}) collective-permute-start(bf16[128,3072]{1,0:T(8,128)(2,1)S(1)} %get-tuple-element.43), channel_id=1, source_target_pairs={{0,1},{1,2},{2,3},{4,5},{5,6},{6,7},{8,9},{9,10},{10,11},{12,13},{... | collective-permute-start | bytes 2359304 | tf_op jit(solution)/shard_map/ppermute | solution.py:172
  334.5 26.8 %collective-permute-start.26 = (bf16[128,3072]{1,0:T(8,128)(2,1)S(1)}, bf16[128,3072]{1,0:T(8,128)(2,1)S(1)}, u32[]{:S(2)}, u32[]{:S(2)}) collective-permute-start(bf16[128,3072]{1,0:T(8,128)(2,1)S(1)} %get-tuple-element.44), channel_id=1, source_target_pairs={{1,0},{2,1},{3,2},{5,4},{6,5},{7,6},{9,8},{10,9},{11,10},{13,12},{... | collective-permute-start | bytes 2359304 | tf_op jit(solution)/shard_map/ppermute | solution.py:173
  335.9 32.9 %collective-permute-start.14 = (bf16[128,3072]{1,0:T(8,128)(2,1)S(1)}, bf16[128,3072]{1,0:T(8,128)(2,1)S(1)}, u32[]{:S(2)}, u32[]{:S(2)}) collective-permute-start(bf16[128,3072]{1,0:T(8,128)(2,1)S(1)} %add_convert_fusion.3), channel_id=1, source_target_pairs={{1,0},{2,1},{3,2},{5,4},{6,5},{7,6},{9,8},{10,9},{11,10},{13,12},{... | collective-permute-start | bytes 2359304 | tf_op jit(solution)/shard_map/ppermute | solution.py:173
  337.3 25.3 %copy-start.14 = (bf16[1,2,256,3072]{3,2,1,0:T(8,128)(2,1)}, bf16[1,2,256,3072]{3,2,1,0:T(8,128)(2,1)S(1)}, u32[]{:S(2)}) copy-start(bf16[1,2,256,3072]{3,2,1,0:T(8,128)(2,1)S(1)} %bitcast_dynamic-update-slice_fusion) | copy-start | bytes 9437188
  (18 other events, 125.8 us)
Sparse Core Ops, SparseCore 0:
  228.5 137.9 all-reduce.2

commit v2 on v1

v2 whole, which is shorter than its diff:
```python
import functools
import math

import jax
import jax.numpy as jnp
from jax import lax
from jax.experimental import pallas as pl
from jax.experimental.pallas import tpu as pltpu
from jax.sharding import PartitionSpec as P

HD = 128
TILE = 128
F32 = jnp.float32
BF16 = jnp.bfloat16
NEG = -1e30


def contract_last(left, right):
    return lax.dot_general(left, right, (((1,), (1,)), ((), ())), preferred_element_type=F32)


def contract_first(left, right):
    return lax.dot_general(left, right, (((0,), (0,)), ((), ())), preferred_element_type=F32)


def tile_table(tile_lists, ref_tiles, me, n):
    matched = jnp.any(tile_lists[..., None] == jnp.arange(ref_tiles, dtype=jnp.int32), axis=-2)
    table = jnp.transpose(matched, (1, 0, 2)).reshape(matched.shape[1], -1).astype(jnp.int32)
    source = lax.rem(me - jnp.arange(n, dtype=jnp.int32) + n, n)
    table = table.reshape(n, -1, table.shape[1])[source].reshape(table.shape)
    return table.reshape(table.shape[0], n, -1)[:, source].reshape(table.shape)


def masked(scores, table_ref, row, first, scale, axis):
    tiles = []
    for t in range(scores.shape[axis] // TILE):
        part = lax.slice_in_dim(scores, t * TILE, (t + 1) * TILE, axis=axis) * scale
        tiles.append(jnp.where(table_ref[row, first + t] != 0, part, NEG))
    return tiles


def forward_kernel(n, scale, table_ref, q_ref, *refs):
    kv_refs, out_ref = refs[:n], refs[n]
    local = kv_refs[0].shape[1] // TILE
    wide = math.gcd(q_ref.shape[0] // TILE, 4)

    def block(i, carry):
        rows = pl.ds(pl.multiple_of(i * wide * TILE, TILE), wide * TILE)
        query = q_ref[rows, :]
        scores = []
        for k in range(n):
            part = contract_last(kv_refs[k][0], query)
            for t in range(local):
                tiles = []
                for j in range(wide):
                    tile = part[t * TILE : (t + 1) * TILE, j * TILE : (j + 1) * TILE] * scale
                    tiles.append(jnp.where(table_ref[i * wide + j, k * local + t] != 0, tile, NEG))
                scores.append(jnp.concatenate(tiles, axis=1))
        peak = jnp.max(functools.reduce(jnp.maximum, scores), axis=0, keepdims=True)
        powers = [jnp.exp(s - peak) for s in scores]
        total = jnp.sum(functools.reduce(jnp.add, powers), axis=0, keepdims=True)
        inverse = 1.0 / total
        probs = [(p * inverse).astype(BF16) for p in powers]
        acc = None
        for k in range(n):
            part = jnp.concatenate(probs[k * local : (k + 1) * local], axis=0)
            part = contract_first(kv_refs[k][1], part)
            acc = part if acc is None else acc + part
        out_ref[rows, :] = acc.T.astype(BF16)
        return carry

    lax.fori_loop(0, q_ref.shape[0] // TILE // wide, block, 0)


def backward_kernel(n, scale, table_ref, source_ref, q_ref, g_ref, *refs):
    kv_refs, (dq_ref, dkv_ref, probs_ref, dscores_ref) = refs[:n], refs[-4:]
    length = kv_refs[0].shape[1]
    local = length // TILE

    wide = math.gcd(q_ref.shape[0] // TILE, 4)

    def block(i, carry):
        rows = pl.ds(pl.multiple_of(i * wide * TILE, TILE), wide * TILE)
        query, grad = q_ref[rows, :], g_ref[rows, :]
        scores, dprobs = [], []
        for k in range(n):
            part = contract_last(kv_refs[k][0], query)
            for t in range(local):
                tiles = []
                for j in range(wide):
                    tile = part[t * TILE : (t + 1) * TILE, j * TILE : (j + 1) * TILE] * scale
                    tiles.append(jnp.where(table_ref[i * wide + j, k * local + t] != 0, tile, NEG))
                scores.append(jnp.concatenate(tiles, axis=1))
        peak = functools.reduce(jnp.maximum, scores)
        peak = jnp.max(peak, axis=0, keepdims=True)
        powers = [jnp.exp(s - peak) for s in scores]
        total = jnp.sum(functools.reduce(jnp.add, powers), axis=0, keepdims=True)
        inverse = 1.0 / total
        weights = [p * inverse for p in powers]
        for k in range(n):
            part = contract_last(kv_refs[k][1], grad)
            dprobs += [part[t * TILE : (t + 1) * TILE] for t in range(local)]
        delta = functools.reduce(jnp.add, [d * w for d, w in zip(dprobs, weights)])
        delta = jnp.sum(delta, axis=0, keepdims=True)
        for j in range(n * local):
            keys = pl.ds(j * TILE, TILE)
            probs_ref[keys, rows] = weights[j].astype(BF16)
            dscores_ref[keys, rows] = (weights[j] * (dprobs[j] - delta) * scale).astype(BF16)
        return carry

    lax.fori_loop(0, q_ref.shape[0] // TILE // wide, block, 0)
    dq = None
    for k in range(n):
        keys = pl.ds(k * length, length)
        dscores = dscores_ref[keys, :]
        dkv_ref[source_ref[k], 0] = jnp.dot(dscores, q_ref[...], preferred_element_type=F32).astype(BF16)
        dkv_ref[source_ref[k], 1] = jnp.dot(probs_ref[keys, :], g_ref[...], preferred_element_type=F32).astype(BF16)
        part = contract_first(kv_refs[k][0], dscores)
        dq = part if dq is None else dq + part
    dq_ref[...] = dq.T.astype(BF16)


def attend(table, query, pieces, scale, first, heads):
    n = len(pieces)
    tokens = query.shape[0]
    width = heads * HD
    length = pieces[0].shape[1]
    rows = pl.BlockSpec((tokens, HD), lambda h, t: (0, first + h))
    piece = pl.BlockSpec((2, length, HD), lambda h, t: (0, 0, first + h))
    work = tokens * n * length * width
    return pl.pallas_call(
        functools.partial(forward_kernel, n, scale),
        out_shape=jax.ShapeDtypeStruct((tokens, width), BF16),
        grid_spec=pltpu.PrefetchScalarGridSpec(
            num_scalar_prefetch=1,
            grid=(heads,),
            in_specs=[rows] + [piece] * n,
            out_specs=pl.BlockSpec((tokens, HD), lambda h, t: (0, h)),
        ),
        cost_estimate=pl.CostEstimate(
            flops=4 * work, transcendentals=work // HD, bytes_accessed=4 * width * (tokens + n * length)
        ),
        compiler_params=pltpu.CompilerParams(vmem_limit_bytes=48 << 20),
    )(table, query, *pieces)


def attend_back(table, source, query, grad, pieces, scale, first, heads, earlier=()):
    n = len(pieces)
    tokens, width = query.shape
    length = pieces[0].shape[1]
    rows = pl.BlockSpec((tokens, HD), lambda h, t, s: (0, first + h))
    piece = pl.BlockSpec((2, length, HD), lambda h, t, s: (0, 0, first + h))
    work = tokens * n * length * heads * HD
    return pl.pallas_call(
        functools.partial(backward_kernel, n, scale),
        out_shape=[
            jax.ShapeDtypeStruct((tokens, width), BF16),
            jax.ShapeDtypeStruct((n, 2, length, width), BF16),
        ],
        grid_spec=pltpu.PrefetchScalarGridSpec(
            num_scalar_prefetch=2,
            grid=(heads,),
            in_specs=[rows, rows] + [piece] * n + [pl.BlockSpec(memory_space=pl.ANY)] * len(earlier),
            out_specs=[rows, pl.BlockSpec((n, 2, length, HD), lambda h, t, s: (0, 0, 0, first + h))],
            scratch_shapes=[pltpu.VMEM((n * length, tokens), BF16)] * 2,
        ),
        input_output_aliases={4 + n + i: i for i in range(len(earlier))},
        cost_estimate=pl.CostEstimate(
            flops=10 * work,
            transcendentals=work // HD,
            bytes_accessed=2 * heads * HD * (3 * tokens + 4 * n * length),
        ),
        compiler_params=pltpu.CompilerParams(vmem_limit_bytes=48 << 20),
    )(table, source, query, grad, *pieces, *earlier)


def after(array, *others):
    return lax.optimization_barrier((array, *others))[0]


def shift(array, n, by):
    return lax.ppermute(array, "seq", [(i, (i + by) % n) for i in range(n)])


def both_ways(right, left, ups, downs, me):
    up, down = [(i, i + 1) for i in ups], [(i, i - 1) for i in downs]
    apart = not {i for i, _ in up} & {i for i, _ in down} and not {j for _, j in up} & {j for _, j in down}
    if not apart:
        return lax.ppermute(right, "seq", up), lax.ppermute(left, "seq", down)
    rightward = (me >= ups[0]) & (me <= ups[-1])
    came = lax.ppermute(jnp.where(rightward, right, left), "seq", up + down)
    none = jnp.zeros_like(came)
    from_left = (me > ups[0]) & (me <= ups[-1] + 1)
    from_right = (me >= downs[0] - 1) & (me < downs[-1])
    return jnp.where(from_left, came, none), jnp.where(from_right, came, none)


def gather_step(block, state, n, me):
    s = len(state[0]) + 1
    right, left = (side[-1] if side else block for side in state)
    right, left = both_ways(right, left, range(s - 1, n - 1), range(1, n - s + 1), me)
    return (state[0] + [right], state[1] + [left])


def join(block, state, me):
    right, left = state
    others = [jnp.where(me > k, right[k], left[len(left) - 1 - k]) for k in range(len(right))]
    return jnp.concatenate([block] + others, axis=0)


def scatter_step(parts, state, n, me):
    steps, right, left = state
    s = steps + 1
    right = parts[s] if right is None else parts[s] + right.astype(F32)
    left = parts[n - s] if left is None else parts[n - s] + left.astype(F32)
    return s, *both_ways(right.astype(BF16), left.astype(BF16), range(s), range(n - s, n), me)


def split(partial, n):
    size = partial.shape[0] // n
    return [partial[k * size : (k + 1) * size].astype(F32) for k in range(n)]


class ClipSum:
    def __init__(self, array, paths):
        self.size = lax.axis_size("dp")
        self.index = lax.axis_index("dp")
        rows = array.shape[0] // len(paths)
        self.blocks = [array[p * rows : (p + 1) * rows] for p in range(len(paths))]
        self.paths = paths
        self.done = 0

    def exchange(self, block, mask):
        return lax.ppermute(block, "dp", [(i, i ^ mask) for i in range(self.size)])

    def step(self, *others):
        count = len(self.paths[0])
        if self.done == 2 * count:
            return ()
        for p, path in enumerate(self.paths):
            block = self.blocks[p]
            if self.done < count:
                mask = path[self.done]
                high = lax.shift_right_logical(self.index, mask.bit_length() - 1) & 1
                half = block.shape[0] // 2
                give = lax.dynamic_slice_in_dim(block, (1 - high) * half, half).astype(BF16)
                keep = lax.dynamic_slice_in_dim(block, high * half, half).astype(F32)
                self.blocks[p] = keep + self.exchange(after(give, *others), mask).astype(F32)
            else:
                mask = path[2 * count - 1 - self.done]
                high = lax.shift_right_logical(self.index, mask.bit_length() - 1) & 1
                block = after(block.astype(BF16), *others)
                other = self.exchange(block, mask)
                pair = jnp.concatenate([block, other]), jnp.concatenate([other, block])
                self.blocks[p] = jnp.where(high == 0, *pair)
        self.done += 1
        return tuple(self.blocks)

    def result(self):
        while self.done < 2 * len(self.paths[0]):
            self.step()
        return jnp.concatenate(self.blocks).astype(F32)


def body(video, cotangent, w_query, w_out, ref_kv, tile_lists):
    n = lax.axis_size("seq")
    me = lax.axis_index("seq")
    masks = [1 << b for b in range(lax.axis_size("dp").bit_length() - 1)]
    width = w_query.shape[1]
    heads = width // HD
    chunks = 2 if heads % 2 == 0 else 1
    length = ref_kv.shape[2]
    ref_tiles = length * n // TILE // tile_lists.shape[1]
    scale = 1.0 / math.sqrt(HD)
    table = tile_table(tile_lists[0], ref_tiles, me, n)

    pieces = []
    for k in range(n):
        columns = lax.rem(me + k, n) * width
        piece = lax.dynamic_slice_in_dim(ref_kv[0], columns, width, axis=2)
        pieces.append(shift(piece, n, k) if k else piece)
    order = sorted(range(1, n), key=lambda k: (min(k, n - k), -k))
    rows = ([], [])
    for s in range(1, n):
        block = video[0]
        if s > 1:
            rows = tuple(side[:-1] + [after(side[-1], pieces[order[s - 2]])] for side in rows)
        rows = gather_step(block, rows, n, me)
    gathered = join(video[0], rows, me)
    query = jnp.dot(gathered, w_query, preferred_element_type=F32).astype(BF16)
    per = heads // chunks
    grad = after(cotangent[0], rows[0][-1], rows[1][-1], *pieces[1:])
    cots = gather_step(grad, ([], []), n, me)
    attention = []
    for c in range(chunks):
        source = after(query, cots[0][0], cots[1][0]) if c else query
        attention.append(attend(table, source, pieces, scale, c * per, per))
    attention = jnp.concatenate(attention, axis=1)
    partial = split(jnp.dot(attention, w_out, preferred_element_type=F32), n)
    for s in range(2, n):
        if s == n - 1:
            partial = [after(p, cots[0][-1], cots[1][-1]) for p in partial]
        cots = gather_step(grad, cots, n, me)
    grad_rows = join(grad, cots, me)
    sums, marks = (0, None, None), []
    for _ in range(1, n):
        sums = scatter_step(partial, sums, n, me)
        marks.append(sums[1:])
    output = (partial[0] + sums[1].astype(F32) + sums[2].astype(F32)).astype(BF16)
    grad_rows = after(grad_rows, *marks[0])

    grad_wo = contract_first(attention, grad_rows).astype(BF16)
    grad_attention = after(contract_last(grad_rows, w_out).astype(BF16), grad_wo, *marks[-2])
    sum_wo = ClipSum(grad_wo, [masks, masks[:1] + masks[:0:-1]])
    source = lax.rem(me - jnp.arange(n, dtype=jnp.int32) + n, n)
    back = attend_back(table, source, query, grad_attention, pieces, scale, 0, per)
    grad_attention = after(grad_attention, *sum_wo.step())
    for c in range(1, chunks):
        back = attend_back(table, source, query, grad_attention, pieces, scale, c * per, per, back)
    grad_query, grad_kv = back
    grad_kv = lax.all_to_all(grad_kv, "seq", split_axis=0, concat_axis=0, tiled=True)
    grad_ref = jnp.concatenate([grad_kv[k] for k in range(n)], axis=2)
    grad_wq = contract_first(gathered, grad_query).astype(BF16)
    sum_wq = ClipSum(grad_wq, [masks, masks[:1] + masks[:0:-1]])
    grad_query = after(grad_query, grad_wq)
    sum_wq.step()
    sum_wq.step(output)
    parts = split(contract_last(grad_query, w_query).astype(BF16), n)
    sums = (0, None, None)
    for s in range(1, n):
        if s == 2:
            parts = [after(p, grad_kv) for p in parts]
        sums = scatter_step(parts, sums, n, me)
        if s == 1:
            sum_wq.step(*sums[1:])
    grad_video = (parts[0] + sums[1].astype(F32) + sums[2].astype(F32)).astype(BF16)
    return (output[None], grad_video[None], sum_wq.result(), sum_wo.result(), grad_ref[None])


def solution(mesh):
    in_specs = (
        P("dp", "seq", None),
        P("dp", "seq", None),
        P(None, "seq"),
        P("seq", None),
        P("dp", None, "seq", None),
        P("dp", None, None, None),
    )
    out_specs = (
        P("dp", "seq", None),
        P("dp", "seq", None),
        P(None, "seq"),
        P("seq", None),
        P("dp", None, "seq", None),
    )
    return jax.shard_map(body, mesh=mesh, in_specs=in_specs, out_specs=out_specs, check_vma=False)
```

time: 390 us -> 386 us (0.990)
  other arithmetic: 25.5 us -> 42.3 us
  between operations: 14.9 us -> 1.48 us
  Pallas kernels: 35.9 us -> 27.4 us
  local copies, waits for them, and re-layouts: 9.6 us -> 16.7 us
  waiting for transfers between devices: 200 us -> 194 us
    ppermute x12 -> x3, waiting for transfers between devices: 89.8 us -> 46.3 us  [shift(): return lax.ppermute(array, 'seq', [(i, (i + by) % n) for i in range(n)])]
    ppermute x24 -> x44, waiting for transfers between devices: 110 us -> 147 us  [the longest x16 72.6 us: both_ways(): return (lax.ppermute(right, 'seq', up), lax.ppermute(left, 'seq', down))]
    ppermute x12 -> x3, starting transfers between devices: 19.3 us -> 4.49 us  [shift(): return lax.ppermute(array, 'seq', [(i, (i + by) % n) for i in range(n)])]
    ppermute x24 -> x44, starting transfers between devices: 58.6 us -> 68.6 us  [the longest x16 37.7 us: both_ways(): return (lax.ppermute(right, 'seq', up), lax.ppermute(left, 'seq', down))]
    select_n x6 -> x17, other arithmetic: 6.96 us -> 13.3 us  [the longest x4 6.79 us: join(): jnp.where(me > k, right[k], left[len(left) - 1 - k])]
    all_to_all x0 -> x1, starting transfers between devices: none -> 5.17 us  [body(): lax.all_to_all(grad_kv, 'seq', split_axis=0, concat_axis=0, tiled=True)]
    pallas_call x3 -> x2, Pallas kernels: 22.7 us -> 18.2 us  [attend_back(): pl.pallas_call(functools.partial(backward_kernel, n, scale), out_shape=[j...]
    add x0 -> x8, other arithmetic: none -> 4.31 us  [step(): keep + self.exchange(after(give, *others), mask).astype(F32)]
  transfers between devices with their start and end apart: 37 -> 48, of which waited for: 15 -> 23; matrix products, arithmetic and copies ran while one was open for 12% -> 18% of each run, Pallas kernels for 9% -> 7%
where the time goes in v2:
time: 386 us; the launch traced here: 385 us
  waiting for transfers between devices  194 us (50%)
  starting transfers between devices  78.3 us (20%)
  other arithmetic  42.3 us (11%)
  Pallas kernels  27.4 us (7%)
  matrix products  25 us (6%)
  local copies, waits for them, and re-layouts  16.7 us (4%)
    ppermute x16, waiting for transfers between devices, both_ways(): return (lax.ppermute(right, 'seq', up), lax.ppermute(left, 'seq', down))  72.6 us
    ppermute x3, waiting for transfers between devices, shift(): return lax.ppermute(array, 'seq', [(i, (i + by) % n) for i in range(n)])  46.3 us
    ppermute x24, waiting for transfers between devices, exchange(): return lax.ppermute(block, 'dp', [(i, i ^ mask) for i in range(self.size)])  40.4 us
    ppermute x16, starting transfers between devices, both_ways(): return (lax.ppermute(right, 'seq', up), lax.ppermute(left, 'seq', down))  37.7 us
    ppermute x4, waiting for transfers between devices, both_ways(): came = lax.ppermute(jnp.where(rightward, right, left), 'seq', up + down)  34.5 us
    pallas_call x2, Pallas kernels, attend_back(): pl.pallas_call(functools.partial(backward_kernel, n, scale), out_shape=[j...  18.2 us
    ppermute x24, starting transfers between devices, exchange(): return lax.ppermute(block, 'dp', [(i, i ^ mask) for i in range(self.size)])  16.7 us
    ppermute x4, starting transfers between devices, both_ways(): came = lax.ppermute(jnp.where(rightward, right, left), 'seq', up + down)  14.2 us
  transfers between devices with their start and end apart: 48, of which 23 were waited for; matrix products, arithmetic and copies ran while one was open for 18% of the time, Pallas kernels for 7%

profile of v2, /device:TPU:0, one launch (start us, length us, event | category | flops | bytes accessed | tf_op | source)
XLA Modules:
  0.0 384.9 jit_solution(5085298853002504709)
XLA Ops:
  0.6 5.0 %collective-permute-start = (bf16[128,3072]{1,0:T(8,128)(2,1)}, bf16[128,3072]{1,0:T(8,128)(2,1)S(1)}, u32[]{:S(2)}, u32[]{:S(2)}) collective-permute-start(bf16[128,3072]{1,0:T(8,128)(2,1)} %bitcast.46), channel_id=1, source_target_pairs={{0,1},{1,2},{2,3},{4,5},{5,6},{6,7},{8,9},{9,10},{10,11},{12,13},{... | collective-permute-start | bytes 2359304 | tf_op jit(solution)/shard_map/ppermute | solution.py:189
  5.7 3.3 dynamic-slice_bitcast_fusion.1
  11.6 2.7 collective-permute-start.3
  14.3 9.5 %collective-permute-done = bf16[128,3072]{1,0:T(8,128)(2,1)S(1)} collective-permute-done((bf16[128,3072]{1,0:T(8,128)(2,1)}, bf16[128,3072]{1,0:T(8,128)(2,1)S(1)}, u32[]{:S(2)}, u32[]{:S(2)}) %collective-permute-start) | collective-permute-done | bytes 786464 | tf_op jit(solution)/shard_map/ppermute | solution.py:189
  23.8 16.8 %collective-permute-done.1.refs_3_ = bf16[2,256,768]{2,1,0:T(8,128)(2,1)S(1)} collective-permute-done((bf16[2,256,768]{2,1,0:T(8,128)(2,1)S(1)}, bf16[2,256,768]{2,1,0:T(8,128)(2,1)S(1)}, u32[]{:S(2)}, u32[]{:S(2)}) %collective-permute-start.1) | collective-permute-done | bytes 786464 | tf_op jit(solution)/shard_map/ppermute | solution.py:182
  42.2 2.7 collective-permute-done.4
  46.2 17.6 %collective-permute-done.3.refs_1_ = bf16[2,256,768]{2,1,0:T(8,128)(2,1)S(1)} collective-permute-done((bf16[2,256,768]{2,1,0:T(8,128)(2,1)}, bf16[2,256,768]{2,1,0:T(8,128)(2,1)S(1)}, u32[]{:S(2)}, u32[]{:S(2)}) %collective-permute-start.3) | collective-permute-done | bytes 786464 | tf_op jit(solution)/shard_map/ppermute | solution.py:182
  63.8 16.7 %collective-permute-done.5 = bf16[128,3072]{1,0:T(8,128)(2,1)} collective-permute-done((bf16[128,3072]{1,0:T(8,128)(2,1)}, bf16[128,3072]{1,0:T(8,128)(2,1)}, u32[]{:S(2)}, u32[]{:S(2)}) %collective-permute-start.5) | collective-permute-done | bytes 786464 | tf_op jit(solution)/shard_map/ppermute | solution.py:189
  80.6 2.6 broadcast_select_fusion.8
  85.1 22.5 %collective-permute-done.6 = bf16[128,3072]{1,0:T(8,128)(2,1)} collective-permute-done((bf16[128,3072]{1,0:T(8,128)(2,1)}, bf16[128,3072]{1,0:T(8,128)(2,1)}, u32[]{:S(2)}, u32[]{:S(2)}) %collective-permute-start.6) | collective-permute-done | bytes 786464 | tf_op jit(solution)/shard_map/ppermute | solution.py:191
  107.6 2.7 broadcast_select_fusion.12
  110.2 11.9 %collective-permute-done.7.refs_2_ = bf16[2,256,768]{2,1,0:T(8,128)(2,1)S(1)} collective-permute-done((bf16[2,256,768]{2,1,0:T(8,128)(2,1)}, bf16[2,256,768]{2,1,0:T(8,128)(2,1)S(1)}, u32[]{:S(2)}, u32[]{:S(2)}) %collective-permute-start.7) | collective-permute-done | bytes 786464 | tf_op jit(solution)/shard_map/ppermute | solution.py:182
  123.3 5.5 %collective-permute-start.8 = (bf16[128,3072]{1,0:T(8,128)(2,1)}, bf16[128,3072]{1,0:T(8,128)(2,1)}, u32[]{:S(2)}, u32[]{:S(2)}) collective-permute-start(bf16[128,3072]{1,0:T(8,128)(2,1)} %bitcast.12), channel_id=1, source_target_pairs={{0,1},{1,2},{2,3},{4,5},{5,6},{6,7},{8,9},{9,10},{10,11},{12,13},{... | collective-permute-start | bytes 2359304 | tf_op jit(solution)/shard_map/ppermute | solution.py:189
  130.3 12.5 %collective-permute-done.9 = bf16[128,3072]{1,0:T(8,128)(2,1)} collective-permute-done((bf16[128,3072]{1,0:T(8,128)(2,1)}, bf16[128,3072]{1,0:T(8,128)(2,1)}, u32[]{:S(2)}, u32[]{:S(2)}) %collective-permute-start.9) | collective-permute-done | bytes 786464 | tf_op jit(solution)/shard_map/ppermute | solution.py:189
  144.8 5.9 %convolution_convert_fusion.4.q_ref = bf16[512,768]{1,0:T(8,128)(2,1)S(1)} fusion(bf16[3072,768]{1,0:T(8,128)(2,1)} %param.8, bf16[128,3072]{1,0:T(8,128)(2,1)} %get-tuple-element.100, bf16[128,3072]{1,0:T(8,128)(2,1)} %get-tuple-element.96, bf16[128,3072]{1,0:T(8,128)(2,1)} %get-tuple-element.65, bf16[128,3072]{1,0:T(8,128)(2,1)} %bitcast.47), kind=kOutput, calls=%fused_computation.29 | convolution fusion | flops 2428895232 | bytes 8650752 | tf_op jit(solution)/shard_map/dot_general | solution.py:290
  150.7 4.6 %shard_map.101 = bf16[512,384]{1,0:T(8,128)(2,1)S(1)} custom-call(s32[4,8]{1,0:T(4,128)S(1)} %copy.22.table_ref, bf16[512,768]{1,0:T(8,128)(2,1)S(1)} %convolution_convert_fusion.4.q_ref, bf16[2,256,768]{2,1,0:T(8,128)(2,1)S(1)} %get-tuple-element.86.refs_0_, bf16[2,256,768]{2,1,0:T(8,128)(2,1)S(1)} %collective-permute-done.3.refs_1_, ...), custom_call_target="tpu_custom_call" | custom-call | flops 805306368 | bytes 2359296 | tf_op jit(solution)/shard_map/pallas_call | solution.py:131
  155.3 4.6 %shard_map.102 = bf16[512,384]{1,0:T(8,128)(2,1)S(1)} custom-call(s32[4,8]{1,0:T(4,128)S(1)} %copy.22.table_ref, bf16[512,768]{1,0:T(8,128)(2,1)S(1)} %convolution_convert_fusion.4.q_ref, bf16[2,256,768]{2,1,0:T(8,128)(2,1)S(1)} %get-tuple-element.86.refs_0_, bf16[2,256,768]{2,1,0:T(8,128)(2,1)S(1)} %collective-permute-done.3.refs_1_, ...), custom_call_target="tpu_custom_call" | custom-call | flops 805306368 | bytes 2359296 | tf_op jit(solution)/shard_map/pallas_call | solution.py:131
  160.0 4.5 %fusion.1 = f32[512,3072]{1,0:T(8,128)S(1)} fusion(bf16[768,3072]{1,0:T(8,128)(2,1)} %param.9, bf16[512,384]{1,0:T(8,128)(2,1)S(1)} %shard_map.102, bf16[512,384]{1,0:T(8,128)(2,1)S(1)} %shard_map.101), kind=kOutput, calls=%fused_computation.84 | convolution fusion | flops 2417491968 | bytes 11796480 | tf_op jit(solution)/shard_map/dot_general | solution.py:299
  167.7 6.1 %collective-permute-start.12 = (bf16[128,3072]{1,0:T(8,128)(2,1)S(1)}, bf16[128,3072]{1,0:T(8,128)(2,1)S(1)}, u32[]{:S(2)}, u32[]{:S(2)}) collective-permute-start(bf16[128,3072]{1,0:T(8,128)(2,1)S(1)} %convert_select_fusion), channel_id=1, source_target_pairs={{0,1},{3,2},{4,5},{7,6},{8,9},{11,10},{12,13},{15,14},{16,17},{19,... | collective-permute-start | bytes 2359304 | tf_op jit(solution)/shard_map/ppermute | solution.py:191
  173.8 11.8 %collective-permute-done.17 = bf16[128,3072]{1,0:T(8,128)(2,1)S(1)} collective-permute-done((bf16[128,3072]{1,0:T(8,128)(2,1)S(1)}, bf16[128,3072]{1,0:T(8,128)(2,1)S(1)}, u32[]{:S(2)}, u32[]{:S(2)}) %collective-permute-start.17) | collective-permute-done | bytes 786464 | tf_op jit(solution)/shard_map/ppermute | solution.py:191
  189.1 2.7 convolution_convert_fusion.3.g_ref
  191.7 2.9 convolution_convert_fusion.1
  194.6 4.4 %collective-permute-start.13 = (bf16[128,3072]{1,0:T(8,128)(2,1)S(1)}, bf16[128,3072]{1,0:T(8,128)(2,1)S(1)}, u32[]{:S(2)}, u32[]{:S(2)}) collective-permute-start(bf16[128,3072]{1,0:T(8,128)(2,1)S(1)} %get-tuple-element.61), channel_id=1, source_target_pairs={{0,1},{1,2},{4,5},{5,6},{8,9},{9,10},{12,13},{13,14},{16,17},{17,1... | collective-permute-start | bytes 2359304 | tf_op jit(solution)/shard_map/ppermute | solution.py:189
  201.8 11.3 %collective-permute-done.13 = bf16[128,3072]{1,0:T(8,128)(2,1)S(1)} collective-permute-done((bf16[128,3072]{1,0:T(8,128)(2,1)S(1)}, bf16[128,3072]{1,0:T(8,128)(2,1)S(1)}, u32[]{:S(2)}, u32[]{:S(2)}) %collective-permute-start.13) | collective-permute-done | bytes 786464 | tf_op jit(solution)/shard_map/ppermute | solution.py:189
  214.3 5.3 %collective-permute-start.14 = (bf16[128,3072]{1,0:T(8,128)(2,1)}, bf16[128,3072]{1,0:T(8,128)(2,1)}, u32[]{:S(2)}, u32[]{:S(2)}) collective-permute-start(bf16[128,3072]{1,0:T(8,128)(2,1)} %add_convert_fusion.8), channel_id=1, source_target_pairs={{0,1},{1,2},{2,3},{4,5},{5,6},{6,7},{8,9},{9,10},{10,11},{12,13},{... | collective-permute-start | bytes 2359304 | tf_op jit(solution)/shard_map/ppermute | solution.py:189
  221.9 9.1 %shard_map.103 = (bf16[512,768]{1,0:T(8,128)(2,1)S(1)}, bf16[4,2,256,768]{3,2,1,0:T(8,128)(2,1)}) custom-call(s32[4,8]{1,0:T(4,128)S(1)} %copy.22.table_ref, s32[4]{0:T(128)S(1)} %compare_select_fusion.1.source_ref, bf16[512,768]{1,0:T(8,128)(2,1)S(1)} %convolution_convert_fusion.4.q_ref, bf16[512,768]{1,0:T(8,128)(2,1)S(1)} %convolution_convert_fusion.3.g_ref, ...), custom_call_target="tpu_custom_call" | custom-call | flops 2013265920 | bytes 4325376 | tf_op jit(solution)/shard_map/pallas_call | solution.py:154
  235.6 9.1 %shard_map.104 = (bf16[512,768]{1,0:T(8,128)(2,1)S(1)}, bf16[4,2,256,768]{3,2,1,0:T(8,128)(2,1)}) custom-call(s32[4,8]{1,0:T(4,128)S(1)} %copy.22.table_ref, s32[4]{0:T(128)S(1)} %compare_select_fusion.1.source_ref, bf16[512,768]{1,0:T(8,128)(2,1)S(1)} %convolution_convert_fusion.4.q_ref, ...), custom_call_target="tpu_custom_call", output_to_operand_aliasing={{0}: (8, {}), {1}: (9, {})} | custom-call | flops 2013265920 | bytes 4325376 | tf_op jit(solution)/shard_map/pallas_call | solution.py:154
  245.6 5.2 %all-to-all-start = ((bf16[4,2,256,768]{3,2,1,0:T(8,128)(2,1)}), bf16[4,2,256,768]{3,2,1,0:T(8,128)(2,1)}, u32[]{:S(2)}, u32[]{:S(2)}) async-start(bf16[4,2,256,768]{3,2,1,0:T(8,128)(2,1)} %get-tuple-element.48), calls=%async_computation | async-start | bytes 6291456 | tf_op jit(solution)/shard_map/all_to_all | solution.py:321
  253.7 3.8 convolution_convert_fusion
  257.5 5.2 %convolution_convert_fusion.2 = bf16[512,3072]{1,0:T(8,128)(2,1)S(1)} fusion(bf16[512,768]{1,0:T(8,128)(2,1)S(1)} %copy-done.1, bf16[3072,768]{1,0:T(8,128)(2,1)} %param.8), kind=kOutput, calls=%fused_computation.6 | convolution fusion | flops 2417491968 | bytes 8650752 | tf_op jit(solution)/shard_map/dot_general | solution.py:19
  262.7 3.1 slice_convert_fusion.3
  265.8 5.4 %collective-permute-start.20 = (bf16[128,3072]{1,0:T(8,128)(2,1)}, bf16[128,3072]{1,0:T(8,128)(2,1)}, u32[]{:S(2)}, u32[]{:S(2)}) collective-permute-start(bf16[128,3072]{1,0:T(8,128)(2,1)} %get-tuple-element.83), channel_id=1, source_target_pairs={{0,1},{3,2},{4,5},{7,6},{8,9},{11,10},{12,13},{15,14},{16,17},{19,... | collective-permute-start | bytes 2359304 | tf_op jit(solution)/shard_map/ppermute | solution.py:191
  272.9 2.6 add_convert_fusion.5
  278.3 7.1 %collective-permute-done.38 = bf16[48,3072]{1,0:T(8,128)(2,1)S(1)} collective-permute-done((bf16[48,3072]{1,0:T(8,128)(2,1)S(1)}, bf16[48,3072]{1,0:T(8,128)(2,1)S(1)}, u32[]{:S(2)}, u32[]{:S(2)}) %collective-permute-start.38) | collective-permute-done | bytes 294944 | tf_op jit(solution)/shard_map/ppermute | solution.py:234
  286.7 6.3 %collective-permute-done.39 = bf16[48,3072]{1,0:T(8,128)(2,1)S(1)} collective-permute-done((bf16[48,3072]{1,0:T(8,128)(2,1)S(1)}, bf16[48,3072]{1,0:T(8,128)(2,1)S(1)}, u32[]{:S(2)}, u32[]{:S(2)}) %collective-permute-start.39) | collective-permute-done | bytes 294944 | tf_op jit(solution)/shard_map/ppermute | solution.py:234
  296.6 9.5 %collective-permute-done.40 = bf16[96,3072]{1,0:T(8,128)(2,1)S(1)} collective-permute-done((bf16[96,3072]{1,0:T(8,128)(2,1)S(1)}, bf16[96,3072]{1,0:T(8,128)(2,1)S(1)}, u32[]{:S(2)}, u32[]{:S(2)}) %collective-permute-start.40) | collective-permute-done | bytes 589856 | tf_op jit(solution)/shard_map/ppermute | solution.py:234
  307.1 3.1 collective-permute-done.45
  310.5 8.6 %collective-permute-done.32 = bf16[384,768]{1,0:T(8,128)(2,1)S(1)} collective-permute-done((bf16[384,768]{1,0:T(8,128)(2,1)S(1)}, bf16[384,768]{1,0:T(8,128)(2,1)S(1)}, u32[]{:S(2)}, u32[]{:S(2)}) %collective-permute-start.32) | collective-permute-done | bytes 589856 | tf_op jit(solution)/shard_map/ppermute | solution.py:234
  324.4 2.0 add_convert_fusion.4
  328.5 2.0 maximum_select_fusion.3
  331.9 3.3 collective-permute-done.33
  337.4 5.0 %maximum_convert_fusion.1 = f32[768,3072]{1,0:T(8,128)} fusion(bf16[384,3072]{1,0:T(8,128)(2,1)S(1)} %maximum_select_fusion.3, bf16[384,3072]{1,0:T(8,128)(2,1)S(1)} %maximum_select_fusion.2), kind=kLoop, calls=%fused_computation.5 | loop fusion | flops 9437184 | bytes 14155776 | tf_op jit(solution)/shard_map/convert_element_type | solution.py:262
  345.9 2.3 collective-permute-done.21
  348.4 4.7 %collective-permute-start.22 = (bf16[128,3072]{1,0:T(8,128)(2,1)S(1)}, bf16[128,3072]{1,0:T(8,128)(2,1)S(1)}, u32[]{:S(2)}, u32[]{:S(2)}) collective-permute-start(bf16[128,3072]{1,0:T(8,128)(2,1)S(1)} %add_convert_fusion.3), channel_id=1, source_target_pairs={{0,1},{1,2},{2,3},{4,5},{5,6},{6,7},{8,9},{9,10},{10,11},{12,13},{... | collective-permute-start | bytes 2359304 | tf_op jit(solution)/shard_map/ppermute | solution.py:189
  354.6 2.1 slice_bitcast_fusion.3
  360.4 7.8 %collective-permute-done.22 = bf16[128,3072]{1,0:T(8,128)(2,1)S(1)} collective-permute-done((bf16[128,3072]{1,0:T(8,128)(2,1)S(1)}, bf16[128,3072]{1,0:T(8,128)(2,1)S(1)}, u32[]{:S(2)}, u32[]{:S(2)}) %collective-permute-start.22) | collective-permute-done | bytes 786464 | tf_op jit(solution)/shard_map/ppermute | solution.py:189
  368.2 9.6 %collective-permute-done.24 = bf16[128,3072]{1,0:T(8,128)(2,1)S(1)} collective-permute-done((bf16[128,3072]{1,0:T(8,128)(2,1)S(1)}, bf16[128,3072]{1,0:T(8,128)(2,1)S(1)}, u32[]{:S(2)}, u32[]{:S(2)}) %collective-permute-start.24) | collective-permute-done | bytes 786464 | tf_op jit(solution)/shard_map/ppermute | solution.py:189
  380.4 4.5 %maximum_convert_fusion = f32[3072,768]{1,0:T(8,128)} fusion(bf16[1536,768]{1,0:T(8,128)(2,1)S(1)} %maximum_select_fusion.1, bf16[1536,768]{1,0:T(8,128)(2,1)S(1)} %maximum_select_fusion), kind=kLoop, calls=%fused_computation.4 | loop fusion | flops 9437184 | bytes 14155776 | tf_op jit(solution)/shard_map/convert_element_type | solution.py:262
  (176 shorter events, 66.2 us)
Async XLA Ops:
  0.6 23.2 %collective-permute-start = (bf16[128,3072]{1,0:T(8,128)(2,1)}, bf16[128,3072]{1,0:T(8,128)(2,1)S(1)}, u32[]{:S(2)}, u32[]{:S(2)}) collective-permute-start(bf16[128,3072]{1,0:T(8,128)(2,1)} %bitcast.46), channel_id=1, source_target_pairs={{0,1},{1,2},{2,3},{4,5},{5,6},{6,7},{8,9},{9,10},{10,11},{12,13},{... | collective-permute-start | bytes 2359304 | tf_op jit(solution)/shard_map/ppermute | solution.py:189
  8.9 31.7 %collective-permute-start.1 = (bf16[2,256,768]{2,1,0:T(8,128)(2,1)S(1)}, bf16[2,256,768]{2,1,0:T(8,128)(2,1)S(1)}, u32[]{:S(2)}, u32[]{:S(2)}) collective-permute-start(bf16[2,256,768]{2,1,0:T(8,128)(2,1)S(1)} %get-tuple-element.88), channel_id=1, source_target_pairs={{0,3},{1,0},{2,1},{3,2},{4,7},{5,4},{6,5},{7,6},{8,11},{9,8},{10,9... | collective-permute-start | bytes 2359304 | tf_op jit(solution)/shard_map/ppermute | solution.py:182
  10.3 34.6 %collective-permute-start.4 = (bf16[128,3072]{1,0:T(8,128)(2,1)S(1)}, bf16[128,3072]{1,0:T(8,128)(2,1)}, u32[]{:S(2)}, u32[]{:S(2)}) collective-permute-start(bf16[128,3072]{1,0:T(8,128)(2,1)S(1)} %bitcast.49), channel_id=1, source_target_pairs={{1,0},{2,1},{3,2},{5,4},{6,5},{7,6},{9,8},{10,9},{11,10},{13,12},{... | collective-permute-start | bytes 2359304 | tf_op jit(solution)/shard_map/ppermute | solution.py:189
  11.6 52.2 %collective-permute-start.3 = (bf16[2,256,768]{2,1,0:T(8,128)(2,1)}, bf16[2,256,768]{2,1,0:T(8,128)(2,1)S(1)}, u32[]{:S(2)}, u32[]{:S(2)}) collective-permute-start(bf16[2,256,768]{2,1,0:T(8,128)(2,1)} %get-tuple-element.87), channel_id=1, source_target_pairs={{0,1},{1,2},{2,3},{3,0},{4,5},{5,6},{6,7},{7,4},{8,9},{9,10},{10,1... | collective-permute-start | bytes 2359304 | tf_op jit(solution)/shard_map/ppermute | solution.py:182
  40.6 23.2 %collective-permute-start.2 = (bf16[128,3072]{1,0:T(8,128)(2,1)S(1)}, bf16[128,3072]{1,0:T(8,128)(2,1)}, u32[]{:S(2)}, u32[]{:S(2)}) collective-permute-start(bf16[128,3072]{1,0:T(8,128)(2,1)S(1)} %collective-permute-done), channel_id=1, source_target_pairs={{1,2},{2,3},{5,6},{6,7},{9,10},{10,11},{13,14},{14,15},{17,18},{18... | collective-permute-start | bytes 2359304 | tf_op jit(solution)/shard_map/ppermute | solution.py:189
  44.9 35.7 %collective-permute-start.5 = (bf16[128,3072]{1,0:T(8,128)(2,1)}, bf16[128,3072]{1,0:T(8,128)(2,1)}, u32[]{:S(2)}, u32[]{:S(2)}) collective-permute-start(bf16[128,3072]{1,0:T(8,128)(2,1)} %collective-permute-done.4), channel_id=1, source_target_pairs={{1,0},{2,1},{5,4},{6,5},{9,8},{10,9},{13,12},{14,13},{17,16},{18,1... | collective-permute-start | bytes 2359304 | tf_op jit(solution)/shard_map/ppermute | solution.py:189
  83.2 24.4 %collective-permute-start.6 = (bf16[128,3072]{1,0:T(8,128)(2,1)}, bf16[128,3072]{1,0:T(8,128)(2,1)}, u32[]{:S(2)}, u32[]{:S(2)}) collective-permute-start(bf16[128,3072]{1,0:T(8,128)(2,1)} %get-tuple-element.97), channel_id=1, source_target_pairs={{2,3},{1,0},{6,7},{5,4},{10,11},{9,8},{14,15},{13,12},{18,19},{17,... | collective-permute-start | bytes 2359304 | tf_op jit(solution)/shard_map/ppermute | solution.py:191
  84.6 37.4 %collective-permute-start.7 = (bf16[2,256,768]{2,1,0:T(8,128)(2,1)}, bf16[2,256,768]{2,1,0:T(8,128)(2,1)S(1)}, u32[]{:S(2)}, u32[]{:S(2)}) collective-permute-start(bf16[2,256,768]{2,1,0:T(8,128)(2,1)} %get-tuple-element.89), channel_id=1, source_target_pairs={{0,2},{1,3},{2,0},{3,1},{4,6},{5,7},{6,4},{7,5},{8,10},{9,11},{10,... | collective-permute-start | bytes 2359304 | tf_op jit(solution)/shard_map/ppermute | solution.py:182
  122.1 20.7 %collective-permute-start.9 = (bf16[128,3072]{1,0:T(8,128)(2,1)}, bf16[128,3072]{1,0:T(8,128)(2,1)}, u32[]{:S(2)}, u32[]{:S(2)}) collective-permute-start(bf16[128,3072]{1,0:T(8,128)(2,1)} %bitcast.12), channel_id=1, source_target_pairs={{1,0},{2,1},{3,2},{5,4},{6,5},{7,6},{9,8},{10,9},{11,10},{13,12},{... | collective-permute-start | bytes 2359304 | tf_op jit(solution)/shard_map/ppermute | solution.py:189
  123.3 20.8 %collective-permute-start.8 = (bf16[128,3072]{1,0:T(8,128)(2,1)}, bf16[128,3072]{1,0:T(8,128)(2,1)}, u32[]{:S(2)}, u32[]{:S(2)}) collective-permute-start(bf16[128,3072]{1,0:T(8,128)(2,1)} %bitcast.12), channel_id=1, source_target_pairs={{0,1},{1,2},{2,3},{4,5},{5,6},{6,7},{8,9},{9,10},{10,11},{12,13},{... | collective-permute-start | bytes 2359304 | tf_op jit(solution)/shard_map/ppermute | solution.py:189
  142.8 21.7 %collective-permute-start.11 = (bf16[128,3072]{1,0:T(8,128)(2,1)}, bf16[128,3072]{1,0:T(8,128)(2,1)S(1)}, u32[]{:S(2)}, u32[]{:S(2)}) collective-permute-start(bf16[128,3072]{1,0:T(8,128)(2,1)} %collective-permute-done.9), channel_id=1, source_target_pairs={{1,0},{2,1},{5,4},{6,5},{9,8},{10,9},{13,12},{14,13},{17,16},{18,1... | collective-permute-start | bytes 2359304 | tf_op jit(solution)/shard_map/ppermute | solution.py:189
  144.1 20.4 %collective-permute-start.10 = (bf16[128,3072]{1,0:T(8,128)(2,1)}, bf16[128,3072]{1,0:T(8,128)(2,1)S(1)}, u32[]{:S(2)}, u32[]{:S(2)}) collective-permute-start(bf16[128,3072]{1,0:T(8,128)(2,1)} %collective-permute-done.8), channel_id=1, source_target_pairs={{1,2},{2,3},{5,6},{6,7},{9,10},{10,11},{13,14},{14,15},{17,18},{18... | collective-permute-start | bytes 2359304 | tf_op jit(solution)/shard_map/ppermute | solution.py:189
  164.6 21.0 %collective-permute-start.17 = (bf16[128,3072]{1,0:T(8,128)(2,1)S(1)}, bf16[128,3072]{1,0:T(8,128)(2,1)S(1)}, u32[]{:S(2)}, u32[]{:S(2)}) collective-permute-start(bf16[128,3072]{1,0:T(8,128)(2,1)S(1)} %get-tuple-element.95), channel_id=1, source_target_pairs={{2,3},{1,0},{6,7},{5,4},{10,11},{9,8},{14,15},{13,12},{18,19},{17,... | collective-permute-start | bytes 2359304 | tf_op jit(solution)/shard_map/ppermute | solution.py:191
  167.7 20.9 %collective-permute-start.12 = (bf16[128,3072]{1,0:T(8,128)(2,1)S(1)}, bf16[128,3072]{1,0:T(8,128)(2,1)S(1)}, u32[]{:S(2)}, u32[]{:S(2)}) collective-permute-start(bf16[128,3072]{1,0:T(8,128)(2,1)S(1)} %convert_select_fusion), channel_id=1, source_target_pairs={{0,1},{3,2},{4,5},{7,6},{8,9},{11,10},{12,13},{15,14},{16,17},{19,... | collective-permute-start | bytes 2359304 | tf_op jit(solution)/shard_map/ppermute | solution.py:191
  194.6 18.6 %collective-permute-start.13 = (bf16[128,3072]{1,0:T(8,128)(2,1)S(1)}, bf16[128,3072]{1,0:T(8,128)(2,1)S(1)}, u32[]{:S(2)}, u32[]{:S(2)}) collective-permute-start(bf16[128,3072]{1,0:T(8,128)(2,1)S(1)} %get-tuple-element.61), channel_id=1, source_target_pairs={{0,1},{1,2},{4,5},{5,6},{8,9},{9,10},{12,13},{13,14},{16,17},{17,1... | collective-permute-start | bytes 2359304 | tf_op jit(solution)/shard_map/ppermute | solution.py:189
  199.1 20.5 %collective-permute-start.15 = (bf16[128,3072]{1,0:T(8,128)(2,1)S(1)}, bf16[128,3072]{1,0:T(8,128)(2,1)S(1)}, u32[]{:S(2)}, u32[]{:S(2)}) collective-permute-start(bf16[128,3072]{1,0:T(8,128)(2,1)S(1)} %get-tuple-element.92), channel_id=1, source_target_pairs={{2,1},{3,2},{6,5},{7,6},{10,9},{11,10},{14,13},{15,14},{18,17},{19... | collective-permute-start | bytes 2359304 | tf_op jit(solution)/shard_map/ppermute | solution.py:189
  201.3 29.7 %collective-permute-start.18 = (bf16[192,3072]{1,0:T(8,128)(2,1)}, bf16[192,3072]{1,0:T(8,128)(2,1)S(1)}, u32[]{:S(2)}, u32[]{:S(2)}) collective-permute-start(bf16[192,3072]{1,0:T(8,128)(2,1)} %constant_dynamic-slice_fusion.3), channel_id=1, source_target_pairs={{0,4},{4,0},{8,12},{12,8},{16,20},{20,16},{24,28},{28,24},{1,5},{5... | collective-permute-start | bytes 3538952 | tf_op jit(solution)/shard_map/ppermute | solution.py:234
  201.3 32.5 %collective-permute-start.19 = (bf16[192,3072]{1,0:T(8,128)(2,1)S(1)}, bf16[192,3072]{1,0:T(8,128)(2,1)S(1)}, u32[]{:S(2)}, u32[]{:S(2)}) collective-permute-start(bf16[192,3072]{1,0:T(8,128)(2,1)S(1)} %constant_dynamic-slice_fusion.2), channel_id=1, source_target_pairs={{0,4},{4,0},{8,12},{12,8},{16,20},{20,16},{24,28},{28,24},{1,5},{5... | collective-permute-start | bytes 3538952 | tf_op jit(solution)/shard_map/ppermute | solution.py:234
  214.3 57.4 %collective-permute-start.14 = (bf16[128,3072]{1,0:T(8,128)(2,1)}, bf16[128,3072]{1,0:T(8,128)(2,1)}, u32[]{:S(2)}, u32[]{:S(2)}) collective-permute-start(bf16[128,3072]{1,0:T(8,128)(2,1)} %add_convert_fusion.8), channel_id=1, source_target_pairs={{0,1},{1,2},{2,3},{4,5},{5,6},{6,7},{8,9},{9,10},{10,11},{12,13},{... | collective-permute-start | bytes 2359304 | tf_op jit(solution)/shard_map/ppermute | solution.py:189
  220.7 51.2 %collective-permute-start.16 = (bf16[128,3072]{1,0:T(8,128)(2,1)}, bf16[128,3072]{1,0:T(8,128)(2,1)}, u32[]{:S(2)}, u32[]{:S(2)}) collective-permute-start(bf16[128,3072]{1,0:T(8,128)(2,1)} %add_convert_fusion.6), channel_id=1, source_target_pairs={{1,0},{2,1},{3,2},{5,4},{6,5},{7,6},{9,8},{10,9},{11,10},{13,12},{... | collective-permute-start | bytes 2359304 | tf_op jit(solution)/shard_map/ppermute | solution.py:189
  232.4 43.1 %collective-permute-start.37 = (bf16[96,3072]{1,0:T(8,128)(2,1)}, bf16[96,3072]{1,0:T(8,128)(2,1)}, u32[]{:S(2)}, u32[]{:S(2)}) collective-permute-start(bf16[96,3072]{1,0:T(8,128)(2,1)} %dynamic-slice_convert_fusion.1), channel_id=1, source_target_pairs={{0,8},{4,12},{8,0},{12,4},{16,24},{20,28},{24,16},{28,20},{1,9},{5... | collective-permute-start | bytes 1769480 | tf_op jit(solution)/shard_map/ppermute | solution.py:234
  245.6 78.8 %all-to-all-start = ((bf16[4,2,256,768]{3,2,1,0:T(8,128)(2,1)}), bf16[4,2,256,768]{3,2,1,0:T(8,128)(2,1)}, u32[]{:S(2)}, u32[]{:S(2)}) async-start(bf16[4,2,256,768]{3,2,1,0:T(8,128)(2,1)} %get-tuple-element.48), calls=%async_computation | async-start | bytes 6291456 | tf_op jit(solution)/shard_map/all_to_all | solution.py:321
  252.1 25.4 %collective-permute-start.42 = (bf16[96,3072]{1,0:T(8,128)(2,1)S(1)}, bf16[96,3072]{1,0:T(8,128)(2,1)S(1)}, u32[]{:S(2)}, u32[]{:S(2)}) collective-permute-start(bf16[96,3072]{1,0:T(8,128)(2,1)S(1)} %dynamic-slice_convert_fusion), channel_id=1, source_target_pairs={{0,16},{4,20},{8,24},{12,28},{16,0},{20,4},{24,8},{28,12},{1,17},{... | collective-permute-start | bytes 1769480 | tf_op jit(solution)/shard_map/ppermute | solution.py:234
  265.8 58.6 %collective-permute-start.20 = (bf16[128,3072]{1,0:T(8,128)(2,1)}, bf16[128,3072]{1,0:T(8,128)(2,1)}, u32[]{:S(2)}, u32[]{:S(2)}) collective-permute-start(bf16[128,3072]{1,0:T(8,128)(2,1)} %get-tuple-element.83), channel_id=1, source_target_pairs={{0,1},{3,2},{4,5},{7,6},{8,9},{11,10},{12,13},{15,14},{16,17},{19,... | collective-permute-start | bytes 2359304 | tf_op jit(solution)/shard_map/ppermute | solution.py:191
  271.7 24.0 %collective-permute-start.31 = (bf16[768,768]{1,0:T(8,128)(2,1)S(1)}, bf16[768,768]{1,0:T(8,128)(2,1)S(1)}, u32[]{:S(2)}, u32[]{:S(2)}) collective-permute-start(bf16[768,768]{1,0:T(8,128)(2,1)S(1)} %constant_dynamic-slice_fusion), channel_id=1, source_target_pairs={{0,4},{4,0},{8,12},{12,8},{16,20},{20,16},{24,28},{28,24},{1,5},{5... | collective-permute-start | bytes 3538952 | tf_op jit(solution)/shard_map/ppermute | solution.py:234
  271.8 24.5 %collective-permute-start.25 = (bf16[768,768]{1,0:T(8,128)(2,1)S(1)}, bf16[768,768]{1,0:T(8,128)(2,1)S(1)}, u32[]{:S(2)}, u32[]{:S(2)}) collective-permute-start(bf16[768,768]{1,0:T(8,128)(2,1)S(1)} %constant_dynamic-slice_fusion.1), channel_id=1, source_target_pairs={{0,4},{4,0},{8,12},{12,8},{16,20},{20,16},{24,28},{28,24},{1,5},{5... | collective-permute-start | bytes 3538952 | tf_op jit(solution)/shard_map/ppermute | solution.py:234
  276.9 8.5 %collective-permute-start.38 = (bf16[48,3072]{1,0:T(8,128)(2,1)S(1)}, bf16[48,3072]{1,0:T(8,128)(2,1)S(1)}, u32[]{:S(2)}, u32[]{:S(2)}) collective-permute-start(bf16[48,3072]{1,0:T(8,128)(2,1)S(1)} %dynamic-slice_convert_fusion.5), channel_id=1, source_target_pairs={{0,16},{4,20},{8,24},{12,28},{16,0},{20,4},{24,8},{28,12},{1,17},{... | collective-permute-start | bytes 884744 | tf_op jit(solution)/shard_map/ppermute | solution.py:234
  277.7 8.3 %collective-permute-start.43 = (bf16[48,3072]{1,0:T(8,128)(2,1)S(1)}, bf16[48,3072]{1,0:T(8,128)(2,1)S(1)}, u32[]{:S(2)}, u32[]{:S(2)}) collective-permute-start(bf16[48,3072]{1,0:T(8,128)(2,1)S(1)} %dynamic-slice_convert_fusion.4), channel_id=1, source_target_pairs={{0,8},{4,12},{8,0},{12,4},{16,24},{20,28},{24,16},{28,20},{1,9},{5... | collective-permute-start | bytes 884744 | tf_op jit(solution)/shard_map/ppermute | solution.py:234
  285.4 7.5 %collective-permute-start.39 = (bf16[48,3072]{1,0:T(8,128)(2,1)S(1)}, bf16[48,3072]{1,0:T(8,128)(2,1)S(1)}, u32[]{:S(2)}, u32[]{:S(2)}) collective-permute-start(bf16[48,3072]{1,0:T(8,128)(2,1)S(1)} %add_convert_fusion.11), channel_id=1, source_target_pairs={{0,16},{4,20},{8,24},{12,28},{16,0},{20,4},{24,8},{28,12},{1,17},{... | collective-permute-start | bytes 884744 | tf_op jit(solution)/shard_map/ppermute | solution.py:234
  286.1 7.6 %collective-permute-start.44 = (bf16[48,3072]{1,0:T(8,128)(2,1)S(1)}, bf16[48,3072]{1,0:T(8,128)(2,1)S(1)}, u32[]{:S(2)}, u32[]{:S(2)}) collective-permute-start(bf16[48,3072]{1,0:T(8,128)(2,1)S(1)} %add_convert_fusion.10), channel_id=1, source_target_pairs={{0,8},{4,12},{8,0},{12,4},{16,24},{20,28},{24,16},{28,20},{1,9},{5... | collective-permute-start | bytes 884744 | tf_op jit(solution)/shard_map/ppermute | solution.py:234
  293.1 13.0 %collective-permute-start.40 = (bf16[96,3072]{1,0:T(8,128)(2,1)S(1)}, bf16[96,3072]{1,0:T(8,128)(2,1)S(1)}, u32[]{:S(2)}, u32[]{:S(2)}) collective-permute-start(bf16[96,3072]{1,0:T(8,128)(2,1)S(1)} %maximum_select_fusion.10), channel_id=1, source_target_pairs={{0,8},{4,12},{8,0},{12,4},{16,24},{20,28},{24,16},{28,20},{1,9},{5... | collective-permute-start | bytes 1769480 | tf_op jit(solution)/shard_map/ppermute | solution.py:234
  293.8 16.3 %collective-permute-start.45 = (bf16[96,3072]{1,0:T(8,128)(2,1)S(1)}, bf16[96,3072]{1,0:T(8,128)(2,1)S(1)}, u32[]{:S(2)}, u32[]{:S(2)}) collective-permute-start(bf16[96,3072]{1,0:T(8,128)(2,1)S(1)} %maximum_select_fusion.11), channel_id=1, source_target_pairs={{0,16},{4,20},{8,24},{12,28},{16,0},{20,4},{24,8},{28,12},{1,17},{... | collective-permute-start | bytes 1769480 | tf_op jit(solution)/shard_map/ppermute | solution.py:234
  296.0 23.1 %collective-permute-start.32 = (bf16[384,768]{1,0:T(8,128)(2,1)S(1)}, bf16[384,768]{1,0:T(8,128)(2,1)S(1)}, u32[]{:S(2)}, u32[]{:S(2)}) collective-permute-start(bf16[384,768]{1,0:T(8,128)(2,1)S(1)} %dynamic-slice_convert_fusion.2), channel_id=1, source_target_pairs={{0,16},{4,20},{8,24},{12,28},{16,0},{20,4},{24,8},{28,12},{1,17},{... | collective-permute-start | bytes 1769480 | tf_op jit(solution)/shard_map/ppermute | solution.py:234
  306.3 17.2 %collective-permute-start.41 = (bf16[192,3072]{1,0:T(8,128)(2,1)S(1)}, bf16[192,3072]{1,0:T(8,128)(2,1)S(1)}, u32[]{:S(2)}, u32[]{:S(2)}) collective-permute-start(bf16[192,3072]{1,0:T(8,128)(2,1)S(1)} %maximum_select_fusion.6), channel_id=1, source_target_pairs={{0,4},{4,0},{8,12},{12,8},{16,20},{20,16},{24,28},{28,24},{1,5},{5... | collective-permute-start | bytes 3538952 | tf_op jit(solution)/shard_map/ppermute | solution.py:234
  306.5 15.8 %collective-permute-start.26 = (bf16[384,768]{1,0:T(8,128)(2,1)S(1)}, bf16[384,768]{1,0:T(8,128)(2,1)S(1)}, u32[]{:S(2)}, u32[]{:S(2)}) collective-permute-start(bf16[384,768]{1,0:T(8,128)(2,1)S(1)} %dynamic-slice_convert_fusion.3), channel_id=1, source_target_pairs={{0,8},{4,12},{8,0},{12,4},{16,24},{20,28},{24,16},{28,20},{1,9},{5... | collective-permute-start | bytes 1769480 | tf_op jit(solution)/shard_map/ppermute | solution.py:234
  310.4 18.1 %collective-permute-start.46 = (bf16[192,3072]{1,0:T(8,128)(2,1)S(1)}, bf16[192,3072]{1,0:T(8,128)(2,1)}, u32[]{:S(2)}, u32[]{:S(2)}) collective-permute-start(bf16[192,3072]{1,0:T(8,128)(2,1)S(1)} %maximum_select_fusion.7), channel_id=1, source_target_pairs={{0,4},{4,0},{8,12},{12,8},{16,20},{20,16},{24,28},{28,24},{1,5},{5... | collective-permute-start | bytes 3538952 | tf_op jit(solution)/shard_map/ppermute | solution.py:234
  326.5 8.7 %collective-permute-start.33 = (bf16[192,768]{1,0:T(8,128)(2,1)S(1)}, bf16[192,768]{1,0:T(8,128)(2,1)S(1)}, u32[]{:S(2)}, u32[]{:S(2)}) collective-permute-start(bf16[192,768]{1,0:T(8,128)(2,1)S(1)} %copy-done.18), channel_id=1, source_target_pairs={{0,8},{4,12},{8,0},{12,4},{16,24},{20,28},{24,16},{28,20},{1,9},{5... | collective-permute-start | bytes 884744 | tf_op jit(solution)/shard_map/ppermute | solution.py:234
  327.1 8.7 %collective-permute-start.27 = (bf16[192,768]{1,0:T(8,128)(2,1)S(1)}, bf16[192,768]{1,0:T(8,128)(2,1)S(1)}, u32[]{:S(2)}, u32[]{:S(2)}) collective-permute-start(bf16[192,768]{1,0:T(8,128)(2,1)S(1)} %copy-done.17), channel_id=1, source_target_pairs={{0,16},{4,20},{8,24},{12,28},{16,0},{20,4},{24,8},{28,12},{1,17},{... | collective-permute-start | bytes 884744 | tf_op jit(solution)/shard_map/ppermute | solution.py:234
  330.5 17.7 %collective-permute-start.21 = (bf16[128,3072]{1,0:T(8,128)(2,1)S(1)}, bf16[128,3072]{1,0:T(8,128)(2,1)S(1)}, u32[]{:S(2)}, u32[]{:S(2)}) collective-permute-start(bf16[128,3072]{1,0:T(8,128)(2,1)S(1)} %get-tuple-element.57), channel_id=1, source_target_pairs={{0,1},{1,2},{4,5},{5,6},{8,9},{9,10},{12,13},{13,14},{16,17},{17,1... | collective-permute-start | bytes 2359304 | tf_op jit(solution)/shard_map/ppermute | solution.py:189
  335.2 8.0 %collective-permute-start.34 = (bf16[192,768]{1,0:T(8,128)(2,1)S(1)}, bf16[192,768]{1,0:T(8,128)(2,1)S(1)}, u32[]{:S(2)}, u32[]{:S(2)}) collective-permute-start(bf16[192,768]{1,0:T(8,128)(2,1)S(1)} %add_convert_fusion.12), channel_id=1, source_target_pairs={{0,8},{4,12},{8,0},{12,4},{16,24},{20,28},{24,16},{28,20},{1,9},{5... | collective-permute-start | bytes 884744 | tf_op jit(solution)/shard_map/ppermute | solution.py:234
  335.9 8.8 %collective-permute-start.28 = (bf16[192,768]{1,0:T(8,128)(2,1)S(1)}, bf16[192,768]{1,0:T(8,128)(2,1)S(1)}, u32[]{:S(2)}, u32[]{:S(2)}) collective-permute-start(bf16[192,768]{1,0:T(8,128)(2,1)S(1)} %add_convert_fusion.13), channel_id=1, source_target_pairs={{0,16},{4,20},{8,24},{12,28},{16,0},{20,4},{24,8},{28,12},{1,17},{... | collective-permute-start | bytes 884744 | tf_op jit(solution)/shard_map/ppermute | solution.py:234
  342.4 10.7 %collective-permute-start.23 = (bf16[128,3072]{1,0:T(8,128)(2,1)S(1)}, bf16[128,3072]{1,0:T(8,128)(2,1)S(1)}, u32[]{:S(2)}, u32[]{:S(2)}) collective-permute-start(bf16[128,3072]{1,0:T(8,128)(2,1)S(1)} %get-tuple-element.90), channel_id=1, source_target_pairs={{2,1},{3,2},{6,5},{7,6},{10,9},{11,10},{14,13},{15,14},{18,17},{19... | collective-permute-start | bytes 2359304 | tf_op jit(solution)/shard_map/ppermute | solution.py:189
  343.4 13.5 %collective-permute-start.35 = (bf16[384,768]{1,0:T(8,128)(2,1)S(1)}, bf16[384,768]{1,0:T(8,128)(2,1)S(1)}, u32[]{:S(2)}, u32[]{:S(2)}) collective-permute-start(bf16[384,768]{1,0:T(8,128)(2,1)S(1)} %maximum_select_fusion.9), channel_id=1, source_target_pairs={{0,16},{4,20},{8,24},{12,28},{16,0},{20,4},{24,8},{28,12},{1,17},{... | collective-permute-start | bytes 1769480 | tf_op jit(solution)/shard_map/ppermute | solution.py:234
  344.9 12.9 %collective-permute-start.29 = (bf16[384,768]{1,0:T(8,128)(2,1)S(1)}, bf16[384,768]{1,0:T(8,128)(2,1)S(1)}, u32[]{:S(2)}, u32[]{:S(2)}) collective-permute-start(bf16[384,768]{1,0:T(8,128)(2,1)S(1)} %maximum_select_fusion.8), channel_id=1, source_target_pairs={{0,8},{4,12},{8,0},{12,4},{16,24},{20,28},{24,16},{28,20},{1,9},{5... | collective-permute-start | bytes 1769480 | tf_op jit(solution)/shard_map/ppermute | solution.py:234
  348.4 19.8 %collective-permute-start.22 = (bf16[128,3072]{1,0:T(8,128)(2,1)S(1)}, bf16[128,3072]{1,0:T(8,128)(2,1)S(1)}, u32[]{:S(2)}, u32[]{:S(2)}) collective-permute-start(bf16[128,3072]{1,0:T(8,128)(2,1)S(1)} %add_convert_fusion.3), channel_id=1, source_target_pairs={{0,1},{1,2},{2,3},{4,5},{5,6},{6,7},{8,9},{9,10},{10,11},{12,13},{... | collective-permute-start | bytes 2359304 | tf_op jit(solution)/shard_map/ppermute | solution.py:189
  353.3 24.5 %collective-permute-start.24 = (bf16[128,3072]{1,0:T(8,128)(2,1)S(1)}, bf16[128,3072]{1,0:T(8,128)(2,1)S(1)}, u32[]{:S(2)}, u32[]{:S(2)}) collective-permute-start(bf16[128,3072]{1,0:T(8,128)(2,1)S(1)} %add_convert_fusion.1), channel_id=1, source_target_pairs={{1,0},{2,1},{3,2},{5,4},{6,5},{7,6},{9,8},{10,9},{11,10},{13,12},{... | collective-permute-start | bytes 2359304 | tf_op jit(solution)/shard_map/ppermute | solution.py:189
  357.4 21.5 %collective-permute-start.36 = (bf16[768,768]{1,0:T(8,128)(2,1)S(1)}, bf16[768,768]{1,0:T(8,128)(2,1)S(1)}, u32[]{:S(2)}, u32[]{:S(2)}) collective-permute-start(bf16[768,768]{1,0:T(8,128)(2,1)S(1)} %maximum_select_fusion.5), channel_id=1, source_target_pairs={{0,4},{4,0},{8,12},{12,8},{16,20},{20,16},{24,28},{28,24},{1,5},{5... | collective-permute-start | bytes 3538952 | tf_op jit(solution)/shard_map/ppermute | solution.py:234
  358.2 21.5 %collective-permute-start.30 = (bf16[768,768]{1,0:T(8,128)(2,1)S(1)}, bf16[768,768]{1,0:T(8,128)(2,1)S(1)}, u32[]{:S(2)}, u32[]{:S(2)}) collective-permute-start(bf16[768,768]{1,0:T(8,128)(2,1)S(1)} %maximum_select_fusion.4), channel_id=1, source_target_pairs={{0,4},{4,0},{8,12},{12,8},{16,20},{20,16},{24,28},{28,24},{1,5},{5... | collective-permute-start | bytes 3538952 | tf_op jit(solution)/shard_map/ppermute | solution.py:234
  (23 other events, 221.0 us)

commit v3 on v2

--- a/solution.py
+++ b/solution.py
@@ -289,7 +289,7 @@
     gathered = join(video[0], rows, me)
     query = jnp.dot(gathered, w_query, preferred_element_type=F32).astype(BF16)
     per = heads // chunks
-    grad = after(cotangent[0], rows[0][-1], rows[1][-1], *pieces[1:])
+    grad = after(cotangent[0], rows[0][-2], rows[1][-2], *[pieces[k] for k in order[:-1]])
     cots = gather_step(grad, ([], []), n, me)
     attention = []
     for c in range(chunks):
@@ -310,11 +310,11 @@
     grad_rows = after(grad_rows, *marks[0])
 
     grad_wo = contract_first(attention, grad_rows).astype(BF16)
-    grad_attention = after(contract_last(grad_rows, w_out).astype(BF16), grad_wo, *marks[-2])
+    grad_attention = after(contract_last(grad_rows, w_out).astype(BF16), grad_wo)
     sum_wo = ClipSum(grad_wo, [masks, masks[:1] + masks[:0:-1]])
     source = lax.rem(me - jnp.arange(n, dtype=jnp.int32) + n, n)
     back = attend_back(table, source, query, grad_attention, pieces, scale, 0, per)
-    grad_attention = after(grad_attention, *sum_wo.step())
+    grad_attention = after(grad_attention, *sum_wo.step(), *marks[-2])
     for c in range(1, chunks):
         back = attend_back(table, source, query, grad_attention, pieces, scale, c * per, per, back)
     grad_query, grad_kv = back
@@ -333,8 +333,10 @@
         sums = scatter_step(parts, sums, n, me)
         if s == 1:
             sum_wq.step(*sums[1:])
-    grad_video = (parts[0] + sums[1].astype(F32) + sums[2].astype(F32)).astype(BF16)
-    return (output[None], grad_video[None], sum_wq.result(), sum_wo.result(), grad_ref[None])
+    weights = sum_wq.result(), sum_wo.result()
+    last = after(parts[0], *weights)
+    grad_video = (last + sums[1].astype(F32) + sums[2].astype(F32)).astype(BF16)
+    return (output[None], grad_video[None], *weights, grad_ref[None])
 
 
 def solution(mesh):

time: 386 us -> 370 us (0.959)
  waiting for transfers between devices: 194 us -> 176 us
    ppermute x16, waiting for transfers between devices: 72.6 us -> 53.4 us  [both_ways(): return (lax.ppermute(right, 'seq', up), lax.ppermute(left, 'seq', down))]
    ppermute x3, waiting for transfers between devices: 46.3 us -> 34.4 us  [shift(): return lax.ppermute(array, 'seq', [(i, (i + by) % n) for i in range(n)])]
    ppermute x24, waiting for transfers between devices: 40.4 us -> 48.8 us  [exchange(): return lax.ppermute(block, 'dp', [(i, i ^ mask) for i in range(self.size)])]
    ppermute x4, waiting for transfers between devices: 34.5 us -> 38.9 us  [both_ways(): came = lax.ppermute(jnp.where(rightward, right, left), 'seq', up + down)]
  transfers between devices with their start and end apart: 48 -> 48, of which waited for: 23 -> 21; matrix products, arithmetic and copies ran while one was open for 18% -> 21% of each run, Pallas kernels for 7% -> 7%
where the time goes in v3:
time: 370 us; the launch traced here: 368 us
  waiting for transfers between devices  176 us (48%)
  starting transfers between devices  76.7 us (21%)
  other arithmetic  45.8 us (12%)
  Pallas kernels  27.4 us (7%)
  matrix products  24.6 us (7%)
  local copies, waits for them, and re-layouts  16.9 us (5%)
    ppermute x16, waiting for transfers between devices, both_ways(): return (lax.ppermute(right, 'seq', up), lax.ppermute(left, 'seq', down))  53.4 us
    ppermute x24, waiting for transfers between devices, exchange(): return lax.ppermute(block, 'dp', [(i, i ^ mask) for i in range(self.size)])  48.8 us
    ppermute x4, waiting for transfers between devices, both_ways(): came = lax.ppermute(jnp.where(rightward, right, left), 'seq', up + down)  38.9 us
    ppermute x16, starting transfers between devices, both_ways(): return (lax.ppermute(right, 'seq', up), lax.ppermute(left, 'seq', down))  37.1 us
    ppermute x3, waiting for transfers between devices, shift(): return lax.ppermute(array, 'seq', [(i, (i + by) % n) for i in range(n)])  34.4 us
    pallas_call x2, Pallas kernels, attend_back(): pl.pallas_call(functools.partial(backward_kernel, n, scale), out_shape=[j...  18.2 us
    ppermute x24, starting transfers between devices, exchange(): return lax.ppermute(block, 'dp', [(i, i ^ mask) for i in range(self.size)])  16.9 us
    ppermute x4, starting transfers between devices, both_ways(): came = lax.ppermute(jnp.where(rightward, right, left), 'seq', up + down)  12.2 us
  transfers between devices with their start and end apart: 48, of which 21 were waited for; matrix products, arithmetic and copies ran while one was open for 21% of the time, Pallas kernels for 7%

profile of v3, /device:TPU:0, one launch (start us, length us, event | category | flops | bytes accessed | tf_op | source)
XLA Modules:
  0.0 368.4 jit_solution(14600070176229511881)
XLA Ops:
  0.6 5.0 %collective-permute-start = (bf16[128,3072]{1,0:T(8,128)(2,1)}, bf16[128,3072]{1,0:T(8,128)(2,1)S(1)}, u32[]{:S(2)}, u32[]{:S(2)}) collective-permute-start(bf16[128,3072]{1,0:T(8,128)(2,1)} %bitcast.46), channel_id=1, source_target_pairs={{0,1},{1,2},{2,3},{4,5},{5,6},{6,7},{8,9},{9,10},{10,11},{12,13},{... | collective-permute-start | bytes 2359304 | tf_op jit(solution)/shard_map/ppermute | solution.py:189
  5.7 3.3 dynamic-slice_bitcast_fusion
  11.6 2.7 collective-permute-start.3
  14.3 9.5 %collective-permute-done = bf16[128,3072]{1,0:T(8,128)(2,1)S(1)} collective-permute-done((bf16[128,3072]{1,0:T(8,128)(2,1)}, bf16[128,3072]{1,0:T(8,128)(2,1)S(1)}, u32[]{:S(2)}, u32[]{:S(2)}) %collective-permute-start) | collective-permute-done | bytes 786464 | tf_op jit(solution)/shard_map/ppermute | solution.py:189
  23.8 16.8 %collective-permute-done.1.refs_3_ = bf16[2,256,768]{2,1,0:T(8,128)(2,1)S(1)} collective-permute-done((bf16[2,256,768]{2,1,0:T(8,128)(2,1)S(1)}, bf16[2,256,768]{2,1,0:T(8,128)(2,1)S(1)}, u32[]{:S(2)}, u32[]{:S(2)}) %collective-permute-start.1) | collective-permute-done | bytes 786464 | tf_op jit(solution)/shard_map/ppermute | solution.py:182
  42.1 2.8 collective-permute-done.4
  46.2 17.6 %collective-permute-done.3.refs_1_ = bf16[2,256,768]{2,1,0:T(8,128)(2,1)S(1)} collective-permute-done((bf16[2,256,768]{2,1,0:T(8,128)(2,1)}, bf16[2,256,768]{2,1,0:T(8,128)(2,1)S(1)}, u32[]{:S(2)}, u32[]{:S(2)}) %collective-permute-start.3) | collective-permute-done | bytes 786464 | tf_op jit(solution)/shard_map/ppermute | solution.py:182
  63.8 16.7 %collective-permute-done.5 = bf16[128,3072]{1,0:T(8,128)(2,1)} collective-permute-done((bf16[128,3072]{1,0:T(8,128)(2,1)}, bf16[128,3072]{1,0:T(8,128)(2,1)}, u32[]{:S(2)}, u32[]{:S(2)}) %collective-permute-start.5) | collective-permute-done | bytes 786464 | tf_op jit(solution)/shard_map/ppermute | solution.py:189
  81.9 5.5 %collective-permute-start.8 = (bf16[128,3072]{1,0:T(8,128)(2,1)}, bf16[128,3072]{1,0:T(8,128)(2,1)}, u32[]{:S(2)}, u32[]{:S(2)}) collective-permute-start(bf16[128,3072]{1,0:T(8,128)(2,1)} %bitcast.12), channel_id=1, source_target_pairs={{0,1},{1,2},{2,3},{4,5},{5,6},{6,7},{8,9},{9,10},{10,11},{12,13},{... | collective-permute-start | bytes 2359304 | tf_op jit(solution)/shard_map/ppermute | solution.py:189
  87.3 2.6 broadcast_select_fusion.6
  93.2 10.1 %collective-permute-done.9 = bf16[128,3072]{1,0:T(8,128)(2,1)} collective-permute-done((bf16[128,3072]{1,0:T(8,128)(2,1)}, bf16[128,3072]{1,0:T(8,128)(2,1)}, u32[]{:S(2)}, u32[]{:S(2)}) %collective-permute-start.9) | collective-permute-done | bytes 786464 | tf_op jit(solution)/shard_map/ppermute | solution.py:189
  105.4 31.4 %collective-permute-done.6 = bf16[128,3072]{1,0:T(8,128)(2,1)} collective-permute-done((bf16[128,3072]{1,0:T(8,128)(2,1)}, bf16[128,3072]{1,0:T(8,128)(2,1)}, u32[]{:S(2)}, u32[]{:S(2)}) %collective-permute-start.6) | collective-permute-done | bytes 786464 | tf_op jit(solution)/shard_map/ppermute | solution.py:191
  138.4 5.5 %convolution_convert_fusion.4.q_ref = bf16[512,768]{1,0:T(8,128)(2,1)S(1)} fusion(bf16[3072,768]{1,0:T(8,128)(2,1)} %param.8, bf16[128,3072]{1,0:T(8,128)(2,1)S(1)} %get-tuple-element.99, bf16[128,3072]{1,0:T(8,128)(2,1)S(1)} %copy-done.18, bf16[128,3072]{1,0:T(8,128)(2,1)S(1)} %get-tuple-element.98, bf16[128,3072]{1,0:T(8,128)(2,1)S(1)} %bitcast.49), kind=kOutput, calls=%fused_computation.29 | convolution fusion | flops 2428895232 | bytes 8650752 | tf_op jit(solution)/shard_map/dot_general | solution.py:290
  143.9 4.6 %shard_map.101 = bf16[512,384]{1,0:T(8,128)(2,1)S(1)} custom-call(s32[4,8]{1,0:T(4,128)S(1)} %copy.22.table_ref, bf16[512,768]{1,0:T(8,128)(2,1)S(1)} %convolution_convert_fusion.4.q_ref, bf16[2,256,768]{2,1,0:T(8,128)(2,1)S(1)} %get-tuple-element.87.refs_0_, bf16[2,256,768]{2,1,0:T(8,128)(2,1)S(1)} %collective-permute-done.3.refs_1_, ...), custom_call_target="tpu_custom_call" | custom-call | flops 805306368 | bytes 2359296 | tf_op jit(solution)/shard_map/pallas_call | solution.py:131
  148.5 4.6 %shard_map.102 = bf16[512,384]{1,0:T(8,128)(2,1)S(1)} custom-call(s32[4,8]{1,0:T(4,128)S(1)} %copy.22.table_ref, bf16[512,768]{1,0:T(8,128)(2,1)S(1)} %convolution_convert_fusion.4.q_ref, bf16[2,256,768]{2,1,0:T(8,128)(2,1)S(1)} %get-tuple-element.87.refs_0_, bf16[2,256,768]{2,1,0:T(8,128)(2,1)S(1)} %collective-permute-done.3.refs_1_, ...), custom_call_target="tpu_custom_call" | custom-call | flops 805306368 | bytes 2359296 | tf_op jit(solution)/shard_map/pallas_call | solution.py:131
  153.2 4.5 %fusion.1 = f32[512,3072]{1,0:T(8,128)S(1)} fusion(bf16[768,3072]{1,0:T(8,128)(2,1)} %param.9, bf16[512,384]{1,0:T(8,128)(2,1)S(1)} %shard_map.102, bf16[512,384]{1,0:T(8,128)(2,1)S(1)} %shard_map.101), kind=kOutput, calls=%fused_computation.82 | convolution fusion | flops 2417491968 | bytes 11796480 | tf_op jit(solution)/shard_map/dot_general | solution.py:299
  161.1 4.8 %collective-permute-start.12 = (bf16[128,3072]{1,0:T(8,128)(2,1)S(1)}, bf16[128,3072]{1,0:T(8,128)(2,1)S(1)}, u32[]{:S(2)}, u32[]{:S(2)}) collective-permute-start(bf16[128,3072]{1,0:T(8,128)(2,1)S(1)} %convert_select_fusion), channel_id=1, source_target_pairs={{0,1},{3,2},{4,5},{7,6},{8,9},{11,10},{12,13},{15,14},{16,17},{19,... | collective-permute-start | bytes 2359304 | tf_op jit(solution)/shard_map/ppermute | solution.py:191
  165.9 7.2 %collective-permute-done.17 = bf16[128,3072]{1,0:T(8,128)(2,1)S(1)} collective-permute-done((bf16[128,3072]{1,0:T(8,128)(2,1)S(1)}, bf16[128,3072]{1,0:T(8,128)(2,1)S(1)}, u32[]{:S(2)}, u32[]{:S(2)}) %collective-permute-start.17) | collective-permute-done | bytes 786464 | tf_op jit(solution)/shard_map/ppermute | solution.py:191
  176.7 2.7 convolution_convert_fusion.3.g_ref
  179.4 2.9 convolution_convert_fusion.1
  182.6 5.3 %collective-permute-start.13 = (bf16[128,3072]{1,0:T(8,128)(2,1)S(1)}, bf16[128,3072]{1,0:T(8,128)(2,1)}, u32[]{:S(2)}, u32[]{:S(2)}) collective-permute-start(bf16[128,3072]{1,0:T(8,128)(2,1)S(1)} %get-tuple-element.63), channel_id=1, source_target_pairs={{0,1},{1,2},{4,5},{5,6},{8,9},{9,10},{12,13},{13,14},{16,17},{17,1... | collective-permute-start | bytes 2359304 | tf_op jit(solution)/shard_map/ppermute | solution.py:189
  191.2 9.1 %shard_map.103 = (bf16[512,768]{1,0:T(8,128)(2,1)S(1)}, bf16[4,2,256,768]{3,2,1,0:T(8,128)(2,1)}) custom-call(s32[4,8]{1,0:T(4,128)S(1)} %copy.22.table_ref, s32[4]{0:T(128)S(1)} %compare_select_fusion.1.source_ref, bf16[512,768]{1,0:T(8,128)(2,1)S(1)} %convolution_convert_fusion.4.q_ref, bf16[512,768]{1,0:T(8,128)(2,1)S(1)} %convolution_convert_fusion.3.g_ref, ...), custom_call_target="tpu_custom_call" | custom-call | flops 2013265920 | bytes 4325376 | tf_op jit(solution)/shard_map/pallas_call | solution.py:154
  200.3 2.2 add_convert_fusion.8
  202.5 4.1 %collective-permute-start.14 = (bf16[128,3072]{1,0:T(8,128)(2,1)}, bf16[128,3072]{1,0:T(8,128)(2,1)}, u32[]{:S(2)}, u32[]{:S(2)}) collective-permute-start(bf16[128,3072]{1,0:T(8,128)(2,1)} %add_convert_fusion.8), channel_id=1, source_target_pairs={{0,1},{1,2},{2,3},{4,5},{5,6},{6,7},{8,9},{9,10},{10,11},{12,13},{... | collective-permute-start | bytes 2359304 | tf_op jit(solution)/shard_map/ppermute | solution.py:189
  206.6 2.2 add_convert_fusion.6
  214.2 3.0 convert_add_fusion.2
  217.2 9.1 %shard_map.104 = (bf16[512,768]{1,0:T(8,128)(2,1)S(1)}, bf16[4,2,256,768]{3,2,1,0:T(8,128)(2,1)}) custom-call(s32[4,8]{1,0:T(4,128)S(1)} %copy.22.table_ref, s32[4]{0:T(128)S(1)} %compare_select_fusion.1.source_ref, bf16[512,768]{1,0:T(8,128)(2,1)S(1)} %convolution_convert_fusion.4.q_ref, ...), custom_call_target="tpu_custom_call", output_to_operand_aliasing={{0}: (8, {}), {1}: (9, {})} | custom-call | flops 2013265920 | bytes 4325376 | tf_op jit(solution)/shard_map/pallas_call | solution.py:154
  227.2 5.9 %all-to-all-start = ((bf16[4,2,256,768]{3,2,1,0:T(8,128)(2,1)}), bf16[4,2,256,768]{3,2,1,0:T(8,128)(2,1)}, u32[]{:S(2)}, u32[]{:S(2)}) async-start(bf16[4,2,256,768]{3,2,1,0:T(8,128)(2,1)} %get-tuple-element.49), calls=%async_computation | async-start | bytes 6291456 | tf_op jit(solution)/shard_map/all_to_all | solution.py:321
  236.1 3.8 %convolution_convert_fusion = bf16[3072,768]{1,0:T(8,128)(2,1)S(1)} fusion(bf16[512,768]{1,0:T(8,128)(2,1)S(1)} %copy-done.1, bf16[128,3072]{1,0:T(8,128)(2,1)S(1)} %copy-done.17, bf16[128,3072]{1,0:T(8,128)(2,1)S(1)} %copy-done.19, bf16[128,3072]{1,0:T(8,128)(2,1)S(1)} %copy-done.15, bf16[128,3072]{1,0:T(8,128)(2,1)} %bitcast.47), kind=kOutput, calls=%fused_computation.2 | convolution fusion | flops 2430861312 | bytes 8650752 | tf_op jit(solution)/shard_map/dot_general | solution.py:23
  239.9 5.2 %convolution_convert_fusion.2 = bf16[512,3072]{1,0:T(8,128)(2,1)S(1)} fusion(bf16[512,768]{1,0:T(8,128)(2,1)S(1)} %copy-done.1, bf16[3072,768]{1,0:T(8,128)(2,1)} %param.8), kind=kOutput, calls=%fused_computation.6 | convolution fusion | flops 2417491968 | bytes 8650752 | tf_op jit(solution)/shard_map/dot_general | solution.py:19
  245.1 3.0 slice_convert_fusion.2
  248.1 4.8 %collective-permute-start.22 = (bf16[128,3072]{1,0:T(8,128)(2,1)}, bf16[128,3072]{1,0:T(8,128)(2,1)}, u32[]{:S(2)}, u32[]{:S(2)}) collective-permute-start(bf16[128,3072]{1,0:T(8,128)(2,1)} %get-tuple-element.81), channel_id=1, source_target_pairs={{0,1},{3,2},{4,5},{7,6},{8,9},{11,10},{12,13},{15,14},{16,17},{19,... | collective-permute-start | bytes 2359304 | tf_op jit(solution)/shard_map/ppermute | solution.py:191
  254.6 2.6 add_convert_fusion.5
  260.0 7.1 %collective-permute-done.34 = bf16[48,3072]{1,0:T(8,128)(2,1)S(1)} collective-permute-done((bf16[48,3072]{1,0:T(8,128)(2,1)S(1)}, bf16[48,3072]{1,0:T(8,128)(2,1)S(1)}, u32[]{:S(2)}, u32[]{:S(2)}) %collective-permute-start.34) | collective-permute-done | bytes 294944 | tf_op jit(solution)/shard_map/ppermute | solution.py:234
  268.4 6.4 %collective-permute-done.35 = bf16[48,3072]{1,0:T(8,128)(2,1)S(1)} collective-permute-done((bf16[48,3072]{1,0:T(8,128)(2,1)S(1)}, bf16[48,3072]{1,0:T(8,128)(2,1)S(1)}, u32[]{:S(2)}, u32[]{:S(2)}) %collective-permute-start.35) | collective-permute-done | bytes 294944 | tf_op jit(solution)/shard_map/ppermute | solution.py:234
  278.4 9.5 %collective-permute-done.36 = bf16[96,3072]{1,0:T(8,128)(2,1)S(1)} collective-permute-done((bf16[96,3072]{1,0:T(8,128)(2,1)S(1)}, bf16[96,3072]{1,0:T(8,128)(2,1)S(1)}, u32[]{:S(2)}, u32[]{:S(2)}) %collective-permute-start.36) | collective-permute-done | bytes 589856 | tf_op jit(solution)/shard_map/ppermute | solution.py:234
  289.0 3.0 collective-permute-done.41
  292.3 8.7 %collective-permute-done.28 = bf16[384,768]{1,0:T(8,128)(2,1)S(1)} collective-permute-done((bf16[384,768]{1,0:T(8,128)(2,1)S(1)}, bf16[384,768]{1,0:T(8,128)(2,1)S(1)}, u32[]{:S(2)}, u32[]{:S(2)}) %collective-permute-start.28) | collective-permute-done | bytes 589856 | tf_op jit(solution)/shard_map/ppermute | solution.py:234
  306.3 2.0 add_convert_fusion.4
  310.4 2.0 maximum_select_fusion.3
  312.4 4.8 %collective-permute-done.29 = bf16[192,768]{1,0:T(8,128)(2,1)S(1)} collective-permute-done((bf16[192,768]{1,0:T(8,128)(2,1)S(1)}, bf16[192,768]{1,0:T(8,128)(2,1)S(1)}, u32[]{:S(2)}, u32[]{:S(2)}) %collective-permute-start.29) | collective-permute-done | bytes 294944 | tf_op jit(solution)/shard_map/ppermute | solution.py:234
  319.3 5.0 %maximum_convert_fusion.1 = f32[768,3072]{1,0:T(8,128)} fusion(bf16[384,3072]{1,0:T(8,128)(2,1)S(1)} %maximum_select_fusion.3, bf16[384,3072]{1,0:T(8,128)(2,1)S(1)} %maximum_select_fusion.2), kind=kLoop, calls=%fused_computation.5 | loop fusion | flops 9437184 | bytes 14155776 | tf_op jit(solution)/shard_map/convert_element_type | solution.py:262
  329.3 2.0 slice_bitcast_fusion.3
  333.2 7.3 %collective-permute-done.31 = bf16[384,768]{1,0:T(8,128)(2,1)S(1)} collective-permute-done((bf16[384,768]{1,0:T(8,128)(2,1)S(1)}, bf16[384,768]{1,0:T(8,128)(2,1)S(1)}, u32[]{:S(2)}, u32[]{:S(2)}) %collective-permute-start.31) | collective-permute-done | bytes 589856 | tf_op jit(solution)/shard_map/ppermute | solution.py:234
  342.3 3.6 collective-permute-start.44
  348.7 4.5 %maximum_convert_fusion = f32[3072,768]{1,0:T(8,128)} fusion(bf16[1536,768]{1,0:T(8,128)(2,1)S(1)} %maximum_select_fusion.1, bf16[1536,768]{1,0:T(8,128)(2,1)S(1)} %maximum_select_fusion), kind=kLoop, calls=%fused_computation.4 | loop fusion | flops 9437184 | bytes 14155776 | tf_op jit(solution)/shard_map/convert_element_type | solution.py:262
  353.1 9.1 %collective-permute-done.44 = bf16[128,3072]{1,0:T(8,128)(2,1)S(1)} collective-permute-done((bf16[128,3072]{1,0:T(8,128)(2,1)S(1)}, bf16[128,3072]{1,0:T(8,128)(2,1)S(1)}, u32[]{:S(2)}, u32[]{:S(2)}) %collective-permute-start.44) | collective-permute-done | bytes 786464 | tf_op jit(solution)/shard_map/ppermute | solution.py:189
  362.3 5.0 %collective-permute-done.46 = bf16[128,3072]{1,0:T(8,128)(2,1)S(1)} collective-permute-done((bf16[128,3072]{1,0:T(8,128)(2,1)S(1)}, bf16[128,3072]{1,0:T(8,128)(2,1)S(1)}, u32[]{:S(2)}, u32[]{:S(2)}) %collective-permute-start.46) | collective-permute-done | bytes 786464 | tf_op jit(solution)/shard_map/ppermute | solution.py:189
  (184 shorter events, 65.8 us)
Async XLA Ops:
  0.6 23.2 %collective-permute-start = (bf16[128,3072]{1,0:T(8,128)(2,1)}, bf16[128,3072]{1,0:T(8,128)(2,1)S(1)}, u32[]{:S(2)}, u32[]{:S(2)}) collective-permute-start(bf16[128,3072]{1,0:T(8,128)(2,1)} %bitcast.46), channel_id=1, source_target_pairs={{0,1},{1,2},{2,3},{4,5},{5,6},{6,7},{8,9},{9,10},{10,11},{12,13},{... | collective-permute-start | bytes 2359304 | tf_op jit(solution)/shard_map/ppermute | solution.py:189
  8.9 31.7 %collective-permute-start.1 = (bf16[2,256,768]{2,1,0:T(8,128)(2,1)S(1)}, bf16[2,256,768]{2,1,0:T(8,128)(2,1)S(1)}, u32[]{:S(2)}, u32[]{:S(2)}) collective-permute-start(bf16[2,256,768]{2,1,0:T(8,128)(2,1)S(1)} %get-tuple-element.86), channel_id=1, source_target_pairs={{0,3},{1,0},{2,1},{3,2},{4,7},{5,4},{6,5},{7,6},{8,11},{9,8},{10,9... | collective-permute-start | bytes 2359304 | tf_op jit(solution)/shard_map/ppermute | solution.py:182
  10.3 34.6 %collective-permute-start.4 = (bf16[128,3072]{1,0:T(8,128)(2,1)S(1)}, bf16[128,3072]{1,0:T(8,128)(2,1)}, u32[]{:S(2)}, u32[]{:S(2)}) collective-permute-start(bf16[128,3072]{1,0:T(8,128)(2,1)S(1)} %bitcast.48), channel_id=1, source_target_pairs={{1,0},{2,1},{3,2},{5,4},{6,5},{7,6},{9,8},{10,9},{11,10},{13,12},{... | collective-permute-start | bytes 2359304 | tf_op jit(solution)/shard_map/ppermute | solution.py:189
  11.6 52.2 %collective-permute-start.3 = (bf16[2,256,768]{2,1,0:T(8,128)(2,1)}, bf16[2,256,768]{2,1,0:T(8,128)(2,1)S(1)}, u32[]{:S(2)}, u32[]{:S(2)}) collective-permute-start(bf16[2,256,768]{2,1,0:T(8,128)(2,1)} %get-tuple-element.85), channel_id=1, source_target_pairs={{0,1},{1,2},{2,3},{3,0},{4,5},{5,6},{6,7},{7,4},{8,9},{9,10},{10,1... | collective-permute-start | bytes 2359304 | tf_op jit(solution)/shard_map/ppermute | solution.py:182
  40.6 23.2 %collective-permute-start.2 = (bf16[128,3072]{1,0:T(8,128)(2,1)S(1)}, bf16[128,3072]{1,0:T(8,128)(2,1)}, u32[]{:S(2)}, u32[]{:S(2)}) collective-permute-start(bf16[128,3072]{1,0:T(8,128)(2,1)S(1)} %collective-permute-done), channel_id=1, source_target_pairs={{1,2},{2,3},{5,6},{6,7},{9,10},{10,11},{13,14},{14,15},{17,18},{18... | collective-permute-start | bytes 2359304 | tf_op jit(solution)/shard_map/ppermute | solution.py:189
  44.9 35.7 %collective-permute-start.5 = (bf16[128,3072]{1,0:T(8,128)(2,1)}, bf16[128,3072]{1,0:T(8,128)(2,1)}, u32[]{:S(2)}, u32[]{:S(2)}) collective-permute-start(bf16[128,3072]{1,0:T(8,128)(2,1)} %collective-permute-done.4), channel_id=1, source_target_pairs={{1,0},{2,1},{5,4},{6,5},{9,8},{10,9},{13,12},{14,13},{17,16},{18,1... | collective-permute-start | bytes 2359304 | tf_op jit(solution)/shard_map/ppermute | solution.py:189
  80.6 22.7 %collective-permute-start.9 = (bf16[128,3072]{1,0:T(8,128)(2,1)}, bf16[128,3072]{1,0:T(8,128)(2,1)}, u32[]{:S(2)}, u32[]{:S(2)}) collective-permute-start(bf16[128,3072]{1,0:T(8,128)(2,1)} %bitcast.12), channel_id=1, source_target_pairs={{1,0},{2,1},{3,2},{5,4},{6,5},{7,6},{9,8},{10,9},{11,10},{13,12},{... | collective-permute-start | bytes 2359304 | tf_op jit(solution)/shard_map/ppermute | solution.py:189
  81.9 22.8 %collective-permute-start.8 = (bf16[128,3072]{1,0:T(8,128)(2,1)}, bf16[128,3072]{1,0:T(8,128)(2,1)}, u32[]{:S(2)}, u32[]{:S(2)}) collective-permute-start(bf16[128,3072]{1,0:T(8,128)(2,1)} %bitcast.12), channel_id=1, source_target_pairs={{0,1},{1,2},{2,3},{4,5},{5,6},{6,7},{8,9},{9,10},{10,11},{12,13},{... | collective-permute-start | bytes 2359304 | tf_op jit(solution)/shard_map/ppermute | solution.py:189
  89.9 46.9 %collective-permute-start.6 = (bf16[128,3072]{1,0:T(8,128)(2,1)}, bf16[128,3072]{1,0:T(8,128)(2,1)}, u32[]{:S(2)}, u32[]{:S(2)}) collective-permute-start(bf16[128,3072]{1,0:T(8,128)(2,1)} %get-tuple-element.95), channel_id=1, source_target_pairs={{2,3},{1,0},{6,7},{5,4},{10,11},{9,8},{14,15},{13,12},{18,19},{17,... | collective-permute-start | bytes 2359304 | tf_op jit(solution)/shard_map/ppermute | solution.py:191
  91.2 52.7 %collective-permute-start.7 = (bf16[2,256,768]{2,1,0:T(8,128)(2,1)}, bf16[2,256,768]{2,1,0:T(8,128)(2,1)S(1)}, u32[]{:S(2)}, u32[]{:S(2)}) collective-permute-start(bf16[2,256,768]{2,1,0:T(8,128)(2,1)} %get-tuple-element.84), channel_id=1, source_target_pairs={{0,2},{1,3},{2,0},{3,1},{4,6},{5,7},{6,4},{7,5},{8,10},{9,11},{10,... | collective-permute-start | bytes 2359304 | tf_op jit(solution)/shard_map/ppermute | solution.py:182
  103.2 54.5 %collective-permute-start.11 = (bf16[128,3072]{1,0:T(8,128)(2,1)}, bf16[128,3072]{1,0:T(8,128)(2,1)S(1)}, u32[]{:S(2)}, u32[]{:S(2)}) collective-permute-start(bf16[128,3072]{1,0:T(8,128)(2,1)} %collective-permute-done.9), channel_id=1, source_target_pairs={{1,0},{2,1},{5,4},{6,5},{9,8},{10,9},{13,12},{14,13},{17,16},{18,1... | collective-permute-start | bytes 2359304 | tf_op jit(solution)/shard_map/ppermute | solution.py:189
  104.7 53.0 %collective-permute-start.10 = (bf16[128,3072]{1,0:T(8,128)(2,1)}, bf16[128,3072]{1,0:T(8,128)(2,1)S(1)}, u32[]{:S(2)}, u32[]{:S(2)}) collective-permute-start(bf16[128,3072]{1,0:T(8,128)(2,1)} %collective-permute-done.8), channel_id=1, source_target_pairs={{1,2},{2,3},{5,6},{6,7},{9,10},{10,11},{13,14},{14,15},{17,18},{18... | collective-permute-start | bytes 2359304 | tf_op jit(solution)/shard_map/ppermute | solution.py:189
  157.8 15.3 %collective-permute-start.17 = (bf16[128,3072]{1,0:T(8,128)(2,1)S(1)}, bf16[128,3072]{1,0:T(8,128)(2,1)S(1)}, u32[]{:S(2)}, u32[]{:S(2)}) collective-permute-start(bf16[128,3072]{1,0:T(8,128)(2,1)S(1)} %get-tuple-element.93), channel_id=1, source_target_pairs={{2,3},{1,0},{6,7},{5,4},{10,11},{9,8},{14,15},{13,12},{18,19},{17,... | collective-permute-start | bytes 2359304 | tf_op jit(solution)/shard_map/ppermute | solution.py:191
  161.1 15.2 %collective-permute-start.12 = (bf16[128,3072]{1,0:T(8,128)(2,1)S(1)}, bf16[128,3072]{1,0:T(8,128)(2,1)S(1)}, u32[]{:S(2)}, u32[]{:S(2)}) collective-permute-start(bf16[128,3072]{1,0:T(8,128)(2,1)S(1)} %convert_select_fusion), channel_id=1, source_target_pairs={{0,1},{3,2},{4,5},{7,6},{8,9},{11,10},{12,13},{15,14},{16,17},{19,... | collective-permute-start | bytes 2359304 | tf_op jit(solution)/shard_map/ppermute | solution.py:191
  182.6 17.7 %collective-permute-start.13 = (bf16[128,3072]{1,0:T(8,128)(2,1)S(1)}, bf16[128,3072]{1,0:T(8,128)(2,1)}, u32[]{:S(2)}, u32[]{:S(2)}) collective-permute-start(bf16[128,3072]{1,0:T(8,128)(2,1)S(1)} %get-tuple-element.63), channel_id=1, source_target_pairs={{0,1},{1,2},{4,5},{5,6},{8,9},{9,10},{12,13},{13,14},{16,17},{17,1... | collective-permute-start | bytes 2359304 | tf_op jit(solution)/shard_map/ppermute | solution.py:189
  187.9 18.7 %collective-permute-start.15 = (bf16[128,3072]{1,0:T(8,128)(2,1)S(1)}, bf16[128,3072]{1,0:T(8,128)(2,1)}, u32[]{:S(2)}, u32[]{:S(2)}) collective-permute-start(bf16[128,3072]{1,0:T(8,128)(2,1)S(1)} %get-tuple-element.90), channel_id=1, source_target_pairs={{2,1},{3,2},{6,5},{7,6},{10,9},{11,10},{14,13},{15,14},{18,17},{19... | collective-permute-start | bytes 2359304 | tf_op jit(solution)/shard_map/ppermute | solution.py:189
  190.6 19.4 %collective-permute-start.18 = (bf16[192,3072]{1,0:T(8,128)(2,1)S(1)}, bf16[192,3072]{1,0:T(8,128)(2,1)}, u32[]{:S(2)}, u32[]{:S(2)}) collective-permute-start(bf16[192,3072]{1,0:T(8,128)(2,1)S(1)} %constant_dynamic-slice_fusion.3), channel_id=1, source_target_pairs={{0,4},{4,0},{8,12},{12,8},{16,20},{20,16},{24,28},{28,24},{1,5},{5... | collective-permute-start | bytes 3538952 | tf_op jit(solution)/shard_map/ppermute | solution.py:234
  190.7 23.5 %collective-permute-start.19 = (bf16[192,3072]{1,0:T(8,128)(2,1)}, bf16[192,3072]{1,0:T(8,128)(2,1)}, u32[]{:S(2)}, u32[]{:S(2)}) collective-permute-start(bf16[192,3072]{1,0:T(8,128)(2,1)} %constant_dynamic-slice_fusion.2), channel_id=1, source_target_pairs={{0,4},{4,0},{8,12},{12,8},{16,20},{20,16},{24,28},{28,24},{1,5},{5... | collective-permute-start | bytes 3538952 | tf_op jit(solution)/shard_map/ppermute | solution.py:234
  202.5 50.9 %collective-permute-start.14 = (bf16[128,3072]{1,0:T(8,128)(2,1)}, bf16[128,3072]{1,0:T(8,128)(2,1)}, u32[]{:S(2)}, u32[]{:S(2)}) collective-permute-start(bf16[128,3072]{1,0:T(8,128)(2,1)} %add_convert_fusion.8), channel_id=1, source_target_pairs={{0,1},{1,2},{2,3},{4,5},{5,6},{6,7},{8,9},{9,10},{10,11},{12,13},{... | collective-permute-start | bytes 2359304 | tf_op jit(solution)/shard_map/ppermute | solution.py:189
  208.8 44.7 %collective-permute-start.16 = (bf16[128,3072]{1,0:T(8,128)(2,1)}, bf16[128,3072]{1,0:T(8,128)(2,1)}, u32[]{:S(2)}, u32[]{:S(2)}) collective-permute-start(bf16[128,3072]{1,0:T(8,128)(2,1)} %add_convert_fusion.6), channel_id=1, source_target_pairs={{1,0},{2,1},{3,2},{5,4},{6,5},{7,6},{9,8},{10,9},{11,10},{13,12},{... | collective-permute-start | bytes 2359304 | tf_op jit(solution)/shard_map/ppermute | solution.py:189
  212.7 44.5 %collective-permute-start.33 = (bf16[96,3072]{1,0:T(8,128)(2,1)}, bf16[96,3072]{1,0:T(8,128)(2,1)}, u32[]{:S(2)}, u32[]{:S(2)}) collective-permute-start(bf16[96,3072]{1,0:T(8,128)(2,1)} %dynamic-slice_convert_fusion.1), channel_id=1, source_target_pairs={{0,8},{4,12},{8,0},{12,4},{16,24},{20,28},{24,16},{28,20},{1,9},{5... | collective-permute-start | bytes 1769480 | tf_op jit(solution)/shard_map/ppermute | solution.py:234
  227.2 79.1 %all-to-all-start = ((bf16[4,2,256,768]{3,2,1,0:T(8,128)(2,1)}), bf16[4,2,256,768]{3,2,1,0:T(8,128)(2,1)}, u32[]{:S(2)}, u32[]{:S(2)}) async-start(bf16[4,2,256,768]{3,2,1,0:T(8,128)(2,1)} %get-tuple-element.49), calls=%async_computation | async-start | bytes 6291456 | tf_op jit(solution)/shard_map/all_to_all | solution.py:321
  234.5 24.7 %collective-permute-start.38 = (bf16[96,3072]{1,0:T(8,128)(2,1)S(1)}, bf16[96,3072]{1,0:T(8,128)(2,1)S(1)}, u32[]{:S(2)}, u32[]{:S(2)}) collective-permute-start(bf16[96,3072]{1,0:T(8,128)(2,1)S(1)} %dynamic-slice_convert_fusion), channel_id=1, source_target_pairs={{0,16},{4,20},{8,24},{12,28},{16,0},{20,4},{24,8},{28,12},{1,17},{... | collective-permute-start | bytes 1769480 | tf_op jit(solution)/shard_map/ppermute | solution.py:234
  248.1 58.2 %collective-permute-start.22 = (bf16[128,3072]{1,0:T(8,128)(2,1)}, bf16[128,3072]{1,0:T(8,128)(2,1)}, u32[]{:S(2)}, u32[]{:S(2)}) collective-permute-start(bf16[128,3072]{1,0:T(8,128)(2,1)} %get-tuple-element.81), channel_id=1, source_target_pairs={{0,1},{3,2},{4,5},{7,6},{8,9},{11,10},{12,13},{15,14},{16,17},{19,... | collective-permute-start | bytes 2359304 | tf_op jit(solution)/shard_map/ppermute | solution.py:191
  253.5 24.2 %collective-permute-start.27 = (bf16[768,768]{1,0:T(8,128)(2,1)S(1)}, bf16[768,768]{1,0:T(8,128)(2,1)S(1)}, u32[]{:S(2)}, u32[]{:S(2)}) collective-permute-start(bf16[768,768]{1,0:T(8,128)(2,1)S(1)} %constant_dynamic-slice_fusion), channel_id=1, source_target_pairs={{0,4},{4,0},{8,12},{12,8},{16,20},{20,16},{24,28},{28,24},{1,5},{5... | collective-permute-start | bytes 3538952 | tf_op jit(solution)/shard_map/ppermute | solution.py:234
  253.5 24.6 %collective-permute-start.20 = (bf16[768,768]{1,0:T(8,128)(2,1)S(1)}, bf16[768,768]{1,0:T(8,128)(2,1)S(1)}, u32[]{:S(2)}, u32[]{:S(2)}) collective-permute-start(bf16[768,768]{1,0:T(8,128)(2,1)S(1)} %constant_dynamic-slice_fusion.1), channel_id=1, source_target_pairs={{0,4},{4,0},{8,12},{12,8},{16,20},{20,16},{24,28},{28,24},{1,5},{5... | collective-permute-start | bytes 3538952 | tf_op jit(solution)/shard_map/ppermute | solution.py:234
  258.6 8.5 %collective-permute-start.34 = (bf16[48,3072]{1,0:T(8,128)(2,1)S(1)}, bf16[48,3072]{1,0:T(8,128)(2,1)S(1)}, u32[]{:S(2)}, u32[]{:S(2)}) collective-permute-start(bf16[48,3072]{1,0:T(8,128)(2,1)S(1)} %dynamic-slice_convert_fusion.5), channel_id=1, source_target_pairs={{0,16},{4,20},{8,24},{12,28},{16,0},{20,4},{24,8},{28,12},{1,17},{... | collective-permute-start | bytes 884744 | tf_op jit(solution)/shard_map/ppermute | solution.py:234
  259.4 8.3 %collective-permute-start.39 = (bf16[48,3072]{1,0:T(8,128)(2,1)S(1)}, bf16[48,3072]{1,0:T(8,128)(2,1)S(1)}, u32[]{:S(2)}, u32[]{:S(2)}) collective-permute-start(bf16[48,3072]{1,0:T(8,128)(2,1)S(1)} %dynamic-slice_convert_fusion.4), channel_id=1, source_target_pairs={{0,8},{4,12},{8,0},{12,4},{16,24},{20,28},{24,16},{28,20},{1,9},{5... | collective-permute-start | bytes 884744 | tf_op jit(solution)/shard_map/ppermute | solution.py:234
  267.2 7.6 %collective-permute-start.35 = (bf16[48,3072]{1,0:T(8,128)(2,1)S(1)}, bf16[48,3072]{1,0:T(8,128)(2,1)S(1)}, u32[]{:S(2)}, u32[]{:S(2)}) collective-permute-start(bf16[48,3072]{1,0:T(8,128)(2,1)S(1)} %add_convert_fusion.11), channel_id=1, source_target_pairs={{0,16},{4,20},{8,24},{12,28},{16,0},{20,4},{24,8},{28,12},{1,17},{... | collective-permute-start | bytes 884744 | tf_op jit(solution)/shard_map/ppermute | solution.py:234
  267.8 7.7 %collective-permute-start.40 = (bf16[48,3072]{1,0:T(8,128)(2,1)S(1)}, bf16[48,3072]{1,0:T(8,128)(2,1)S(1)}, u32[]{:S(2)}, u32[]{:S(2)}) collective-permute-start(bf16[48,3072]{1,0:T(8,128)(2,1)S(1)} %add_convert_fusion.10), channel_id=1, source_target_pairs={{0,8},{4,12},{8,0},{12,4},{16,24},{20,28},{24,16},{28,20},{1,9},{5... | collective-permute-start | bytes 884744 | tf_op jit(solution)/shard_map/ppermute | solution.py:234
  274.9 13.0 %collective-permute-start.36 = (bf16[96,3072]{1,0:T(8,128)(2,1)S(1)}, bf16[96,3072]{1,0:T(8,128)(2,1)S(1)}, u32[]{:S(2)}, u32[]{:S(2)}) collective-permute-start(bf16[96,3072]{1,0:T(8,128)(2,1)S(1)} %maximum_select_fusion.10), channel_id=1, source_target_pairs={{0,8},{4,12},{8,0},{12,4},{16,24},{20,28},{24,16},{28,20},{1,9},{5... | collective-permute-start | bytes 1769480 | tf_op jit(solution)/shard_map/ppermute | solution.py:234
  275.6 16.3 %collective-permute-start.41 = (bf16[96,3072]{1,0:T(8,128)(2,1)S(1)}, bf16[96,3072]{1,0:T(8,128)(2,1)S(1)}, u32[]{:S(2)}, u32[]{:S(2)}) collective-permute-start(bf16[96,3072]{1,0:T(8,128)(2,1)S(1)} %maximum_select_fusion.11), channel_id=1, source_target_pairs={{0,16},{4,20},{8,24},{12,28},{16,0},{20,4},{24,8},{28,12},{1,17},{... | collective-permute-start | bytes 1769480 | tf_op jit(solution)/shard_map/ppermute | solution.py:234
  278.0 23.1 %collective-permute-start.28 = (bf16[384,768]{1,0:T(8,128)(2,1)S(1)}, bf16[384,768]{1,0:T(8,128)(2,1)S(1)}, u32[]{:S(2)}, u32[]{:S(2)}) collective-permute-start(bf16[384,768]{1,0:T(8,128)(2,1)S(1)} %dynamic-slice_convert_fusion.2), channel_id=1, source_target_pairs={{0,16},{4,20},{8,24},{12,28},{16,0},{20,4},{24,8},{28,12},{1,17},{... | collective-permute-start | bytes 1769480 | tf_op jit(solution)/shard_map/ppermute | solution.py:234
  288.2 17.2 %collective-permute-start.37 = (bf16[192,3072]{1,0:T(8,128)(2,1)S(1)}, bf16[192,3072]{1,0:T(8,128)(2,1)S(1)}, u32[]{:S(2)}, u32[]{:S(2)}) collective-permute-start(bf16[192,3072]{1,0:T(8,128)(2,1)S(1)} %maximum_select_fusion.6), channel_id=1, source_target_pairs={{0,4},{4,0},{8,12},{12,8},{16,20},{20,16},{24,28},{28,24},{1,5},{5... | collective-permute-start | bytes 3538952 | tf_op jit(solution)/shard_map/ppermute | solution.py:234
  288.4 15.8 %collective-permute-start.21 = (bf16[384,768]{1,0:T(8,128)(2,1)S(1)}, bf16[384,768]{1,0:T(8,128)(2,1)S(1)}, u32[]{:S(2)}, u32[]{:S(2)}) collective-permute-start(bf16[384,768]{1,0:T(8,128)(2,1)S(1)} %dynamic-slice_convert_fusion.3), channel_id=1, source_target_pairs={{0,8},{4,12},{8,0},{12,4},{16,24},{20,28},{24,16},{28,20},{1,9},{5... | collective-permute-start | bytes 1769480 | tf_op jit(solution)/shard_map/ppermute | solution.py:234
  292.2 18.1 %collective-permute-start.42 = (bf16[192,3072]{1,0:T(8,128)(2,1)S(1)}, bf16[192,3072]{1,0:T(8,128)(2,1)}, u32[]{:S(2)}, u32[]{:S(2)}) collective-permute-start(bf16[192,3072]{1,0:T(8,128)(2,1)S(1)} %maximum_select_fusion.7), channel_id=1, source_target_pairs={{0,4},{4,0},{8,12},{12,8},{16,20},{20,16},{24,28},{28,24},{1,5},{5... | collective-permute-start | bytes 3538952 | tf_op jit(solution)/shard_map/ppermute | solution.py:234
  308.4 8.8 %collective-permute-start.29 = (bf16[192,768]{1,0:T(8,128)(2,1)S(1)}, bf16[192,768]{1,0:T(8,128)(2,1)S(1)}, u32[]{:S(2)}, u32[]{:S(2)}) collective-permute-start(bf16[192,768]{1,0:T(8,128)(2,1)S(1)} %copy-done.21), channel_id=1, source_target_pairs={{0,8},{4,12},{8,0},{12,4},{16,24},{20,28},{24,16},{28,20},{1,9},{5... | collective-permute-start | bytes 884744 | tf_op jit(solution)/shard_map/ppermute | solution.py:234
  309.0 8.8 %collective-permute-start.23 = (bf16[192,768]{1,0:T(8,128)(2,1)S(1)}, bf16[192,768]{1,0:T(8,128)(2,1)S(1)}, u32[]{:S(2)}, u32[]{:S(2)}) collective-permute-start(bf16[192,768]{1,0:T(8,128)(2,1)S(1)} %copy-done.20), channel_id=1, source_target_pairs={{0,16},{4,20},{8,24},{12,28},{16,0},{20,4},{24,8},{28,12},{1,17},{... | collective-permute-start | bytes 884744 | tf_op jit(solution)/shard_map/ppermute | solution.py:234
  317.2 9.4 %collective-permute-start.30 = (bf16[192,768]{1,0:T(8,128)(2,1)S(1)}, bf16[192,768]{1,0:T(8,128)(2,1)S(1)}, u32[]{:S(2)}, u32[]{:S(2)}) collective-permute-start(bf16[192,768]{1,0:T(8,128)(2,1)S(1)} %add_convert_fusion.12), channel_id=1, source_target_pairs={{0,8},{4,12},{8,0},{12,4},{16,24},{20,28},{24,16},{28,20},{1,9},{5... | collective-permute-start | bytes 884744 | tf_op jit(solution)/shard_map/ppermute | solution.py:234
  317.9 9.7 %collective-permute-start.24 = (bf16[192,768]{1,0:T(8,128)(2,1)S(1)}, bf16[192,768]{1,0:T(8,128)(2,1)S(1)}, u32[]{:S(2)}, u32[]{:S(2)}) collective-permute-start(bf16[192,768]{1,0:T(8,128)(2,1)S(1)} %add_convert_fusion.13), channel_id=1, source_target_pairs={{0,16},{4,20},{8,24},{12,28},{16,0},{20,4},{24,8},{28,12},{1,17},{... | collective-permute-start | bytes 884744 | tf_op jit(solution)/shard_map/ppermute | solution.py:234
  324.3 17.8 %collective-permute-start.43 = (bf16[128,3072]{1,0:T(8,128)(2,1)S(1)}, bf16[128,3072]{1,0:T(8,128)(2,1)S(1)}, u32[]{:S(2)}, u32[]{:S(2)}) collective-permute-start(bf16[128,3072]{1,0:T(8,128)(2,1)S(1)} %get-tuple-element.59), channel_id=1, source_target_pairs={{0,1},{1,2},{4,5},{5,6},{8,9},{9,10},{12,13},{13,14},{16,17},{17,1... | collective-permute-start | bytes 2359304 | tf_op jit(solution)/shard_map/ppermute | solution.py:189
  325.7 20.1 %collective-permute-start.45 = (bf16[128,3072]{1,0:T(8,128)(2,1)S(1)}, bf16[128,3072]{1,0:T(8,128)(2,1)S(1)}, u32[]{:S(2)}, u32[]{:S(2)}) collective-permute-start(bf16[128,3072]{1,0:T(8,128)(2,1)S(1)} %get-tuple-element.88), channel_id=1, source_target_pairs={{2,1},{3,2},{6,5},{7,6},{10,9},{11,10},{14,13},{15,14},{18,17},{19... | collective-permute-start | bytes 2359304 | tf_op jit(solution)/shard_map/ppermute | solution.py:189
  326.8 13.7 %collective-permute-start.31 = (bf16[384,768]{1,0:T(8,128)(2,1)S(1)}, bf16[384,768]{1,0:T(8,128)(2,1)S(1)}, u32[]{:S(2)}, u32[]{:S(2)}) collective-permute-start(bf16[384,768]{1,0:T(8,128)(2,1)S(1)} %maximum_select_fusion.9), channel_id=1, source_target_pairs={{0,16},{4,20},{8,24},{12,28},{16,0},{20,4},{24,8},{28,12},{1,17},{... | collective-permute-start | bytes 1769480 | tf_op jit(solution)/shard_map/ppermute | solution.py:234
  327.8 13.4 %collective-permute-start.25 = (bf16[384,768]{1,0:T(8,128)(2,1)S(1)}, bf16[384,768]{1,0:T(8,128)(2,1)S(1)}, u32[]{:S(2)}, u32[]{:S(2)}) collective-permute-start(bf16[384,768]{1,0:T(8,128)(2,1)S(1)} %maximum_select_fusion.8), channel_id=1, source_target_pairs={{0,8},{4,12},{8,0},{12,4},{16,24},{20,28},{24,16},{28,20},{1,9},{5... | collective-permute-start | bytes 1769480 | tf_op jit(solution)/shard_map/ppermute | solution.py:234
  341.0 6.3 %collective-permute-start.32 = (bf16[768,768]{1,0:T(8,128)(2,1)S(1)}, bf16[768,768]{1,0:T(8,128)(2,1)S(1)}, u32[]{:S(2)}, u32[]{:S(2)}) collective-permute-start(bf16[768,768]{1,0:T(8,128)(2,1)S(1)} %maximum_select_fusion.5), channel_id=1, source_target_pairs={{0,4},{4,0},{8,12},{12,8},{16,20},{20,16},{24,28},{28,24},{1,5},{5... | collective-permute-start | bytes 3538952 | tf_op jit(solution)/shard_map/ppermute | solution.py:234
  341.6 6.4 %collective-permute-start.26 = (bf16[768,768]{1,0:T(8,128)(2,1)S(1)}, bf16[768,768]{1,0:T(8,128)(2,1)S(1)}, u32[]{:S(2)}, u32[]{:S(2)}) collective-permute-start(bf16[768,768]{1,0:T(8,128)(2,1)S(1)} %maximum_select_fusion.4), channel_id=1, source_target_pairs={{0,4},{4,0},{8,12},{12,8},{16,20},{20,16},{24,28},{28,24},{1,5},{5... | collective-permute-start | bytes 3538952 | tf_op jit(solution)/shard_map/ppermute | solution.py:234
  342.3 20.0 %collective-permute-start.44 = (bf16[128,3072]{1,0:T(8,128)(2,1)S(1)}, bf16[128,3072]{1,0:T(8,128)(2,1)S(1)}, u32[]{:S(2)}, u32[]{:S(2)}) collective-permute-start(bf16[128,3072]{1,0:T(8,128)(2,1)S(1)} %add_convert_fusion.3), channel_id=1, source_target_pairs={{0,1},{1,2},{2,3},{4,5},{5,6},{6,7},{8,9},{9,10},{10,11},{12,13},{... | collective-permute-start | bytes 2359304 | tf_op jit(solution)/shard_map/ppermute | solution.py:189
  346.0 21.2 %collective-permute-start.46 = (bf16[128,3072]{1,0:T(8,128)(2,1)S(1)}, bf16[128,3072]{1,0:T(8,128)(2,1)S(1)}, u32[]{:S(2)}, u32[]{:S(2)}) collective-permute-start(bf16[128,3072]{1,0:T(8,128)(2,1)S(1)} %add_convert_fusion.1), channel_id=1, source_target_pairs={{1,0},{2,1},{3,2},{5,4},{6,5},{7,6},{9,8},{10,9},{11,10},{13,12},{... | collective-permute-start | bytes 2359304 | tf_op jit(solution)/shard_map/ppermute | solution.py:189
  (27 other events, 368.6 us)

commit v4 on v3

--- a/solution.py
+++ b/solution.py
@@ -314,12 +314,13 @@
     sum_wo = ClipSum(grad_wo, [masks, masks[:1] + masks[:0:-1]])
     source = lax.rem(me - jnp.arange(n, dtype=jnp.int32) + n, n)
     back = attend_back(table, source, query, grad_attention, pieces, scale, 0, per)
-    grad_attention = after(grad_attention, *sum_wo.step(), *marks[-2])
+    grad_attention = after(grad_attention, *sum_wo.step())
     for c in range(1, chunks):
         back = attend_back(table, source, query, grad_attention, pieces, scale, c * per, per, back)
     grad_query, grad_kv = back
     grad_kv = lax.all_to_all(grad_kv, "seq", split_axis=0, concat_axis=0, tiled=True)
     grad_ref = jnp.concatenate([grad_kv[k] for k in range(n)], axis=2)
+    grad_query = after(grad_query, *marks[-2])
     grad_wq = contract_first(gathered, grad_query).astype(BF16)
     sum_wq = ClipSum(grad_wq, [masks, masks[:1] + masks[:0:-1]])
     grad_query = after(grad_query, grad_wq)

time: 370 us -> 366 us (0.989)
  transfers between devices with their start and end apart: 48 -> 48, of which waited for: 21 -> 21; matrix products, arithmetic and copies ran while one was open for 21% -> 21% of each run, Pallas kernels for 7% -> 8%
where the time goes in v4:
time: 366 us; the launch traced here: 365 us
  waiting for transfers between devices  174 us (48%)
  starting transfers between devices  76.6 us (21%)
  other arithmetic  45.9 us (13%)
  Pallas kernels  27.4 us (7%)
  matrix products  22.2 us (6%)
  local copies, waits for them, and re-layouts  17.1 us (5%)
    ppermute x16, waiting for transfers between devices, both_ways(): return (lax.ppermute(right, 'seq', up), lax.ppermute(left, 'seq', down))  52 us
    ppermute x24, waiting for transfers between devices, exchange(): return lax.ppermute(block, 'dp', [(i, i ^ mask) for i in range(self.size)])  48.7 us
    ppermute x4, waiting for transfers between devices, both_ways(): came = lax.ppermute(jnp.where(rightward, right, left), 'seq', up + down)  38.9 us
    ppermute x16, starting transfers between devices, both_ways(): return (lax.ppermute(right, 'seq', up), lax.ppermute(left, 'seq', down))  37.1 us
    ppermute x3, waiting for transfers between devices, shift(): return lax.ppermute(array, 'seq', [(i, (i + by) % n) for i in range(n)])  34.4 us
    pallas_call x2, Pallas kernels, attend_back(): pl.pallas_call(functools.partial(backward_kernel, n, scale), out_shape=[j...  18.2 us
    ppermute x24, starting transfers between devices, exchange(): return lax.ppermute(block, 'dp', [(i, i ^ mask) for i in range(self.size)])  16.8 us
    ppermute x4, starting transfers between devices, both_ways(): came = lax.ppermute(jnp.where(rightward, right, left), 'seq', up + down)  12.2 us
  transfers between devices with their start and end apart: 48, of which 21 were waited for; matrix products, arithmetic and copies ran while one was open for 21% of the time, Pallas kernels for 8%

profile of v4, /device:TPU:0, one launch (start us, length us, event | category | flops | bytes accessed | tf_op | source)
XLA Modules:
  0.0 364.9 jit_solution(1994376001580065480)
XLA Ops:
  0.6 5.0 %collective-permute-start = (bf16[128,3072]{1,0:T(8,128)(2,1)}, bf16[128,3072]{1,0:T(8,128)(2,1)S(1)}, u32[]{:S(2)}, u32[]{:S(2)}) collective-permute-start(bf16[128,3072]{1,0:T(8,128)(2,1)} %bitcast.48), channel_id=1, source_target_pairs={{0,1},{1,2},{2,3},{4,5},{5,6},{6,7},{8,9},{9,10},{10,11},{12,13},{... | collective-permute-start | bytes 2359304 | tf_op jit(solution)/shard_map/ppermute | solution.py:189
  5.7 3.3 dynamic-slice_bitcast_fusion
  11.6 2.7 collective-permute-start.3
  14.3 9.5 %collective-permute-done = bf16[128,3072]{1,0:T(8,128)(2,1)S(1)} collective-permute-done((bf16[128,3072]{1,0:T(8,128)(2,1)}, bf16[128,3072]{1,0:T(8,128)(2,1)S(1)}, u32[]{:S(2)}, u32[]{:S(2)}) %collective-permute-start) | collective-permute-done | bytes 786464 | tf_op jit(solution)/shard_map/ppermute | solution.py:189
  23.8 16.8 %collective-permute-done.1.refs_3_ = bf16[2,256,768]{2,1,0:T(8,128)(2,1)S(1)} collective-permute-done((bf16[2,256,768]{2,1,0:T(8,128)(2,1)S(1)}, bf16[2,256,768]{2,1,0:T(8,128)(2,1)S(1)}, u32[]{:S(2)}, u32[]{:S(2)}) %collective-permute-start.1) | collective-permute-done | bytes 786464 | tf_op jit(solution)/shard_map/ppermute | solution.py:182
  42.1 2.8 collective-permute-done.4
  46.2 17.6 %collective-permute-done.3.refs_1_ = bf16[2,256,768]{2,1,0:T(8,128)(2,1)S(1)} collective-permute-done((bf16[2,256,768]{2,1,0:T(8,128)(2,1)}, bf16[2,256,768]{2,1,0:T(8,128)(2,1)S(1)}, u32[]{:S(2)}, u32[]{:S(2)}) %collective-permute-start.3) | collective-permute-done | bytes 786464 | tf_op jit(solution)/shard_map/ppermute | solution.py:182
  63.8 16.7 %collective-permute-done.5 = bf16[128,3072]{1,0:T(8,128)(2,1)} collective-permute-done((bf16[128,3072]{1,0:T(8,128)(2,1)}, bf16[128,3072]{1,0:T(8,128)(2,1)}, u32[]{:S(2)}, u32[]{:S(2)}) %collective-permute-start.5) | collective-permute-done | bytes 786464 | tf_op jit(solution)/shard_map/ppermute | solution.py:189
  81.9 5.4 %collective-permute-start.8 = (bf16[128,3072]{1,0:T(8,128)(2,1)}, bf16[128,3072]{1,0:T(8,128)(2,1)}, u32[]{:S(2)}, u32[]{:S(2)}) collective-permute-start(bf16[128,3072]{1,0:T(8,128)(2,1)} %bitcast.12), channel_id=1, source_target_pairs={{0,1},{1,2},{2,3},{4,5},{5,6},{6,7},{8,9},{9,10},{10,11},{12,13},{... | collective-permute-start | bytes 2359304 | tf_op jit(solution)/shard_map/ppermute | solution.py:189
  87.3 2.6 broadcast_select_fusion.6
  93.2 10.1 %collective-permute-done.9 = bf16[128,3072]{1,0:T(8,128)(2,1)} collective-permute-done((bf16[128,3072]{1,0:T(8,128)(2,1)}, bf16[128,3072]{1,0:T(8,128)(2,1)}, u32[]{:S(2)}, u32[]{:S(2)}) %collective-permute-start.9) | collective-permute-done | bytes 786464 | tf_op jit(solution)/shard_map/ppermute | solution.py:189
  105.4 31.4 %collective-permute-done.6 = bf16[128,3072]{1,0:T(8,128)(2,1)} collective-permute-done((bf16[128,3072]{1,0:T(8,128)(2,1)}, bf16[128,3072]{1,0:T(8,128)(2,1)}, u32[]{:S(2)}, u32[]{:S(2)}) %collective-permute-start.6) | collective-permute-done | bytes 786464 | tf_op jit(solution)/shard_map/ppermute | solution.py:191
  138.4 5.5 %convolution_convert_fusion.4.q_ref = bf16[512,768]{1,0:T(8,128)(2,1)S(1)} fusion(bf16[3072,768]{1,0:T(8,128)(2,1)} %param.8, bf16[128,3072]{1,0:T(8,128)(2,1)S(1)} %get-tuple-element.101, bf16[128,3072]{1,0:T(8,128)(2,1)S(1)} %copy-done.18, bf16[128,3072]{1,0:T(8,128)(2,1)S(1)} %get-tuple-element.100, bf16[128,3072]{1,0:T(8,128)(2,1)S(1)} %bitcast.51), kind=kOutput, calls=%fused_computation.29 | convolution fusion | flops 2428895232 | bytes 8650752 | tf_op jit(solution)/shard_map/dot_general | solution.py:290
  143.9 4.6 %shard_map.101 = bf16[512,384]{1,0:T(8,128)(2,1)S(1)} custom-call(s32[4,8]{1,0:T(4,128)S(1)} %copy.22.table_ref, bf16[512,768]{1,0:T(8,128)(2,1)S(1)} %convolution_convert_fusion.4.q_ref, bf16[2,256,768]{2,1,0:T(8,128)(2,1)S(1)} %get-tuple-element.89.refs_0_, bf16[2,256,768]{2,1,0:T(8,128)(2,1)S(1)} %collective-permute-done.3.refs_1_, ...), custom_call_target="tpu_custom_call" | custom-call | flops 805306368 | bytes 2359296 | tf_op jit(solution)/shard_map/pallas_call | solution.py:131
  148.5 4.6 %shard_map.102 = bf16[512,384]{1,0:T(8,128)(2,1)S(1)} custom-call(s32[4,8]{1,0:T(4,128)S(1)} %copy.22.table_ref, bf16[512,768]{1,0:T(8,128)(2,1)S(1)} %convolution_convert_fusion.4.q_ref, bf16[2,256,768]{2,1,0:T(8,128)(2,1)S(1)} %get-tuple-element.89.refs_0_, bf16[2,256,768]{2,1,0:T(8,128)(2,1)S(1)} %collective-permute-done.3.refs_1_, ...), custom_call_target="tpu_custom_call" | custom-call | flops 805306368 | bytes 2359296 | tf_op jit(solution)/shard_map/pallas_call | solution.py:131
  153.2 4.5 %fusion.1 = f32[512,3072]{1,0:T(8,128)S(1)} fusion(bf16[768,3072]{1,0:T(8,128)(2,1)} %param.9, bf16[512,384]{1,0:T(8,128)(2,1)S(1)} %shard_map.102, bf16[512,384]{1,0:T(8,128)(2,1)S(1)} %shard_map.101), kind=kOutput, calls=%fused_computation.82 | convolution fusion | flops 2417491968 | bytes 11796480 | tf_op jit(solution)/shard_map/dot_general | solution.py:299
  161.1 4.8 %collective-permute-start.12 = (bf16[128,3072]{1,0:T(8,128)(2,1)S(1)}, bf16[128,3072]{1,0:T(8,128)(2,1)S(1)}, u32[]{:S(2)}, u32[]{:S(2)}) collective-permute-start(bf16[128,3072]{1,0:T(8,128)(2,1)S(1)} %convert_select_fusion), channel_id=1, source_target_pairs={{0,1},{3,2},{4,5},{7,6},{8,9},{11,10},{12,13},{15,14},{16,17},{19,... | collective-permute-start | bytes 2359304 | tf_op jit(solution)/shard_map/ppermute | solution.py:191
  165.9 7.2 %collective-permute-done.17 = bf16[128,3072]{1,0:T(8,128)(2,1)S(1)} collective-permute-done((bf16[128,3072]{1,0:T(8,128)(2,1)S(1)}, bf16[128,3072]{1,0:T(8,128)(2,1)S(1)}, u32[]{:S(2)}, u32[]{:S(2)}) %collective-permute-start.17) | collective-permute-done | bytes 786464 | tf_op jit(solution)/shard_map/ppermute | solution.py:191
  176.7 2.7 convolution_convert_fusion.3.g_ref
  179.4 2.9 convolution_convert_fusion.1
  182.6 5.3 %collective-permute-start.13 = (bf16[128,3072]{1,0:T(8,128)(2,1)S(1)}, bf16[128,3072]{1,0:T(8,128)(2,1)}, u32[]{:S(2)}, u32[]{:S(2)}) collective-permute-start(bf16[128,3072]{1,0:T(8,128)(2,1)S(1)} %get-tuple-element.65), channel_id=1, source_target_pairs={{0,1},{1,2},{4,5},{5,6},{8,9},{9,10},{12,13},{13,14},{16,17},{17,1... | collective-permute-start | bytes 2359304 | tf_op jit(solution)/shard_map/ppermute | solution.py:189
  191.2 9.1 %shard_map.103 = (bf16[512,768]{1,0:T(8,128)(2,1)S(1)}, bf16[4,2,256,768]{3,2,1,0:T(8,128)(2,1)}) custom-call(s32[4,8]{1,0:T(4,128)S(1)} %copy.22.table_ref, s32[4]{0:T(128)S(1)} %compare_select_fusion.1.source_ref, bf16[512,768]{1,0:T(8,128)(2,1)S(1)} %convolution_convert_fusion.4.q_ref, bf16[512,768]{1,0:T(8,128)(2,1)S(1)} %convolution_convert_fusion.3.g_ref, ...), custom_call_target="tpu_custom_call" | custom-call | flops 2013265920 | bytes 4325376 | tf_op jit(solution)/shard_map/pallas_call | solution.py:154
  200.3 2.2 add_convert_fusion.8
  202.5 4.1 %collective-permute-start.14 = (bf16[128,3072]{1,0:T(8,128)(2,1)}, bf16[128,3072]{1,0:T(8,128)(2,1)}, u32[]{:S(2)}, u32[]{:S(2)}) collective-permute-start(bf16[128,3072]{1,0:T(8,128)(2,1)} %add_convert_fusion.8), channel_id=1, source_target_pairs={{0,1},{1,2},{2,3},{4,5},{5,6},{6,7},{8,9},{9,10},{10,11},{12,13},{... | collective-permute-start | bytes 2359304 | tf_op jit(solution)/shard_map/ppermute | solution.py:189
  206.6 2.2 add_convert_fusion.6
  214.2 3.0 convert_add_fusion.2
  217.2 9.1 %shard_map.104 = (bf16[512,768]{1,0:T(8,128)(2,1)S(1)}, bf16[4,2,256,768]{3,2,1,0:T(8,128)(2,1)}) custom-call(s32[4,8]{1,0:T(4,128)S(1)} %copy.22.table_ref, s32[4]{0:T(128)S(1)} %compare_select_fusion.1.source_ref, bf16[512,768]{1,0:T(8,128)(2,1)S(1)} %convolution_convert_fusion.4.q_ref, ...), custom_call_target="tpu_custom_call", output_to_operand_aliasing={{0}: (8, {}), {1}: (9, {})} | custom-call | flops 2013265920 | bytes 4325376 | tf_op jit(solution)/shard_map/pallas_call | solution.py:154
  227.3 5.9 %all-to-all-start = ((bf16[4,2,256,768]{3,2,1,0:T(8,128)(2,1)}), bf16[4,2,256,768]{3,2,1,0:T(8,128)(2,1)}, u32[]{:S(2)}, u32[]{:S(2)}) async-start(bf16[4,2,256,768]{3,2,1,0:T(8,128)(2,1)} %get-tuple-element.51), calls=%async_computation | async-start | bytes 6291456 | tf_op jit(solution)/shard_map/all_to_all | solution.py:321
  236.3 3.8 %convolution_convert_fusion = bf16[3072,768]{1,0:T(8,128)(2,1)S(1)} fusion(bf16[512,768]{1,0:T(8,128)(2,1)S(1)} %copy-done.1, bf16[128,3072]{1,0:T(8,128)(2,1)S(1)} %copy-done.17, bf16[128,3072]{1,0:T(8,128)(2,1)S(1)} %copy-done.19, bf16[128,3072]{1,0:T(8,128)(2,1)S(1)} %copy-done.15, bf16[128,3072]{1,0:T(8,128)(2,1)} %bitcast.49), kind=kOutput, calls=%fused_computation.2 | convolution fusion | flops 2430861312 | bytes 8650752 | tf_op jit(solution)/shard_map/dot_general | solution.py:23
  240.1 2.9 convolution_convert_fusion.2
  243.0 3.0 slice_convert_fusion.2
  246.0 4.8 %collective-permute-start.22 = (bf16[128,3072]{1,0:T(8,128)(2,1)}, bf16[128,3072]{1,0:T(8,128)(2,1)}, u32[]{:S(2)}, u32[]{:S(2)}) collective-permute-start(bf16[128,3072]{1,0:T(8,128)(2,1)} %get-tuple-element.83), channel_id=1, source_target_pairs={{0,1},{3,2},{4,5},{7,6},{8,9},{11,10},{12,13},{15,14},{16,17},{19,... | collective-permute-start | bytes 2359304 | tf_op jit(solution)/shard_map/ppermute | solution.py:191
  252.5 2.6 add_convert_fusion.5
  257.9 7.1 %collective-permute-done.34 = bf16[48,3072]{1,0:T(8,128)(2,1)S(1)} collective-permute-done((bf16[48,3072]{1,0:T(8,128)(2,1)S(1)}, bf16[48,3072]{1,0:T(8,128)(2,1)S(1)}, u32[]{:S(2)}, u32[]{:S(2)}) %collective-permute-start.34) | collective-permute-done | bytes 294944 | tf_op jit(solution)/shard_map/ppermute | solution.py:234
  266.3 6.4 %collective-permute-done.35 = bf16[48,3072]{1,0:T(8,128)(2,1)S(1)} collective-permute-done((bf16[48,3072]{1,0:T(8,128)(2,1)S(1)}, bf16[48,3072]{1,0:T(8,128)(2,1)S(1)}, u32[]{:S(2)}, u32[]{:S(2)}) %collective-permute-start.35) | collective-permute-done | bytes 294944 | tf_op jit(solution)/shard_map/ppermute | solution.py:234
  276.3 9.5 %collective-permute-done.36 = bf16[96,3072]{1,0:T(8,128)(2,1)S(1)} collective-permute-done((bf16[96,3072]{1,0:T(8,128)(2,1)S(1)}, bf16[96,3072]{1,0:T(8,128)(2,1)S(1)}, u32[]{:S(2)}, u32[]{:S(2)}) %collective-permute-start.36) | collective-permute-done | bytes 589856 | tf_op jit(solution)/shard_map/ppermute | solution.py:234
  286.8 3.0 collective-permute-done.41
  290.2 8.7 %collective-permute-done.28 = bf16[384,768]{1,0:T(8,128)(2,1)S(1)} collective-permute-done((bf16[384,768]{1,0:T(8,128)(2,1)S(1)}, bf16[384,768]{1,0:T(8,128)(2,1)S(1)}, u32[]{:S(2)}, u32[]{:S(2)}) %collective-permute-start.28) | collective-permute-done | bytes 589856 | tf_op jit(solution)/shard_map/ppermute | solution.py:234
  304.2 2.0 add_convert_fusion.4
  308.2 2.1 maximum_select_fusion.3
  310.4 4.7 %collective-permute-done.29 = bf16[192,768]{1,0:T(8,128)(2,1)S(1)} collective-permute-done((bf16[192,768]{1,0:T(8,128)(2,1)S(1)}, bf16[192,768]{1,0:T(8,128)(2,1)S(1)}, u32[]{:S(2)}, u32[]{:S(2)}) %collective-permute-start.29) | collective-permute-done | bytes 294944 | tf_op jit(solution)/shard_map/ppermute | solution.py:234
  317.2 5.0 %maximum_convert_fusion.1 = f32[768,3072]{1,0:T(8,128)} fusion(bf16[384,3072]{1,0:T(8,128)(2,1)S(1)} %maximum_select_fusion.3, bf16[384,3072]{1,0:T(8,128)(2,1)S(1)} %maximum_select_fusion.2), kind=kLoop, calls=%fused_computation.5 | loop fusion | flops 9437184 | bytes 14155776 | tf_op jit(solution)/shard_map/convert_element_type | solution.py:262
  327.2 2.0 slice_bitcast_fusion.3
  331.1 7.2 %collective-permute-done.31 = bf16[384,768]{1,0:T(8,128)(2,1)S(1)} collective-permute-done((bf16[384,768]{1,0:T(8,128)(2,1)S(1)}, bf16[384,768]{1,0:T(8,128)(2,1)S(1)}, u32[]{:S(2)}, u32[]{:S(2)}) %collective-permute-start.31) | collective-permute-done | bytes 589856 | tf_op jit(solution)/shard_map/ppermute | solution.py:234
  340.1 3.6 collective-permute-start.44
  346.5 4.5 %maximum_convert_fusion = f32[3072,768]{1,0:T(8,128)} fusion(bf16[1536,768]{1,0:T(8,128)(2,1)S(1)} %maximum_select_fusion.1, bf16[1536,768]{1,0:T(8,128)(2,1)S(1)} %maximum_select_fusion), kind=kLoop, calls=%fused_computation.4 | loop fusion | flops 9437184 | bytes 14155776 | tf_op jit(solution)/shard_map/convert_element_type | solution.py:262
  351.0 7.8 %collective-permute-done.44 = bf16[128,3072]{1,0:T(8,128)(2,1)S(1)} collective-permute-done((bf16[128,3072]{1,0:T(8,128)(2,1)S(1)}, bf16[128,3072]{1,0:T(8,128)(2,1)S(1)}, u32[]{:S(2)}, u32[]{:S(2)}) %collective-permute-start.44) | collective-permute-done | bytes 786464 | tf_op jit(solution)/shard_map/ppermute | solution.py:189
  358.8 5.0 %collective-permute-done.46 = bf16[128,3072]{1,0:T(8,128)(2,1)S(1)} collective-permute-done((bf16[128,3072]{1,0:T(8,128)(2,1)S(1)}, bf16[128,3072]{1,0:T(8,128)(2,1)S(1)}, u32[]{:S(2)}, u32[]{:S(2)}) %collective-permute-start.46) | collective-permute-done | bytes 786464 | tf_op jit(solution)/shard_map/ppermute | solution.py:189
  (189 shorter events, 66.0 us)
Async XLA Ops:
  0.6 23.2 %collective-permute-start = (bf16[128,3072]{1,0:T(8,128)(2,1)}, bf16[128,3072]{1,0:T(8,128)(2,1)S(1)}, u32[]{:S(2)}, u32[]{:S(2)}) collective-permute-start(bf16[128,3072]{1,0:T(8,128)(2,1)} %bitcast.48), channel_id=1, source_target_pairs={{0,1},{1,2},{2,3},{4,5},{5,6},{6,7},{8,9},{9,10},{10,11},{12,13},{... | collective-permute-start | bytes 2359304 | tf_op jit(solution)/shard_map/ppermute | solution.py:189
  8.9 31.7 %collective-permute-start.1 = (bf16[2,256,768]{2,1,0:T(8,128)(2,1)S(1)}, bf16[2,256,768]{2,1,0:T(8,128)(2,1)S(1)}, u32[]{:S(2)}, u32[]{:S(2)}) collective-permute-start(bf16[2,256,768]{2,1,0:T(8,128)(2,1)S(1)} %get-tuple-element.88), channel_id=1, source_target_pairs={{0,3},{1,0},{2,1},{3,2},{4,7},{5,4},{6,5},{7,6},{8,11},{9,8},{10,9... | collective-permute-start | bytes 2359304 | tf_op jit(solution)/shard_map/ppermute | solution.py:182
  10.3 34.6 %collective-permute-start.4 = (bf16[128,3072]{1,0:T(8,128)(2,1)S(1)}, bf16[128,3072]{1,0:T(8,128)(2,1)}, u32[]{:S(2)}, u32[]{:S(2)}) collective-permute-start(bf16[128,3072]{1,0:T(8,128)(2,1)S(1)} %bitcast.50), channel_id=1, source_target_pairs={{1,0},{2,1},{3,2},{5,4},{6,5},{7,6},{9,8},{10,9},{11,10},{13,12},{... | collective-permute-start | bytes 2359304 | tf_op jit(solution)/shard_map/ppermute | solution.py:189
  11.6 52.2 %collective-permute-start.3 = (bf16[2,256,768]{2,1,0:T(8,128)(2,1)}, bf16[2,256,768]{2,1,0:T(8,128)(2,1)S(1)}, u32[]{:S(2)}, u32[]{:S(2)}) collective-permute-start(bf16[2,256,768]{2,1,0:T(8,128)(2,1)} %get-tuple-element.87), channel_id=1, source_target_pairs={{0,1},{1,2},{2,3},{3,0},{4,5},{5,6},{6,7},{7,4},{8,9},{9,10},{10,1... | collective-permute-start | bytes 2359304 | tf_op jit(solution)/shard_map/ppermute | solution.py:182
  40.6 23.2 %collective-permute-start.2 = (bf16[128,3072]{1,0:T(8,128)(2,1)S(1)}, bf16[128,3072]{1,0:T(8,128)(2,1)}, u32[]{:S(2)}, u32[]{:S(2)}) collective-permute-start(bf16[128,3072]{1,0:T(8,128)(2,1)S(1)} %collective-permute-done), channel_id=1, source_target_pairs={{1,2},{2,3},{5,6},{6,7},{9,10},{10,11},{13,14},{14,15},{17,18},{18... | collective-permute-start | bytes 2359304 | tf_op jit(solution)/shard_map/ppermute | solution.py:189
  44.9 35.7 %collective-permute-start.5 = (bf16[128,3072]{1,0:T(8,128)(2,1)}, bf16[128,3072]{1,0:T(8,128)(2,1)}, u32[]{:S(2)}, u32[]{:S(2)}) collective-permute-start(bf16[128,3072]{1,0:T(8,128)(2,1)} %collective-permute-done.4), channel_id=1, source_target_pairs={{1,0},{2,1},{5,4},{6,5},{9,8},{10,9},{13,12},{14,13},{17,16},{18,1... | collective-permute-start | bytes 2359304 | tf_op jit(solution)/shard_map/ppermute | solution.py:189
  80.6 22.7 %collective-permute-start.9 = (bf16[128,3072]{1,0:T(8,128)(2,1)}, bf16[128,3072]{1,0:T(8,128)(2,1)}, u32[]{:S(2)}, u32[]{:S(2)}) collective-permute-start(bf16[128,3072]{1,0:T(8,128)(2,1)} %bitcast.12), channel_id=1, source_target_pairs={{1,0},{2,1},{3,2},{5,4},{6,5},{7,6},{9,8},{10,9},{11,10},{13,12},{... | collective-permute-start | bytes 2359304 | tf_op jit(solution)/shard_map/ppermute | solution.py:189
  81.9 22.8 %collective-permute-start.8 = (bf16[128,3072]{1,0:T(8,128)(2,1)}, bf16[128,3072]{1,0:T(8,128)(2,1)}, u32[]{:S(2)}, u32[]{:S(2)}) collective-permute-start(bf16[128,3072]{1,0:T(8,128)(2,1)} %bitcast.12), channel_id=1, source_target_pairs={{0,1},{1,2},{2,3},{4,5},{5,6},{6,7},{8,9},{9,10},{10,11},{12,13},{... | collective-permute-start | bytes 2359304 | tf_op jit(solution)/shard_map/ppermute | solution.py:189
  89.9 46.9 %collective-permute-start.6 = (bf16[128,3072]{1,0:T(8,128)(2,1)}, bf16[128,3072]{1,0:T(8,128)(2,1)}, u32[]{:S(2)}, u32[]{:S(2)}) collective-permute-start(bf16[128,3072]{1,0:T(8,128)(2,1)} %get-tuple-element.97), channel_id=1, source_target_pairs={{2,3},{1,0},{6,7},{5,4},{10,11},{9,8},{14,15},{13,12},{18,19},{17,... | collective-permute-start | bytes 2359304 | tf_op jit(solution)/shard_map/ppermute | solution.py:191
  91.2 52.7 %collective-permute-start.7 = (bf16[2,256,768]{2,1,0:T(8,128)(2,1)}, bf16[2,256,768]{2,1,0:T(8,128)(2,1)S(1)}, u32[]{:S(2)}, u32[]{:S(2)}) collective-permute-start(bf16[2,256,768]{2,1,0:T(8,128)(2,1)} %get-tuple-element.86), channel_id=1, source_target_pairs={{0,2},{1,3},{2,0},{3,1},{4,6},{5,7},{6,4},{7,5},{8,10},{9,11},{10,... | collective-permute-start | bytes 2359304 | tf_op jit(solution)/shard_map/ppermute | solution.py:182
  103.2 54.5 %collective-permute-start.11 = (bf16[128,3072]{1,0:T(8,128)(2,1)}, bf16[128,3072]{1,0:T(8,128)(2,1)S(1)}, u32[]{:S(2)}, u32[]{:S(2)}) collective-permute-start(bf16[128,3072]{1,0:T(8,128)(2,1)} %collective-permute-done.9), channel_id=1, source_target_pairs={{1,0},{2,1},{5,4},{6,5},{9,8},{10,9},{13,12},{14,13},{17,16},{18,1... | collective-permute-start | bytes 2359304 | tf_op jit(solution)/shard_map/ppermute | solution.py:189
  104.7 53.0 %collective-permute-start.10 = (bf16[128,3072]{1,0:T(8,128)(2,1)}, bf16[128,3072]{1,0:T(8,128)(2,1)S(1)}, u32[]{:S(2)}, u32[]{:S(2)}) collective-permute-start(bf16[128,3072]{1,0:T(8,128)(2,1)} %collective-permute-done.8), channel_id=1, source_target_pairs={{1,2},{2,3},{5,6},{6,7},{9,10},{10,11},{13,14},{14,15},{17,18},{18... | collective-permute-start | bytes 2359304 | tf_op jit(solution)/shard_map/ppermute | solution.py:189
  157.8 15.3 %collective-permute-start.17 = (bf16[128,3072]{1,0:T(8,128)(2,1)S(1)}, bf16[128,3072]{1,0:T(8,128)(2,1)S(1)}, u32[]{:S(2)}, u32[]{:S(2)}) collective-permute-start(bf16[128,3072]{1,0:T(8,128)(2,1)S(1)} %get-tuple-element.95), channel_id=1, source_target_pairs={{2,3},{1,0},{6,7},{5,4},{10,11},{9,8},{14,15},{13,12},{18,19},{17,... | collective-permute-start | bytes 2359304 | tf_op jit(solution)/shard_map/ppermute | solution.py:191
  161.1 15.2 %collective-permute-start.12 = (bf16[128,3072]{1,0:T(8,128)(2,1)S(1)}, bf16[128,3072]{1,0:T(8,128)(2,1)S(1)}, u32[]{:S(2)}, u32[]{:S(2)}) collective-permute-start(bf16[128,3072]{1,0:T(8,128)(2,1)S(1)} %convert_select_fusion), channel_id=1, source_target_pairs={{0,1},{3,2},{4,5},{7,6},{8,9},{11,10},{12,13},{15,14},{16,17},{19,... | collective-permute-start | bytes 2359304 | tf_op jit(solution)/shard_map/ppermute | solution.py:191
  182.6 17.7 %collective-permute-start.13 = (bf16[128,3072]{1,0:T(8,128)(2,1)S(1)}, bf16[128,3072]{1,0:T(8,128)(2,1)}, u32[]{:S(2)}, u32[]{:S(2)}) collective-permute-start(bf16[128,3072]{1,0:T(8,128)(2,1)S(1)} %get-tuple-element.65), channel_id=1, source_target_pairs={{0,1},{1,2},{4,5},{5,6},{8,9},{9,10},{12,13},{13,14},{16,17},{17,1... | collective-permute-start | bytes 2359304 | tf_op jit(solution)/shard_map/ppermute | solution.py:189
  187.9 18.7 %collective-permute-start.15 = (bf16[128,3072]{1,0:T(8,128)(2,1)S(1)}, bf16[128,3072]{1,0:T(8,128)(2,1)}, u32[]{:S(2)}, u32[]{:S(2)}) collective-permute-start(bf16[128,3072]{1,0:T(8,128)(2,1)S(1)} %get-tuple-element.92), channel_id=1, source_target_pairs={{2,1},{3,2},{6,5},{7,6},{10,9},{11,10},{14,13},{15,14},{18,17},{19... | collective-permute-start | bytes 2359304 | tf_op jit(solution)/shard_map/ppermute | solution.py:189
  190.6 19.4 %collective-permute-start.18 = (bf16[192,3072]{1,0:T(8,128)(2,1)S(1)}, bf16[192,3072]{1,0:T(8,128)(2,1)}, u32[]{:S(2)}, u32[]{:S(2)}) collective-permute-start(bf16[192,3072]{1,0:T(8,128)(2,1)S(1)} %constant_dynamic-slice_fusion.3), channel_id=1, source_target_pairs={{0,4},{4,0},{8,12},{12,8},{16,20},{20,16},{24,28},{28,24},{1,5},{5... | collective-permute-start | bytes 3538952 | tf_op jit(solution)/shard_map/ppermute | solution.py:234
  190.7 23.5 %collective-permute-start.19 = (bf16[192,3072]{1,0:T(8,128)(2,1)}, bf16[192,3072]{1,0:T(8,128)(2,1)}, u32[]{:S(2)}, u32[]{:S(2)}) collective-permute-start(bf16[192,3072]{1,0:T(8,128)(2,1)} %constant_dynamic-slice_fusion.2), channel_id=1, source_target_pairs={{0,4},{4,0},{8,12},{12,8},{16,20},{20,16},{24,28},{28,24},{1,5},{5... | collective-permute-start | bytes 3538952 | tf_op jit(solution)/shard_map/ppermute | solution.py:234
  202.5 48.8 %collective-permute-start.14 = (bf16[128,3072]{1,0:T(8,128)(2,1)}, bf16[128,3072]{1,0:T(8,128)(2,1)}, u32[]{:S(2)}, u32[]{:S(2)}) collective-permute-start(bf16[128,3072]{1,0:T(8,128)(2,1)} %add_convert_fusion.8), channel_id=1, source_target_pairs={{0,1},{1,2},{2,3},{4,5},{5,6},{6,7},{8,9},{9,10},{10,11},{12,13},{... | collective-permute-start | bytes 2359304 | tf_op jit(solution)/shard_map/ppermute | solution.py:189
  208.8 42.7 %collective-permute-start.16 = (bf16[128,3072]{1,0:T(8,128)(2,1)}, bf16[128,3072]{1,0:T(8,128)(2,1)}, u32[]{:S(2)}, u32[]{:S(2)}) collective-permute-start(bf16[128,3072]{1,0:T(8,128)(2,1)} %add_convert_fusion.6), channel_id=1, source_target_pairs={{1,0},{2,1},{3,2},{5,4},{6,5},{7,6},{9,8},{10,9},{11,10},{13,12},{... | collective-permute-start | bytes 2359304 | tf_op jit(solution)/shard_map/ppermute | solution.py:189
  212.7 42.4 %collective-permute-start.33 = (bf16[96,3072]{1,0:T(8,128)(2,1)}, bf16[96,3072]{1,0:T(8,128)(2,1)}, u32[]{:S(2)}, u32[]{:S(2)}) collective-permute-start(bf16[96,3072]{1,0:T(8,128)(2,1)} %dynamic-slice_convert_fusion.1), channel_id=1, source_target_pairs={{0,8},{4,12},{8,0},{12,4},{16,24},{20,28},{24,16},{28,20},{1,9},{5... | collective-permute-start | bytes 1769480 | tf_op jit(solution)/shard_map/ppermute | solution.py:234
  227.3 76.9 %all-to-all-start = ((bf16[4,2,256,768]{3,2,1,0:T(8,128)(2,1)}), bf16[4,2,256,768]{3,2,1,0:T(8,128)(2,1)}, u32[]{:S(2)}, u32[]{:S(2)}) async-start(bf16[4,2,256,768]{3,2,1,0:T(8,128)(2,1)} %get-tuple-element.51), calls=%async_computation | async-start | bytes 6291456 | tf_op jit(solution)/shard_map/all_to_all | solution.py:321
  234.7 22.4 %collective-permute-start.38 = (bf16[96,3072]{1,0:T(8,128)(2,1)S(1)}, bf16[96,3072]{1,0:T(8,128)(2,1)S(1)}, u32[]{:S(2)}, u32[]{:S(2)}) collective-permute-start(bf16[96,3072]{1,0:T(8,128)(2,1)S(1)} %dynamic-slice_convert_fusion), channel_id=1, source_target_pairs={{0,16},{4,20},{8,24},{12,28},{16,0},{20,4},{24,8},{28,12},{1,17},{... | collective-permute-start | bytes 1769480 | tf_op jit(solution)/shard_map/ppermute | solution.py:234
  246.0 58.2 %collective-permute-start.22 = (bf16[128,3072]{1,0:T(8,128)(2,1)}, bf16[128,3072]{1,0:T(8,128)(2,1)}, u32[]{:S(2)}, u32[]{:S(2)}) collective-permute-start(bf16[128,3072]{1,0:T(8,128)(2,1)} %get-tuple-element.83), channel_id=1, source_target_pairs={{0,1},{3,2},{4,5},{7,6},{8,9},{11,10},{12,13},{15,14},{16,17},{19,... | collective-permute-start | bytes 2359304 | tf_op jit(solution)/shard_map/ppermute | solution.py:191
  251.4 24.2 %collective-permute-start.27 = (bf16[768,768]{1,0:T(8,128)(2,1)S(1)}, bf16[768,768]{1,0:T(8,128)(2,1)S(1)}, u32[]{:S(2)}, u32[]{:S(2)}) collective-permute-start(bf16[768,768]{1,0:T(8,128)(2,1)S(1)} %constant_dynamic-slice_fusion), channel_id=1, source_target_pairs={{0,4},{4,0},{8,12},{12,8},{16,20},{20,16},{24,28},{28,24},{1,5},{5... | collective-permute-start | bytes 3538952 | tf_op jit(solution)/shard_map/ppermute | solution.py:234
  251.4 24.6 %collective-permute-start.20 = (bf16[768,768]{1,0:T(8,128)(2,1)S(1)}, bf16[768,768]{1,0:T(8,128)(2,1)S(1)}, u32[]{:S(2)}, u32[]{:S(2)}) collective-permute-start(bf16[768,768]{1,0:T(8,128)(2,1)S(1)} %constant_dynamic-slice_fusion.1), channel_id=1, source_target_pairs={{0,4},{4,0},{8,12},{12,8},{16,20},{20,16},{24,28},{28,24},{1,5},{5... | collective-permute-start | bytes 3538952 | tf_op jit(solution)/shard_map/ppermute | solution.py:234
  256.5 8.5 %collective-permute-start.34 = (bf16[48,3072]{1,0:T(8,128)(2,1)S(1)}, bf16[48,3072]{1,0:T(8,128)(2,1)S(1)}, u32[]{:S(2)}, u32[]{:S(2)}) collective-permute-start(bf16[48,3072]{1,0:T(8,128)(2,1)S(1)} %dynamic-slice_convert_fusion.5), channel_id=1, source_target_pairs={{0,16},{4,20},{8,24},{12,28},{16,0},{20,4},{24,8},{28,12},{1,17},{... | collective-permute-start | bytes 884744 | tf_op jit(solution)/shard_map/ppermute | solution.py:234
  257.3 8.3 %collective-permute-start.39 = (bf16[48,3072]{1,0:T(8,128)(2,1)S(1)}, bf16[48,3072]{1,0:T(8,128)(2,1)S(1)}, u32[]{:S(2)}, u32[]{:S(2)}) collective-permute-start(bf16[48,3072]{1,0:T(8,128)(2,1)S(1)} %dynamic-slice_convert_fusion.4), channel_id=1, source_target_pairs={{0,8},{4,12},{8,0},{12,4},{16,24},{20,28},{24,16},{28,20},{1,9},{5... | collective-permute-start | bytes 884744 | tf_op jit(solution)/shard_map/ppermute | solution.py:234
  265.1 7.6 %collective-permute-start.35 = (bf16[48,3072]{1,0:T(8,128)(2,1)S(1)}, bf16[48,3072]{1,0:T(8,128)(2,1)S(1)}, u32[]{:S(2)}, u32[]{:S(2)}) collective-permute-start(bf16[48,3072]{1,0:T(8,128)(2,1)S(1)} %add_convert_fusion.11), channel_id=1, source_target_pairs={{0,16},{4,20},{8,24},{12,28},{16,0},{20,4},{24,8},{28,12},{1,17},{... | collective-permute-start | bytes 884744 | tf_op jit(solution)/shard_map/ppermute | solution.py:234
  265.7 7.7 %collective-permute-start.40 = (bf16[48,3072]{1,0:T(8,128)(2,1)S(1)}, bf16[48,3072]{1,0:T(8,128)(2,1)S(1)}, u32[]{:S(2)}, u32[]{:S(2)}) collective-permute-start(bf16[48,3072]{1,0:T(8,128)(2,1)S(1)} %add_convert_fusion.10), channel_id=1, source_target_pairs={{0,8},{4,12},{8,0},{12,4},{16,24},{20,28},{24,16},{28,20},{1,9},{5... | collective-permute-start | bytes 884744 | tf_op jit(solution)/shard_map/ppermute | solution.py:234
  272.8 13.0 %collective-permute-start.36 = (bf16[96,3072]{1,0:T(8,128)(2,1)S(1)}, bf16[96,3072]{1,0:T(8,128)(2,1)S(1)}, u32[]{:S(2)}, u32[]{:S(2)}) collective-permute-start(bf16[96,3072]{1,0:T(8,128)(2,1)S(1)} %maximum_select_fusion.10), channel_id=1, source_target_pairs={{0,8},{4,12},{8,0},{12,4},{16,24},{20,28},{24,16},{28,20},{1,9},{5... | collective-permute-start | bytes 1769480 | tf_op jit(solution)/shard_map/ppermute | solution.py:234
  273.5 16.3 %collective-permute-start.41 = (bf16[96,3072]{1,0:T(8,128)(2,1)S(1)}, bf16[96,3072]{1,0:T(8,128)(2,1)S(1)}, u32[]{:S(2)}, u32[]{:S(2)}) collective-permute-start(bf16[96,3072]{1,0:T(8,128)(2,1)S(1)} %maximum_select_fusion.11), channel_id=1, source_target_pairs={{0,16},{4,20},{8,24},{12,28},{16,0},{20,4},{24,8},{28,12},{1,17},{... | collective-permute-start | bytes 1769480 | tf_op jit(solution)/shard_map/ppermute | solution.py:234
  275.9 23.1 %collective-permute-start.28 = (bf16[384,768]{1,0:T(8,128)(2,1)S(1)}, bf16[384,768]{1,0:T(8,128)(2,1)S(1)}, u32[]{:S(2)}, u32[]{:S(2)}) collective-permute-start(bf16[384,768]{1,0:T(8,128)(2,1)S(1)} %dynamic-slice_convert_fusion.2), channel_id=1, source_target_pairs={{0,16},{4,20},{8,24},{12,28},{16,0},{20,4},{24,8},{28,12},{1,17},{... | collective-permute-start | bytes 1769480 | tf_op jit(solution)/shard_map/ppermute | solution.py:234
  286.1 17.2 %collective-permute-start.37 = (bf16[192,3072]{1,0:T(8,128)(2,1)S(1)}, bf16[192,3072]{1,0:T(8,128)(2,1)S(1)}, u32[]{:S(2)}, u32[]{:S(2)}) collective-permute-start(bf16[192,3072]{1,0:T(8,128)(2,1)S(1)} %maximum_select_fusion.6), channel_id=1, source_target_pairs={{0,4},{4,0},{8,12},{12,8},{16,20},{20,16},{24,28},{28,24},{1,5},{5... | collective-permute-start | bytes 3538952 | tf_op jit(solution)/shard_map/ppermute | solution.py:234
  286.3 15.8 %collective-permute-start.21 = (bf16[384,768]{1,0:T(8,128)(2,1)S(1)}, bf16[384,768]{1,0:T(8,128)(2,1)S(1)}, u32[]{:S(2)}, u32[]{:S(2)}) collective-permute-start(bf16[384,768]{1,0:T(8,128)(2,1)S(1)} %dynamic-slice_convert_fusion.3), channel_id=1, source_target_pairs={{0,8},{4,12},{8,0},{12,4},{16,24},{20,28},{24,16},{28,20},{1,9},{5... | collective-permute-start | bytes 1769480 | tf_op jit(solution)/shard_map/ppermute | solution.py:234
  290.1 18.1 %collective-permute-start.42 = (bf16[192,3072]{1,0:T(8,128)(2,1)S(1)}, bf16[192,3072]{1,0:T(8,128)(2,1)}, u32[]{:S(2)}, u32[]{:S(2)}) collective-permute-start(bf16[192,3072]{1,0:T(8,128)(2,1)S(1)} %maximum_select_fusion.7), channel_id=1, source_target_pairs={{0,4},{4,0},{8,12},{12,8},{16,20},{20,16},{24,28},{28,24},{1,5},{5... | collective-permute-start | bytes 3538952 | tf_op jit(solution)/shard_map/ppermute | solution.py:234
  306.3 8.8 %collective-permute-start.29 = (bf16[192,768]{1,0:T(8,128)(2,1)S(1)}, bf16[192,768]{1,0:T(8,128)(2,1)S(1)}, u32[]{:S(2)}, u32[]{:S(2)}) collective-permute-start(bf16[192,768]{1,0:T(8,128)(2,1)S(1)} %copy-done.21), channel_id=1, source_target_pairs={{0,8},{4,12},{8,0},{12,4},{16,24},{20,28},{24,16},{28,20},{1,9},{5... | collective-permute-start | bytes 884744 | tf_op jit(solution)/shard_map/ppermute | solution.py:234
  306.9 8.8 %collective-permute-start.23 = (bf16[192,768]{1,0:T(8,128)(2,1)S(1)}, bf16[192,768]{1,0:T(8,128)(2,1)S(1)}, u32[]{:S(2)}, u32[]{:S(2)}) collective-permute-start(bf16[192,768]{1,0:T(8,128)(2,1)S(1)} %copy-done.20), channel_id=1, source_target_pairs={{0,16},{4,20},{8,24},{12,28},{16,0},{20,4},{24,8},{28,12},{1,17},{... | collective-permute-start | bytes 884744 | tf_op jit(solution)/shard_map/ppermute | solution.py:234
  315.1 9.4 %collective-permute-start.30 = (bf16[192,768]{1,0:T(8,128)(2,1)S(1)}, bf16[192,768]{1,0:T(8,128)(2,1)S(1)}, u32[]{:S(2)}, u32[]{:S(2)}) collective-permute-start(bf16[192,768]{1,0:T(8,128)(2,1)S(1)} %add_convert_fusion.12), channel_id=1, source_target_pairs={{0,8},{4,12},{8,0},{12,4},{16,24},{20,28},{24,16},{28,20},{1,9},{5... | collective-permute-start | bytes 884744 | tf_op jit(solution)/shard_map/ppermute | solution.py:234
  315.8 9.7 %collective-permute-start.24 = (bf16[192,768]{1,0:T(8,128)(2,1)S(1)}, bf16[192,768]{1,0:T(8,128)(2,1)S(1)}, u32[]{:S(2)}, u32[]{:S(2)}) collective-permute-start(bf16[192,768]{1,0:T(8,128)(2,1)S(1)} %add_convert_fusion.13), channel_id=1, source_target_pairs={{0,16},{4,20},{8,24},{12,28},{16,0},{20,4},{24,8},{28,12},{1,17},{... | collective-permute-start | bytes 884744 | tf_op jit(solution)/shard_map/ppermute | solution.py:234
  322.2 17.8 %collective-permute-start.43 = (bf16[128,3072]{1,0:T(8,128)(2,1)S(1)}, bf16[128,3072]{1,0:T(8,128)(2,1)S(1)}, u32[]{:S(2)}, u32[]{:S(2)}) collective-permute-start(bf16[128,3072]{1,0:T(8,128)(2,1)S(1)} %get-tuple-element.61), channel_id=1, source_target_pairs={{0,1},{1,2},{4,5},{5,6},{8,9},{9,10},{12,13},{13,14},{16,17},{17,1... | collective-permute-start | bytes 2359304 | tf_op jit(solution)/shard_map/ppermute | solution.py:189
  323.6 20.1 %collective-permute-start.45 = (bf16[128,3072]{1,0:T(8,128)(2,1)S(1)}, bf16[128,3072]{1,0:T(8,128)(2,1)S(1)}, u32[]{:S(2)}, u32[]{:S(2)}) collective-permute-start(bf16[128,3072]{1,0:T(8,128)(2,1)S(1)} %get-tuple-element.90), channel_id=1, source_target_pairs={{2,1},{3,2},{6,5},{7,6},{10,9},{11,10},{14,13},{15,14},{18,17},{19... | collective-permute-start | bytes 2359304 | tf_op jit(solution)/shard_map/ppermute | solution.py:189
  324.7 13.7 %collective-permute-start.31 = (bf16[384,768]{1,0:T(8,128)(2,1)S(1)}, bf16[384,768]{1,0:T(8,128)(2,1)S(1)}, u32[]{:S(2)}, u32[]{:S(2)}) collective-permute-start(bf16[384,768]{1,0:T(8,128)(2,1)S(1)} %maximum_select_fusion.9), channel_id=1, source_target_pairs={{0,16},{4,20},{8,24},{12,28},{16,0},{20,4},{24,8},{28,12},{1,17},{... | collective-permute-start | bytes 1769480 | tf_op jit(solution)/shard_map/ppermute | solution.py:234
  325.7 13.4 %collective-permute-start.25 = (bf16[384,768]{1,0:T(8,128)(2,1)S(1)}, bf16[384,768]{1,0:T(8,128)(2,1)S(1)}, u32[]{:S(2)}, u32[]{:S(2)}) collective-permute-start(bf16[384,768]{1,0:T(8,128)(2,1)S(1)} %maximum_select_fusion.8), channel_id=1, source_target_pairs={{0,8},{4,12},{8,0},{12,4},{16,24},{20,28},{24,16},{28,20},{1,9},{5... | collective-permute-start | bytes 1769480 | tf_op jit(solution)/shard_map/ppermute | solution.py:234
  338.9 6.3 %collective-permute-start.32 = (bf16[768,768]{1,0:T(8,128)(2,1)S(1)}, bf16[768,768]{1,0:T(8,128)(2,1)S(1)}, u32[]{:S(2)}, u32[]{:S(2)}) collective-permute-start(bf16[768,768]{1,0:T(8,128)(2,1)S(1)} %maximum_select_fusion.5), channel_id=1, source_target_pairs={{0,4},{4,0},{8,12},{12,8},{16,20},{20,16},{24,28},{28,24},{1,5},{5... | collective-permute-start | bytes 3538952 | tf_op jit(solution)/shard_map/ppermute | solution.py:234
  339.5 6.4 %collective-permute-start.26 = (bf16[768,768]{1,0:T(8,128)(2,1)S(1)}, bf16[768,768]{1,0:T(8,128)(2,1)S(1)}, u32[]{:S(2)}, u32[]{:S(2)}) collective-permute-start(bf16[768,768]{1,0:T(8,128)(2,1)S(1)} %maximum_select_fusion.4), channel_id=1, source_target_pairs={{0,4},{4,0},{8,12},{12,8},{16,20},{20,16},{24,28},{28,24},{1,5},{5... | collective-permute-start | bytes 3538952 | tf_op jit(solution)/shard_map/ppermute | solution.py:234
  340.1 18.7 %collective-permute-start.44 = (bf16[128,3072]{1,0:T(8,128)(2,1)S(1)}, bf16[128,3072]{1,0:T(8,128)(2,1)S(1)}, u32[]{:S(2)}, u32[]{:S(2)}) collective-permute-start(bf16[128,3072]{1,0:T(8,128)(2,1)S(1)} %add_convert_fusion.3), channel_id=1, source_target_pairs={{0,1},{1,2},{2,3},{4,5},{5,6},{6,7},{8,9},{9,10},{10,11},{12,13},{... | collective-permute-start | bytes 2359304 | tf_op jit(solution)/shard_map/ppermute | solution.py:189
  343.9 19.9 %collective-permute-start.46 = (bf16[128,3072]{1,0:T(8,128)(2,1)S(1)}, bf16[128,3072]{1,0:T(8,128)(2,1)S(1)}, u32[]{:S(2)}, u32[]{:S(2)}) collective-permute-start(bf16[128,3072]{1,0:T(8,128)(2,1)S(1)} %add_convert_fusion.1), channel_id=1, source_target_pairs={{1,0},{2,1},{3,2},{5,4},{6,5},{7,6},{9,8},{10,9},{11,10},{13,12},{... | collective-permute-start | bytes 2359304 | tf_op jit(solution)/shard_map/ppermute | solution.py:189
  (29 other events, 380.3 us)
